TPU v7x, 32 devices: a whole 2x2x4 slice. The times are simulated.
32 devices in a mesh: dp: 4 (over y, x), expert: 4 (over z), tensor: 2 (over core).
Axes of the slice: x: 2, y: 2, z: 4, core: 2. Of those that a mesh axis runs over, the one named last changes fastest.
Arguments:
- tokens: bfloat16 [4096, 2048], P(('dp', 'expert')), may hold values from -6 to 6
- segments: int32 [4, 1024], P('dp', 'expert'), may hold values from 0 to 7, never falling along the last dimension, each value on 1 to 512 neighbouring positions
- routes: int32 [4096, 4], P(('dp', 'expert')), may hold values from 0 to 7, all different within a row; in each aligned block of 256 rows (0 to 255, 256 to 511, ...) at most 192 rows name the same one
- norm1_gain: bfloat16 [2048], replicated, may hold values from 0.5 to 1.5
- q_weight: bfloat16 [2048, 2048], P(None, 'tensor'), may hold values from -0.125 to 0.125
- k_weight: bfloat16 [2048, 2048], P(None, 'tensor'), may hold values from -0.125 to 0.125
- v_weight: bfloat16 [2048, 2048], P(None, 'tensor'), may hold values from -0.125 to 0.125
- o_weight: bfloat16 [2048, 2048], P(None, 'tensor'), may hold values from -0.5 to 0.5
- norm2_gain: bfloat16 [2048], replicated, may hold values from 0.5 to 1.5
- router_weight: bfloat16 [2048, 8], replicated, may hold values from -0.0625 to 0.0625
- shared_gate_vector: bfloat16 [2048], replicated, may hold values from -0.125 to 0.125
- shared_gate_weight: bfloat16 [2048, 5632], P(None, 'tensor'), may hold values from -0.125 to 0.125
- shared_up_weight: bfloat16 [2048, 5632], P(None, 'tensor'), may hold values from -0.125 to 0.125
- shared_down_weight: bfloat16 [2048, 5632], P(None, 'tensor'), may hold values from -0.25 to 0.25
- expert_gate_weight: bfloat16 [8, 2048, 1408], P('expert', None, 'tensor'), may hold values from -0.125 to 0.125
- expert_up_weight: bfloat16 [8, 2048, 1408], P('expert', None, 'tensor'), may hold values from -0.125 to 0.125
- expert_down_weight: bfloat16 [8, 2048, 1408], P('expert', None, 'tensor'), may hold values from -1 to 1
- out_grad: bfloat16 [4096, 2048], P(('dp', 'expert')), may hold values from -6 to 6
Outputs:
- layer_out: float32 [4096, 2048], P(('dp', 'expert'))
- input_grad: float32 [4096, 2048], P(('dp', 'expert'))
- rms_stats: float32 [2, 4096], P(None, ('dp', 'expert'))
- norm1_gain_grad: float32 [2048], P(('dp', 'expert'))
- q_weight_grad: float32 [2048, 2048], P(('dp', 'expert'), 'tensor')
- k_weight_grad: float32 [2048, 2048], P(('dp', 'expert'), 'tensor')
- v_weight_grad: float32 [2048, 2048], P(('dp', 'expert'), 'tensor')
- o_weight_grad: float32 [2048, 2048], P(('dp', 'expert'), 'tensor')
- norm2_gain_grad: float32 [2048], P(('dp', 'expert'))
- router_grad: float32 [2048, 8], P(('dp', 'expert'))
- shared_vector_grad: float32 [2048], P(('dp', 'expert'))
- shared_gate_grad: float32 [2048, 5632], P(('dp', 'expert'), 'tensor')
- shared_up_grad: float32 [2048, 5632], P(('dp', 'expert'), 'tensor')
- shared_down_grad: float32 [2048, 5632], P(('dp', 'expert'), 'tensor')
- expert_gate_grad: float32 [8, 2048, 1408], P('expert', 'dp', 'tensor')
- expert_up_grad: float32 [8, 2048, 1408], P('expert', 'dp', 'tensor')
- expert_down_grad: float32 [8, 2048, 1408], P('expert', 'dp', 'tensor')
Inputs may be any that keep to these rules, and one draw needn't show every extreme that they name: `segments`: document numbers never fall along a sequence; each of the 8 documents of a sequence is present and holds 1 to 512 tokens, one exactly 512. `routes`: the 4 experts of a token differ. Among the 256 tokens of one index of dp and expert, no expert is named more than 192 times, a bound that some block reaches.
All inputs are finite; a program needn't handle non-finite values.
Results may differ from a plain program's by a relative error of at most 0.02.
Values may be sent and summed in bfloat16 or wider, within the bound.
A program may use at most 384 MiB of HBM per device.

v0:
```python
import jax
import jax.numpy as jnp
from jax import lax
from jax.sharding import PartitionSpec as P

HD = 128


epsilon = 1e-06
precise = lax.Precision.HIGHEST


def norm_forward(values, gain):
    inverse = lax.rsqrt(jnp.mean(values * values, axis=-1, keepdims=True) + epsilon)
    return (values * inverse * gain, inverse)


def norm_backward(values, inverse, gain, upstream):
    scaled = upstream * gain
    gain_grad = jnp.sum(upstream * values * inverse, axis=0)
    inner = jnp.mean(scaled * values, axis=-1, keepdims=True)
    return (inverse * scaled - values * inverse * inverse * inverse * inner, gain_grad)


def silu_slope(values):
    sigma = jax.nn.sigmoid(values)
    return sigma * (1.0 + values * (1.0 - sigma))


def cross_rows(left, right):
    return lax.dot_general(
        left, right, (((0,), (0,)), ((), ())), preferred_element_type=jnp.float32
    )


def cross_cols(left, right):
    return lax.dot_general(
        left, right, (((1,), (1,)), ((), ())), preferred_element_type=jnp.float32
    )


def plain_dot(left, right):
    return jnp.dot(left, right, preferred_element_type=jnp.float32)


def body(
    tokens,
    segments,
    routes,
    norm1_gain,
    q_weight,
    k_weight,
    v_weight,
    o_weight,
    norm2_gain,
    router_weight,
    shared_gate_vector,
    shared_gate_weight,
    shared_up_weight,
    shared_down_weight,
    expert_gate_weight,
    expert_up_weight,
    expert_down_weight,
    out_grad,
):
    tok_rows = tokens.shape[0]
    feat_width = tokens.shape[1]
    local_count = expert_gate_weight.shape[0]
    expert_count = local_count * lax.axis_size("expert")
    top_count = routes.shape[1]
    slot_count = 3 * tok_rows * top_count // (2 * expert_count)
    head_count = q_weight.shape[1] // HD
    score_scale = HD ** (-0.5)
    first_norm_gain = norm1_gain.astype(jnp.float32)
    second_norm_gain = norm2_gain.astype(jnp.float32)
    input_rows = tokens.astype(jnp.float32)
    normed_one, inverse_one = norm_forward(input_rows, first_norm_gain)
    normed_low = normed_one.astype(jnp.bfloat16)
    queries = plain_dot(normed_low, q_weight).astype(jnp.bfloat16)
    own_keys = plain_dot(normed_low, k_weight).astype(jnp.bfloat16)
    own_values = plain_dot(normed_low, v_weight).astype(jnp.bfloat16)
    labels = segments.astype(jnp.bfloat16)
    all_keys, all_values, key_labels = (
        lax.all_gather(own_keys, "expert", axis=0, tiled=True),
        lax.all_gather(own_values, "expert", axis=0, tiled=True),
        lax.all_gather(labels, "expert", axis=1, tiled=True),
    )
    key_span = all_keys.shape[0]
    query_pos = lax.axis_index("expert") * tok_rows + jnp.arange(tok_rows)
    key_pos = jnp.arange(key_span)
    allowed = (key_pos[None, :] <= query_pos[:, None]) & (
        key_labels[0][None, :] == labels[0][:, None]
    )
    query_heads = queries.reshape(tok_rows, head_count, HD)
    key_heads = all_keys.reshape(key_span, head_count, HD)
    value_heads = all_values.reshape(key_span, head_count, HD)

    def masked_scores():
        raw_scores = (
            jnp.einsum("qhd,khd->hqk", query_heads, key_heads, preferred_element_type=jnp.float32)
            * score_scale
        )
        return jnp.where(allowed[None], raw_scores, -jnp.inf)

    scores = masked_scores()
    top_score = jnp.max(scores, axis=-1, keepdims=True)
    exponent = jnp.exp(scores - top_score)
    totals = jnp.sum(exponent, axis=-1, keepdims=True)
    log_total = top_score + jnp.log(totals)
    weights_low = (exponent / totals).astype(jnp.bfloat16)
    mixed_heads = jnp.einsum(
        "hqk,khd->qhd", weights_low, value_heads, preferred_element_type=jnp.float32
    )
    mixed_low = mixed_heads.reshape(tok_rows, -1).astype(jnp.bfloat16)
    residual_state = input_rows + lax.psum(
        cross_cols(mixed_low, o_weight).astype(jnp.bfloat16), "tensor"
    ).astype(jnp.float32)
    normed_two, inverse_two = norm_forward(residual_state, second_norm_gain)
    routed_in = normed_two.astype(jnp.bfloat16)
    router_probs = jax.nn.softmax(plain_dot(routed_in, router_weight), axis=-1)
    chosen = routes[:, :, None] == jnp.arange(expert_count)[None, None, :]
    gate_values = jnp.sum(jnp.where(chosen, router_probs[:, None, :], 0.0), axis=-1)
    shared_gate_pre = plain_dot(routed_in, shared_gate_weight)
    shared_up_pre = plain_dot(routed_in, shared_up_weight)
    shared_hidden = (jax.nn.silu(shared_gate_pre) * shared_up_pre).astype(jnp.bfloat16)
    shared_out = cross_cols(shared_hidden, shared_down_weight)
    shared_sigma = jax.nn.sigmoid(plain_dot(routed_in, shared_gate_vector))
    flat_routes = routes.reshape(-1)
    route_hot = (flat_routes[:, None] == jnp.arange(expert_count)[None, :]).astype(jnp.int32)
    slot_index = jnp.sum((jnp.cumsum(route_hot, axis=0) - 1) * route_hot, axis=1)
    placement = flat_routes * slot_count + slot_index
    assign_total = tok_rows * top_count
    owners = (
        jnp.full((expert_count * slot_count,), assign_total, jnp.int32)
        .at[placement]
        .set(jnp.arange(assign_total, dtype=jnp.int32))
    )
    padded_rows = jnp.concatenate([routed_in, jnp.zeros((1, feat_width), jnp.bfloat16)], axis=0)
    outgoing = padded_rows[owners // top_count].reshape(expert_count, 1, slot_count, feat_width)
    received = lax.all_to_all(outgoing, "expert", split_axis=0, concat_axis=1, tiled=True)
    gate_pre = jnp.einsum(
        "esmd,edf->esmf", received, expert_gate_weight, preferred_element_type=jnp.float32
    )
    up_pre = jnp.einsum(
        "esmd,edf->esmf", received, expert_up_weight, preferred_element_type=jnp.float32
    )
    expert_hidden = (jax.nn.silu(gate_pre) * up_pre).astype(jnp.bfloat16)
    result = jnp.einsum(
        "esmf,edf->esmd", expert_hidden, expert_down_weight, preferred_element_type=jnp.float32
    )
    returned = lax.all_to_all(
        result.astype(jnp.bfloat16), "expert", split_axis=1, concat_axis=0, tiled=True
    ).astype(result.dtype)
    picked = returned.reshape(expert_count * slot_count, feat_width)[placement].reshape(
        tok_rows, top_count, feat_width
    )
    routed_output = jnp.sum(gate_values[:, :, None] * picked, axis=1)
    branch_sum = lax.psum(
        (routed_output + shared_sigma[:, None] * shared_out).astype(jnp.bfloat16), "tensor"
    ).astype(jnp.float32)
    layer_out = residual_state + branch_sum
    upstream = out_grad.astype(jnp.float32)
    d_shared = (shared_sigma[:, None] * upstream).astype(jnp.bfloat16)
    d_sigma = jnp.sum(upstream * shared_out, axis=-1)
    d_shared_hidden = plain_dot(d_shared, shared_down_weight)
    d_shared_gate = (d_shared_hidden * shared_up_pre * silu_slope(shared_gate_pre)).astype(
        jnp.bfloat16
    )
    d_shared_up = (d_shared_hidden * jax.nn.silu(shared_gate_pre)).astype(jnp.bfloat16)
    grad_shared_gate = cross_rows(routed_in, d_shared_gate)
    grad_shared_up = cross_rows(routed_in, d_shared_up)
    grad_shared_down = cross_rows(d_shared, shared_hidden)
    d_routed = cross_cols(d_shared_gate, shared_gate_weight) + cross_cols(
        d_shared_up, shared_up_weight
    )
    d_gates = jnp.sum(upstream[:, None, :] * picked, axis=-1)
    d_expert_out = (
        (gate_values[:, :, None] * upstream[:, None, :])
        .astype(jnp.bfloat16)
        .reshape(assign_total, feat_width)
    )
    padded_grads = jnp.concatenate([d_expert_out, jnp.zeros((1, feat_width), jnp.bfloat16)], axis=0)
    grads_out = padded_grads[owners].reshape(expert_count, 1, slot_count, feat_width)
    incoming = lax.all_to_all(grads_out, "expert", split_axis=0, concat_axis=1, tiled=True)
    expert_hidden = (jax.nn.silu(gate_pre) * up_pre).astype(jnp.bfloat16)
    d_hidden = jnp.einsum(
        "esmd,edf->esmf", incoming, expert_down_weight, preferred_element_type=jnp.float32
    )
    d_gate_pre = (d_hidden * up_pre * silu_slope(gate_pre)).astype(jnp.bfloat16)
    d_up_pre = (d_hidden * jax.nn.silu(gate_pre)).astype(jnp.bfloat16)
    d_rows = jnp.einsum(
        "esmf,edf->esmd", d_gate_pre, expert_gate_weight, preferred_element_type=jnp.float32
    )
    d_rows = d_rows + jnp.einsum(
        "esmf,edf->esmd", d_up_pre, expert_up_weight, preferred_element_type=jnp.float32
    )
    d_back = lax.all_to_all(
        d_rows.astype(jnp.bfloat16), "expert", split_axis=1, concat_axis=0, tiled=True
    ).astype(d_rows.dtype)
    grad_expert_gate = jnp.einsum(
        "esmd,esmf->edf", received, d_gate_pre, preferred_element_type=jnp.float32
    )
    grad_expert_up = jnp.einsum(
        "esmd,esmf->edf", received, d_up_pre, preferred_element_type=jnp.float32
    )
    grad_expert_down = jnp.einsum(
        "esmd,esmf->edf", incoming, expert_hidden, preferred_element_type=jnp.float32
    )
    sum_gate, sum_up, sum_down = (
        lax.psum_scatter(
            grad_expert_gate.astype(jnp.bfloat16), "dp", scatter_dimension=1, tiled=True
        ).astype(jnp.float32),
        lax.psum_scatter(
            grad_expert_up.astype(jnp.bfloat16), "dp", scatter_dimension=1, tiled=True
        ).astype(jnp.float32),
        lax.psum_scatter(
            grad_expert_down.astype(jnp.bfloat16), "dp", scatter_dimension=1, tiled=True
        ).astype(jnp.float32),
    )
    back_rows = d_back.reshape(expert_count * slot_count, feat_width)[placement].reshape(
        tok_rows, top_count, feat_width
    )
    d_routed = d_routed + jnp.sum(back_rows, axis=1)
    d_probs = jnp.sum(jnp.where(chosen, d_gates[:, :, None], 0.0), axis=1)
    d_logits = router_probs * (d_probs - jnp.sum(router_probs * d_probs, axis=-1, keepdims=True))
    d_vector = d_sigma * shared_sigma * (1.0 - shared_sigma)
    router_matrix = router_weight.astype(jnp.float32)
    gate_vector_weight = shared_gate_vector.astype(jnp.float32)
    d_routed = (
        d_routed
        + jnp.dot(d_logits, router_matrix.T, precision=precise)
        + d_vector[:, None] * gate_vector_weight[None, :]
    )
    d_normed_two, d_logits, d_vector = (
        lax.psum(d_routed.astype(jnp.bfloat16), "tensor").astype(jnp.float32),
        lax.psum(d_logits.astype(jnp.bfloat16), "tensor").astype(jnp.float32),
        lax.psum(d_vector.astype(jnp.bfloat16), "tensor").astype(jnp.float32),
    )
    grad_router = jnp.dot(
        routed_in.T, d_logits, precision=precise, preferred_element_type=jnp.float32
    )
    grad_vector = jnp.dot(
        routed_in.T, d_vector, precision=precise, preferred_element_type=jnp.float32
    )
    d_hidden_norm, grad_norm_two = norm_backward(
        residual_state, inverse_two, second_norm_gain, d_normed_two
    )
    d_state = upstream + d_hidden_norm
    d_state_low = d_state.astype(jnp.bfloat16)
    d_mixed = plain_dot(d_state_low, o_weight).astype(jnp.bfloat16)
    grad_out_proj = cross_rows(d_state_low, mixed_low)
    probs_full = jnp.exp(masked_scores() - log_total)
    probs_low = probs_full.astype(jnp.bfloat16)
    d_mixed_heads = d_mixed.reshape(tok_rows, head_count, HD)
    d_value_all = jnp.einsum(
        "hqk,qhd->khd", probs_low, d_mixed_heads, preferred_element_type=jnp.float32
    )
    d_probs_att = jnp.einsum(
        "qhd,khd->hqk", d_mixed_heads, value_heads, preferred_element_type=jnp.float32
    )
    d_scores = (
        probs_full * (d_probs_att - jnp.sum(probs_full * d_probs_att, axis=-1, keepdims=True))
    ).astype(jnp.bfloat16)
    d_queries = (
        (
            jnp.einsum("hqk,khd->qhd", d_scores, key_heads, preferred_element_type=jnp.float32)
            * score_scale
        )
        .reshape(tok_rows, -1)
        .astype(jnp.bfloat16)
    )
    d_key_all = (
        jnp.einsum("hqk,qhd->khd", d_scores, query_heads, preferred_element_type=jnp.float32)
        * score_scale
    )
    d_keys, d_values = (
        lax.psum_scatter(
            d_key_all.reshape(key_span, -1).astype(jnp.bfloat16),
            "expert",
            scatter_dimension=0,
            tiled=True,
        ).astype(jnp.float32),
        lax.psum_scatter(
            d_value_all.reshape(key_span, -1).astype(jnp.bfloat16),
            "expert",
            scatter_dimension=0,
            tiled=True,
        ).astype(jnp.float32),
    )
    d_keys_low = d_keys.astype(jnp.bfloat16)
    d_values_low = d_values.astype(jnp.bfloat16)
    grad_query = cross_rows(normed_low, d_queries)
    grad_key = cross_rows(normed_low, d_keys_low)
    grad_value = cross_rows(normed_low, d_values_low)
    d_normed_one = (
        cross_cols(d_queries, q_weight)
        + cross_cols(d_keys_low, k_weight)
        + cross_cols(d_values_low, v_weight)
    )
    d_normed_one = lax.psum(d_normed_one.astype(jnp.bfloat16), "tensor").astype(jnp.float32)
    d_input_norm, grad_norm_one = norm_backward(
        input_rows, inverse_one, first_norm_gain, d_normed_one
    )
    input_grad = d_state + d_input_norm
    stats = jnp.concatenate([inverse_one.T, inverse_two.T], axis=0)
    g_one, g_query, g_key, g_value, g_out, g_two, g_router, g_vector, g_sgate, g_sup, g_sdown = (
        lax.psum_scatter(grad_norm_one, ("dp", "expert"), scatter_dimension=0, tiled=True),
        lax.psum_scatter(grad_query, ("dp", "expert"), scatter_dimension=0, tiled=True),
        lax.psum_scatter(grad_key, ("dp", "expert"), scatter_dimension=0, tiled=True),
        lax.psum_scatter(grad_value, ("dp", "expert"), scatter_dimension=0, tiled=True),
        lax.psum_scatter(grad_out_proj, ("dp", "expert"), scatter_dimension=0, tiled=True),
        lax.psum_scatter(grad_norm_two, ("dp", "expert"), scatter_dimension=0, tiled=True),
        lax.psum_scatter(grad_router, ("dp", "expert"), scatter_dimension=0, tiled=True),
        lax.psum_scatter(grad_vector, ("dp", "expert"), scatter_dimension=0, tiled=True),
        lax.psum_scatter(grad_shared_gate, ("dp", "expert"), scatter_dimension=0, tiled=True),
        lax.psum_scatter(grad_shared_up, ("dp", "expert"), scatter_dimension=0, tiled=True),
        lax.psum_scatter(grad_shared_down, ("dp", "expert"), scatter_dimension=0, tiled=True),
    )
    return (
        layer_out,
        input_grad,
        stats,
        g_one,
        g_query,
        g_key,
        g_value,
        g_out,
        g_two,
        g_router,
        g_vector,
        g_sgate,
        g_sup,
        g_sdown,
        sum_gate,
        sum_up,
        sum_down,
    )


def solution(mesh):
    placed = (
        P(("dp", "expert"), None),
        P("dp", "expert"),
        P(("dp", "expert"), None),
        P(),
        P(None, "tensor"),
        P(None, "tensor"),
        P(None, "tensor"),
        P(None, "tensor"),
        P(),
        P(),
        P(),
        P(None, "tensor"),
        P(None, "tensor"),
        P(None, "tensor"),
        P("expert", None, "tensor"),
        P("expert", None, "tensor"),
        P("expert", None, "tensor"),
        P(("dp", "expert"), None),
    )
    return jax.shard_map(
        body,
        mesh=mesh,
        in_specs=placed,
        out_specs=(
            P(("dp", "expert"), None),
            P(("dp", "expert"), None),
            P(None, ("dp", "expert")),
            P(("dp", "expert")),
            P(("dp", "expert"), "tensor"),
            P(("dp", "expert"), "tensor"),
            P(("dp", "expert"), "tensor"),
            P(("dp", "expert"), "tensor"),
            P(("dp", "expert")),
            P(("dp", "expert"), None),
            P(("dp", "expert")),
            P(("dp", "expert"), "tensor"),
            P(("dp", "expert"), "tensor"),
            P(("dp", "expert"), "tensor"),
            P("expert", "dp", "tensor"),
            P("expert", "dp", "tensor"),
            P("expert", "dp", "tensor"),
        ),
        check_vma=False,
    )
```

profile of v0, /device:TPU:8, one launch (start us, length us, event | category | flops | bytes accessed | tf_op | source)
XLA Modules:
  0.0 3411.2 jit_solution(6877648826485437788)
XLA Ops:
  23.5 8.3 all_gather.12
  32.9 27.1 all-gather.5.cloned.1.call-done
  71.4 35.4 %all-gather.3.cloned.1.call-done = bf16[1024,1024]{1,0:T(8,128)(2,1)} async-done(((bf16[256,1024]{1,0:T(8,128)(2,1)}), bf16[1024,1024]{1,0:T(8,128)(2,1)}) %all-gather.3.cloned.1.call-update) | async-done | bytes 2097168 | tf_op jit(solution)/shard_map/all_gather | solution.py:85
  123.1 12.5 all-reduce.12.cloned.1.call-done
  157.8 10.0 mul.339
  175.9 15.4 gather_fusion.2
  191.4 96.6 %all-to-all-done = bf16[8,1,192,2048]{3,2,1,0:T(8,128)(2,1)} async-done(((bf16[8,1,192,2048]{3,2,1,0:T(8,128)(2,1)}), bf16[8,1,192,2048]{3,2,1,0:T(8,128)(2,1)}, u32[]{:S(2)}, u32[]{:S(2)}) %all-to-all-start) | async-done | bytes 6291488 | tf_op jit(solution)/shard_map/all_to_all | solution.py:140
  288.0 8.9 all-to-all-start.2
  296.9 10.3 fusion.6
  307.2 124.4 %all-to-all-done.2 = bf16[8,1,192,2048]{3,2,1,0:T(8,128)(2,1)} async-done(((bf16[8,1,192,2048]{3,2,1,0:T(8,128)(2,1)}), bf16[8,1,192,2048]{3,2,1,0:T(8,128)(2,1)}, u32[]{:S(2)}, u32[]{:S(2)}) %all-to-all-start.2) | async-done | bytes 6291488 | tf_op jit(solution)/shard_map/all_to_all | solution.py:184
  431.6 11.0 fusion.4
  442.6 13.4 multiply_convert_fusion.3
  464.6 9.1 all-to-all-start.1
  473.7 11.0 fusion.11
  484.7 10.0 add_convert_fusion
  498.0 110.0 %all-to-all-done.1 = bf16[2,4,192,2048]{3,2,0,1:T(8,128)(2,1)} async-done(((bf16[2,4,192,2048]{3,2,0,1:T(8,128)(2,1)}), bf16[2,4,192,2048]{3,2,0,1:T(8,128)(2,1)}, u32[]{:S(2)}, u32[]{:S(2)}) %all-to-all-start.1) | async-done | bytes 6291488 | tf_op jit(solution)/shard_map/all_to_all | solution.py:151
  608.0 8.6 all-to-all-start.3
  625.0 10.3 multiply_convert_fusion.8
  647.6 9.3 fusion.112
  656.9 8.8 bitcast_convert_fusion.4
  665.7 13.7 gather_fusion.1
  679.5 10.0 reshape.289
  689.5 11.1 multiply_reduce_fusion.1
  700.8 50.1 %all-to-all-done.3 = bf16[2,4,192,2048]{3,2,0,1:T(8,128)(2,1)} async-done(((bf16[2,4,192,2048]{3,2,0,1:T(8,128)(2,1)}), bf16[2,4,192,2048]{3,2,0,1:T(8,128)(2,1)}, u32[]{:S(2)}, u32[]{:S(2)}) %all-to-all-start.3) | async-done | bytes 6291488 | tf_op jit(solution)/shard_map/all_to_all | solution.py:197
  750.9 8.8 bitcast_convert_fusion.3
  759.8 13.6 gather_fusion.3
  773.3 9.8 reshape.291
  783.2 8.6 reduce_sum.163
  791.8 8.5 fusion.44
  802.6 22.0 all-reduce.14.cloned.1.call-done
  850.1 11.0 bitcast_convert_fusion
  861.6 10.7 bitcast_convert_fusion.2
  872.4 10.7 bitcast_convert_fusion.1
  898.6 33.8 reduce-scatter.16.cloned.1.call-done
  967.0 11.0 fusion.84
  978.0 11.3 fusion.116
  989.5 11.0 fusion.115
  1006.6 65.1 %reduce-scatter.34.cloned.1.call-done = bf16[2,512,704]{1,2,0:T(8,128)(2,1)} async-done(((bf16[2,2048,704]{1,2,0:T(8,128)(2,1)}), bf16[2,512,704]{1,2,0:T(8,128)(2,1)}) %reduce-scatter.34.cloned.1.call-update) | async-done | bytes 1441808 | tf_op jit(solution)/shard_map/reduce_scatter | solution.py:210
  1075.0 65.5 %reduce-scatter.36.cloned.1.call-done = bf16[2,512,704]{1,2,0:T(8,128)(2,1)} async-done(((bf16[2,2048,704]{1,2,0:T(8,128)(2,1)}), bf16[2,512,704]{1,2,0:T(8,128)(2,1)}) %reduce-scatter.36.cloned.1.call-update) | async-done | bytes 1441808 | tf_op jit(solution)/shard_map/reduce_scatter | solution.py:213
  1143.9 21.0 all-reduce.16.cloned.1.call-done
  1166.8 71.9 %all-reduce.5 = (f32[2048]{0:T(1024)S(1)}, f32[2048]{0:T(1024)S(1)}, f32[2048]{0:T(1024)S(1)}) all-reduce(f32[2048]{0:T(1024)S(1)} %get-tuple-element.21, f32[2048]{0:T(1024)S(1)} %get-tuple-element.19, f32[2048]{0:T(1024)S(1)} %bitcast.206), channel_id=4, replica_groups=mesh['dp'=4,'expert'=4,'tensor'=2] {'dp','expert'}, use_global_device_ids=true, to_apply=%region_27.28.clone | all-reduce | flops 6144 | bytes 49152
  1246.2 175.2 %reduce-scatter.24.cloned.1.call-done = f32[128,1024]{1,0:T(8,128)} async-done(((f32[2048,1024]{1,0:T(8,128)}), f32[128,1024]{1,0:T(8,128)}) %reduce-scatter.24.cloned.1.call-update) | async-done | bytes 524304 | tf_op jit(solution)/shard_map/reduce_scatter | solution.py:311
  1421.4 182.7 %reduce-scatter.18.cloned.1.call-done = f32[128,1024]{1,0:T(8,128)} async-done(((f32[2048,1024]{1,0:T(8,128)}), f32[128,1024]{1,0:T(8,128)}) %reduce-scatter.18.cloned.1.call-update) | async-done | bytes 524304 | tf_op jit(solution)/shard_map/reduce_scatter | solution.py:308
  1604.2 182.6 %reduce-scatter.22.cloned.1.call-done = f32[128,1024]{1,0:T(8,128)} async-done(((f32[2048,1024]{1,0:T(8,128)}), f32[128,1024]{1,0:T(8,128)}) %reduce-scatter.22.cloned.1.call-update) | async-done | bytes 524304 | tf_op jit(solution)/shard_map/reduce_scatter | solution.py:310
  1786.7 182.6 %reduce-scatter.20.cloned.1.call-done = f32[128,1024]{1,0:T(8,128)} async-done(((f32[2048,1024]{1,0:T(8,128)}), f32[128,1024]{1,0:T(8,128)}) %reduce-scatter.20.cloned.1.call-update) | async-done | bytes 524304 | tf_op jit(solution)/shard_map/reduce_scatter | solution.py:309
  1969.3 478.0 %reduce-scatter.32.cloned.1.call-done = f32[128,2816]{1,0:T(8,128)} async-done(((f32[2048,2816]{1,0:T(8,128)}), f32[128,2816]{1,0:T(8,128)}) %reduce-scatter.32.cloned.1.call-update) | async-done | bytes 1441808 | tf_op jit(solution)/shard_map/reduce_scatter | solution.py:317
  2447.3 478.4 %reduce-scatter.30.cloned.1.call-done = f32[128,2816]{1,0:T(8,128)} async-done(((f32[2048,2816]{1,0:T(8,128)}), f32[128,2816]{1,0:T(8,128)}) %reduce-scatter.30.cloned.1.call-update) | async-done | bytes 1441808 | tf_op jit(solution)/shard_map/reduce_scatter | solution.py:316
  2925.7 478.4 %reduce-scatter.28.cloned.1.call-done = f32[128,2816]{1,0:T(8,128)} async-done(((f32[2048,2816]{1,0:T(8,128)}), f32[128,2816]{1,0:T(8,128)}) %reduce-scatter.28.cloned.1.call-update) | async-done | bytes 1441808 | tf_op jit(solution)/shard_map/reduce_scatter | solution.py:315
  (263 shorter events, 207.2 us)
Async XLA Ops:
  7.2 160.7 %copy-start = (bf16[2048,8]{0,1:T(8,128)(2,1)S(1)}, bf16[2048,8]{0,1:T(8,128)(2,1)}, u32[]{:S(2)}) copy-start(bf16[2048,8]{0,1:T(8,128)(2,1)} %param.27) | copy-start | bytes 98308
  7.2 52.8 %all-gather.5.cloned.1.call-start = ((), (), s32[]{:S(2)}) async-start(), calls=%async_computation.18 | async-start | bytes 2621440 | tf_op jit(solution)/shard_map/all_gather | solution.py:84
  8.8 10.2 copy-start.27
  14.2 92.5 %all-gather.3.cloned.1.call-start = ((), (), s32[]{:S(2)}) async-start(), calls=%async_computation.17 | async-start | bytes 2621440 | tf_op jit(solution)/shard_map/all_gather | solution.py:85
  18.6 117.1 %all-reduce.12.cloned.1.call-start = ((), (), s32[]{:S(2)}) async-start(), calls=%async_computation.19 | async-start | bytes 2097152 | tf_op jit(solution)/shard_map/psum | solution.py:115
  66.3 40.5 %copy-start.31 = (f32[8,256]{1,0:T(8,128)}, f32[8,256]{1,0:T(8,128)S(1)}, u32[]{:S(2)}) copy-start(f32[8,256]{1,0:T(8,128)S(1)} %get-tuple-element.42) | copy-start | bytes 24580
  71.3 41.6 %copy-start.37 = (f32[8,256]{1,0:T(8,128)}, f32[8,256]{1,0:T(8,128)S(1)}, u32[]{:S(2)}) copy-start(f32[8,256]{1,0:T(8,128)S(1)} %fusion) | copy-start | bytes 24580
  115.4 24.1 copy-start.23
  139.6 485.4 %copy-start.4 = (bf16[256,2048]{1,0:T(8,128)(2,1)}, bf16[256,2048]{1,0:T(8,128)(2,1)S(1)}, u32[]{:S(2)}) copy-start(bf16[256,2048]{1,0:T(8,128)(2,1)S(1)} %multiply_convert_fusion.10) | copy-start | bytes 3145732
  146.8 141.2 %all-to-all-start = ((bf16[8,1,192,2048]{3,2,1,0:T(8,128)(2,1)}), bf16[8,1,192,2048]{3,2,1,0:T(8,128)(2,1)}, u32[]{:S(2)}, u32[]{:S(2)}) async-start(bf16[8,1,192,2048]{3,2,1,0:T(8,128)(2,1)} %bitcast.190), calls=%async_computation | async-start | bytes 12582912 | tf_op jit(solution)/shard_map/all_to_all | solution.py:140
  288.0 143.6 %all-to-all-start.2 = ((bf16[8,1,192,2048]{3,2,1,0:T(8,128)(2,1)}), bf16[8,1,192,2048]{3,2,1,0:T(8,128)(2,1)}, u32[]{:S(2)}, u32[]{:S(2)}) async-start(bf16[8,1,192,2048]{3,2,1,0:T(8,128)(2,1)} %bitcast.191), calls=%async_computation.2 | async-start | bytes 12582912 | tf_op jit(solution)/shard_map/all_to_all | solution.py:184
  431.6 24.4 slice-start.5
  442.6 13.4 slice-start.6
  464.6 143.4 %all-to-all-start.1 = ((bf16[2,4,192,2048]{3,2,0,1:T(8,128)(2,1)}), bf16[2,4,192,2048]{3,2,0,1:T(8,128)(2,1)}, u32[]{:S(2)}, u32[]{:S(2)}) async-start(bf16[2,4,192,2048]{3,2,0,1:T(8,128)(2,1)} %copy.121), calls=%async_computation.1 | async-start | bytes 12582912 | tf_op jit(solution)/shard_map/all_to_all | solution.py:151
  473.7 11.0 copy-start.51
  498.0 118.7 %copy-start.41 = (bf16[2048]{0:T(1024)(128)(2,1)S(1)}, bf16[2048]{0:T(1024)(128)(2,1)}, u32[]{:S(2)}) copy-start(bf16[2048]{0:T(1024)(128)(2,1)} %param.28) | copy-start | bytes 12292
  608.0 142.9 %all-to-all-start.3 = ((bf16[2,4,192,2048]{3,2,0,1:T(8,128)(2,1)}), bf16[2,4,192,2048]{3,2,0,1:T(8,128)(2,1)}, u32[]{:S(2)}, u32[]{:S(2)}) async-start(bf16[2,4,192,2048]{3,2,0,1:T(8,128)(2,1)} %copy.125), calls=%async_computation.3 | async-start | bytes 12582912 | tf_op jit(solution)/shard_map/all_to_all | solution.py:197
  616.6 208.0 %all-reduce.14.cloned.1.call-start = ((), (), s32[]{:S(2)}) async-start(), calls=%async_computation.20 | async-start | bytes 2097152 | tf_op jit(solution)/shard_map/psum | solution.py:235
  618.6 16.8 slice-start.2
  618.6 16.8 slice-start.3
  625.0 10.3 copy-start.50
  625.0 10.3 slice-start.4
  679.5 10.0 copy-start.21
  689.5 11.2 copy-start.34
  689.5 11.3 copy-start.26
  689.5 11.3 copy-start.40
  689.5 11.2 copy-start.43
  800.3 24.3 copy-start.3
  800.3 24.3 copy-start.9
  800.3 24.3 copy-start.24
  800.3 24.3 copy-start.36
  802.5 90.4 %reduce-scatter.14.cloned.1.call-start = ((), (), s32[]{:S(2)}) async-start(), calls=%async_computation.21 | async-start | bytes 2621440 | tf_op jit(solution)/shard_map/reduce_scatter | solution.py:277
  843.7 88.7 %reduce-scatter.16.cloned.1.call-start = ((), (), s32[]{:S(2)}) async-start(), calls=%async_computation.22 | async-start | bytes 2621440 | tf_op jit(solution)/shard_map/reduce_scatter | solution.py:283
  850.0 153.2 %reduce-scatter.38.cloned.1.call-start = ((), (), s32[]{:S(2)}) async-start(), calls=%async_computation.33 | async-start | bytes 7208960 | tf_op jit(solution)/shard_map/reduce_scatter | solution.py:216
  861.2 210.5 %reduce-scatter.34.cloned.1.call-start = ((), (), s32[]{:S(2)}) async-start(), calls=%async_computation.31 | async-start | bytes 7208960 | tf_op jit(solution)/shard_map/reduce_scatter | solution.py:210
  872.4 268.1 %reduce-scatter.36.cloned.1.call-start = ((), (), s32[]{:S(2)}) async-start(), calls=%async_computation.32 | async-start | bytes 7208960 | tf_op jit(solution)/shard_map/reduce_scatter | solution.py:213
  883.1 281.8 %all-reduce.16.cloned.1.call-start = ((), (), s32[]{:S(2)}) async-start(), calls=%async_computation.34 | async-start | bytes 4194304 | tf_op jit(solution)/shard_map/psum | solution.py:158
  898.6 39.2 %copy-start.45 = (bf16[256]{0:T(256)(128)(2,1)S(1)}, bf16[256]{0:T(256)(128)(2,1)}, u32[]{:S(2)}) copy-start(bf16[256]{0:T(256)(128)(2,1)} %get-tuple-element.30) | copy-start | bytes 1540
  898.6 41.7 %copy-start.5 = (bf16[256,2048]{1,0:T(8,128)(2,1)S(1)}, bf16[256,2048]{1,0:T(8,128)(2,1)}, u32[]{:S(2)}) copy-start(bf16[256,2048]{1,0:T(8,128)(2,1)} %copy-done.4) | copy-start | bytes 3145732
  937.7 308.5 %reduce-scatter.26.cloned.1.call-start = ((), (), s32[]{:S(2)}) async-start(), calls=%async_computation.27 | async-start | bytes 69632 | tf_op jit(solution)/shard_map/reduce_scatter | solution.py:313
  941.2 480.3 %reduce-scatter.24.cloned.1.call-start = ((), (), s32[]{:S(2)}) async-start(), calls=%async_computation.26 | async-start | bytes 8912896 | tf_op jit(solution)/shard_map/reduce_scatter | solution.py:311
  948.4 655.8 %reduce-scatter.18.cloned.1.call-start = ((), (), s32[]{:S(2)}) async-start(), calls=%async_computation.23 | async-start | bytes 8912896 | tf_op jit(solution)/shard_map/reduce_scatter | solution.py:308
  954.9 831.8 %reduce-scatter.22.cloned.1.call-start = ((), (), s32[]{:S(2)}) async-start(), calls=%async_computation.25 | async-start | bytes 8912896 | tf_op jit(solution)/shard_map/reduce_scatter | solution.py:310
  960.9 1008.4 %reduce-scatter.20.cloned.1.call-start = ((), (), s32[]{:S(2)}) async-start(), calls=%async_computation.24 | async-start | bytes 8912896 | tf_op jit(solution)/shard_map/reduce_scatter | solution.py:309
  966.7 1480.6 %reduce-scatter.32.cloned.1.call-start = ((), (), s32[]{:S(2)}) async-start(), calls=%async_computation.30 | async-start | bytes 24510464 | tf_op jit(solution)/shard_map/reduce_scatter | solution.py:317
  978.0 1947.7 %reduce-scatter.30.cloned.1.call-start = ((), (), s32[]{:S(2)}) async-start(), calls=%async_computation.29 | async-start | bytes 24510464 | tf_op jit(solution)/shard_map/reduce_scatter | solution.py:316
  989.4 2414.7 %reduce-scatter.28.cloned.1.call-start = ((), (), s32[]{:S(2)}) async-start(), calls=%async_computation.28 | async-start | bytes 24510464 | tf_op jit(solution)/shard_map/reduce_scatter | solution.py:315
  1075.0 165.4 %copy-start.10 = (bf16[256,2048]{1,0:T(8,128)(2,1)S(1)}, bf16[256,2048]{1,0:T(8,128)(2,1)}, u32[]{:S(2)}) copy-start(bf16[256,2048]{1,0:T(8,128)(2,1)} %all-reduce.12.cloned.1.call-done) | copy-start | bytes 3145732
  (34 other events, 131.8 us)
Sparse Core Ops, SparseCore 0:
  14.3 45.6 all-gather.4
  62.1 44.5 all-gather.2
  115.4 20.1 all-reduce.11
  802.6 21.9 all-reduce.13
  843.8 42.4 reduce-scatter.13
  889.1 43.1 reduce-scatter.15
  935.4 67.4 reduce-scatter.37
  1005.8 65.8 reduce-scatter.33
  1074.7 65.8 reduce-scatter.35
  1143.3 21.5 all-reduce.15
  1167.8 72.2 reduce-scatter.25
  1242.8 178.5 reduce-scatter.23
  1424.3 179.8 reduce-scatter.17
  1606.9 179.8 reduce-scatter.21
  1789.5 179.8 reduce-scatter.19
  1972.0 475.2 reduce-scatter.31
  2450.0 475.6 reduce-scatter.29
  2928.4 475.6 reduce-scatter.27
where the time goes:
time: 3430 us; the launch traced here: 3410 us
  waiting for transfers between devices  2820 us (82%)
  matrix products  263 us (8%)
  local copies, waits for them, and re-layouts  114 us (3%)
  blocking collectives  82.8 us (2%)
  other arithmetic  80.3 us (2%)
    reduce_scatter x1, waiting for transfers between devices, body(): lax.psum_scatter(grad_shared_gate, ('dp', 'expert'), scatter_dimension=0,...  478 us
    reduce_scatter x1, waiting for transfers between devices, body(): lax.psum_scatter(grad_shared_up, ('dp', 'expert'), scatter_dimension=0, t...  478 us
    reduce_scatter x1, waiting for transfers between devices, body(): lax.psum_scatter(grad_shared_down, ('dp', 'expert'), scatter_dimension=0,...  478 us
    reduce_scatter x1, waiting for transfers between devices, body(): lax.psum_scatter(grad_query, ('dp', 'expert'), scatter_dimension=0, tiled...  183 us
    reduce_scatter x1, waiting for transfers between devices, body(): lax.psum_scatter(grad_value, ('dp', 'expert'), scatter_dimension=0, tiled...  183 us
    reduce_scatter x1, waiting for transfers between devices, body(): lax.psum_scatter(grad_key, ('dp', 'expert'), scatter_dimension=0, tiled=T...  183 us
    reduce_scatter x1, waiting for transfers between devices, body(): lax.psum_scatter(grad_out_proj, ('dp', 'expert'), scatter_dimension=0, ti...  175 us
    all_to_all x1, waiting for transfers between devices, body(): lax.all_to_all(grads_out, 'expert', split_axis=0, concat_axis=1, tiled=True)  124 us
  transfers between devices with their start and end apart: 22, of which 19 were waited for; matrix products, arithmetic and copies ran while one was open for 9% of the time, Pallas kernels for 0%

commit v1 on v0

v1 whole, which is shorter than its diff:
```python
import jax
import jax.numpy as jnp
from jax import lax
from jax.sharding import PartitionSpec as P

HD = 128
SEQ_AXES = ("expert", "tensor")
epsilon = 1e-06
f32 = jnp.float32
bf16 = jnp.bfloat16


def norm_forward(values, gain):
    inverse = lax.rsqrt(jnp.mean(values * values, axis=-1, keepdims=True) + epsilon)
    return (values * inverse * gain, inverse)


def norm_backward(values, inverse, gain, upstream):
    scaled = upstream * gain
    gain_grad = jnp.sum(upstream * values * inverse, axis=0)
    inner = jnp.mean(scaled * values, axis=-1, keepdims=True)
    return (inverse * scaled - values * inverse * inverse * inverse * inner, gain_grad)


def cross_rows(left, right):
    return lax.dot_general(left, right, (((0,), (0,)), ((), ())), preferred_element_type=f32)


def cross_cols(left, right):
    return lax.dot_general(left, right, (((1,), (1,)), ((), ())), preferred_element_type=f32)


def dot(left, right):
    return jnp.dot(left, right, preferred_element_type=f32)


def two_parts(values):
    high = values.astype(bf16)
    return high, (values - high.astype(f32)).astype(bf16)


def gather(values):
    return lax.all_gather(values, SEQ_AXES, axis=0, tiled=True)


def scatter(values):
    return lax.psum_scatter(values.astype(bf16), SEQ_AXES, scatter_dimension=0, tiled=True).astype(f32)


def body(
    tokens, segments, routes, norm1_gain, q_weight, k_weight, v_weight, o_weight, norm2_gain,
    router_weight, shared_gate_vector, shared_gate_weight, shared_up_weight, shared_down_weight,
    expert_gate_weight, expert_up_weight, expert_down_weight, out_grad,
):
    nz = lax.axis_size("expert")
    nc = lax.axis_size("tensor")
    z = lax.axis_index("expert")
    c = lax.axis_index("tensor")
    rows, width = tokens.shape
    own_rows = rows // nc
    local_count, _, ffn = expert_gate_weight.shape
    expert_count = local_count * nz
    head_cols = q_weight.shape[1] // nz
    shared_cols = shared_gate_weight.shape[1] // nz
    heads = head_cols // HD
    seq = rows * nz
    scale = HD ** (-0.5)
    gain1 = norm1_gain.astype(f32)
    gain2 = norm2_gain.astype(f32)

    def own(values):
        return lax.dynamic_slice_in_dim(values, c * own_rows, own_rows, 0)

    def head_slice(values):
        return lax.dynamic_slice_in_dim(values, z * head_cols, head_cols, 1)

    def shared_slice(values):
        return lax.dynamic_slice_in_dim(values, z * shared_cols, shared_cols, 1)

    x_all_rows = tokens.astype(f32)
    inverse_one_rows = lax.rsqrt(jnp.mean(x_all_rows * x_all_rows, axis=-1) + epsilon)
    x = own(tokens).astype(f32)
    n1_own, inv1 = norm_forward(x, gain1)
    n1 = gather(n1_own.astype(bf16))
    dy = gather(own(out_grad))
    all_routes = lax.all_gather(routes, "expert", axis=0, tiled=True)
    labels = lax.all_gather(segments, "expert", axis=1, tiled=True)[0]

    wq, wk, wv, wo = head_slice(q_weight), head_slice(k_weight), head_slice(v_weight), head_slice(o_weight)
    q = dot(n1, wq).astype(bf16).reshape(seq, heads, HD)
    k = dot(n1, wk).astype(bf16).reshape(seq, heads, HD)
    v = dot(n1, wv).astype(bf16).reshape(seq, heads, HD)
    pos = jnp.arange(seq)
    allowed = (pos[None, :] <= pos[:, None]) & (labels[None, :] == labels[:, None])

    def masked_scores():
        raw = jnp.einsum("qhd,khd->hqk", q, k, preferred_element_type=f32) * scale
        return jnp.where(allowed[None], raw, -jnp.inf)

    scores = masked_scores()
    top = jnp.max(scores, axis=-1, keepdims=True)
    expd = jnp.exp(scores - top)
    total = jnp.sum(expd, axis=-1, keepdims=True)
    log_total = top + jnp.log(total)
    p_low = (expd / total).astype(bf16)
    o = jnp.einsum("hqk,khd->qhd", p_low, v, preferred_element_type=f32).reshape(seq, head_cols).astype(bf16)
    h = x + scatter(cross_cols(o, wo))
    n2_own, inv2 = norm_forward(h, gain2)
    n2 = gather(n2_own.astype(bf16))

    probs = jax.nn.softmax(dot(n2, router_weight), axis=-1)
    chosen = jnp.any(all_routes[:, :, None] == jnp.arange(expert_count)[None, None, :], axis=1)
    gates = jnp.where(chosen, probs, 0.0)
    sigma = jax.nn.sigmoid(dot(n2, shared_gate_vector))

    branch = None
    d_n2 = None
    grads = []
    d_gate_parts = []
    for index in range(local_count + 1):
        if index < local_count:
            w_gate, w_up, w_down = expert_gate_weight[index], expert_up_weight[index], expert_down_weight[index]
            gate = lax.dynamic_slice_in_dim(gates, z * local_count + index, 1, 1)
        else:
            w_gate, w_up, w_down = map(shared_slice, (shared_gate_weight, shared_up_weight, shared_down_weight))
            gate = sigma[:, None]
        a = dot(n2, w_gate)
        b = dot(n2, w_up)
        back = dot(dy, w_down)
        sig = jax.nn.sigmoid(a)
        act = a * sig
        u = act * b
        gu = (gate * u).astype(bf16)
        d_gate_parts.append(jnp.sum(u * back, axis=-1, keepdims=True))
        du = gate * back
        da = (du * b * (sig * (1.0 + a * (1.0 - sig)))).astype(bf16)
        db = (du * act).astype(bf16)
        part = cross_cols(gu, w_down)
        branch = part if branch is None else branch + part
        part = cross_cols(da, w_gate) + cross_cols(db, w_up)
        d_n2 = part if d_n2 is None else d_n2 + part
        grads.append((cross_rows(n2, da), cross_rows(n2, db), cross_rows(dy, gu)))

    d_expert = jnp.concatenate(d_gate_parts[:local_count], axis=1)
    d_probs = lax.dynamic_update_slice_in_dim(jnp.zeros_like(probs), d_expert, z * local_count, 1)
    d_probs = jnp.where(chosen, d_probs, 0.0)
    d_logits = probs * (d_probs - jnp.sum(probs * d_probs, axis=-1, keepdims=True))
    d_vector = d_gate_parts[local_count] * (sigma * (1.0 - sigma))[:, None]
    small = jnp.concatenate([d_logits, d_vector], axis=1)
    small_high, small_low = two_parts(small)
    small_weights = jnp.concatenate([router_weight, shared_gate_vector[:, None]], axis=1)
    d_n2 = d_n2 + cross_cols(small_high, small_weights)
    small_grad = cross_rows(n2, jnp.concatenate([small_high, small_low], axis=1))
    small_grad = small_grad[:, : expert_count + 1] + small_grad[:, expert_count + 1 :]

    d_n2_own = scatter(d_n2)
    branch_own = scatter(branch)
    upstream = own(out_grad).astype(f32)
    d_norm, grad_two = norm_backward(h, inv2, gain2, d_n2_own)
    dh = upstream + d_norm
    dhr = gather(dh.astype(bf16))
    d_o = dot(dhr, wo).astype(bf16).reshape(seq, heads, HD)
    grad_o = cross_rows(dhr, o)

    pf = jnp.exp(masked_scores() - log_total)
    pb = pf.astype(bf16)
    d_v = jnp.einsum("hqk,qhd->khd", pb, d_o, preferred_element_type=f32)
    dp = jnp.einsum("qhd,khd->hqk", d_o, v, preferred_element_type=f32)
    ds = (pf * (dp - jnp.sum(pf * dp, axis=-1, keepdims=True))).astype(bf16)
    d_q = jnp.einsum("hqk,khd->qhd", ds, k, preferred_element_type=f32) * scale
    d_k = jnp.einsum("hqk,qhd->khd", ds, q, preferred_element_type=f32) * scale
    d_q, d_k, d_v = (t.reshape(seq, head_cols).astype(bf16) for t in (d_q, d_k, d_v))
    grad_q, grad_k, grad_v = cross_rows(n1, d_q), cross_rows(n1, d_k), cross_rows(n1, d_v)
    d_n1 = cross_cols(d_q, wq) + cross_cols(d_k, wk) + cross_cols(d_v, wv)
    d_norm1, grad_one = norm_backward(x, inv1, gain1, scatter(d_n1))

    def pair(values):
        return lax.all_gather(values, "tensor", axis=0, tiled=True)

    layer_out = pair(h + branch_own)
    input_grad = pair(dh + d_norm1)
    inv2_rows = pair(inv2[:, 0])
    stats = jnp.stack([inverse_one_rows, inv2_rows])

    def over_dp(grad):
        return lax.psum_scatter(grad.astype(bf16), "dp", scatter_dimension=0, tiled=True)

    def over_all(grad):
        part = over_dp(grad)
        return lax.all_to_all(part, "expert", split_axis=0, concat_axis=1, tiled=True).astype(f32)

    small_all = jnp.concatenate([grad_one[:, None], grad_two[:, None], small_grad], axis=1)
    small_all = lax.psum_scatter(small_all, ("dp", "expert"), scatter_dimension=0, tiled=True)
    small_all = lax.psum(small_all, "tensor")
    g_one, g_two, g_router, g_vector = small_all[:, 0], small_all[:, 1], small_all[:, 2 : 2 + expert_count], small_all[:, 2 + expert_count]
    e_grads = [jnp.stack([over_dp(grads[i][j]) for i in range(local_count)]).astype(f32) for j in range(3)]
    s_grads = [over_all(grads[local_count][j]) for j in range(3)]
    g_q, g_k, g_v, g_o = (over_all(t) for t in (grad_q, grad_k, grad_v, grad_o))
    return (
        layer_out, input_grad, stats, g_one, g_q, g_k, g_v, g_o, g_two, g_router, g_vector,
        s_grads[0], s_grads[1], s_grads[2], e_grads[0], e_grads[1], e_grads[2],
    )


def solution(mesh):
    both = ("dp", "expert")
    cols = P(None, "tensor")
    placed = (
        P(both, None), P("dp", "expert"), P(both, None), P(), cols, cols, cols, cols, P(), P(), P(),
        cols, cols, cols, P("expert", None, "tensor"), P("expert", None, "tensor"),
        P("expert", None, "tensor"), P(both, None),
    )
    split = P(both, "tensor")
    experts = P("expert", "dp", "tensor")
    return jax.shard_map(
        body,
        mesh=mesh,
        in_specs=placed,
        out_specs=(
            P(both, None), P(both, None), P(None, both), P(both), split, split, split, split, P(both),
            P(both, None), P(both), split, split, split, experts, experts, experts,
        ),
        check_vma=False,
    )
```

time: 3430 us -> 1220 us (0.36)
  waiting for transfers between devices: 2820 us -> 764 us
  local copies, waits for them, and re-layouts: 114 us -> 21.4 us
  other arithmetic: 80.3 us -> 34.3 us
    reduce_scatter x13 -> x18, waiting for transfers between devices: 2320 us -> 599 us  [the longest x13 378 us: over_dp(): lax.psum_scatter(grad.astype(bf16), 'dp', scatter_dimension=0, tiled=True)]
    all_to_all x4 -> x6, waiting for transfers between devices: 381 us -> 8.83 us  [over_all(): lax.all_to_all(part, 'expert', split_axis=0, concat_axis=1, tiled=True)]
    all_gather x2 -> x6, waiting for transfers between devices: 62.5 us -> 155 us  [the longest x4 131 us: gather(): return lax.all_gather(values, SEQ_AXES, axis=0, tiled=True)]
    unnamed x1 -> x0, blocking collectives: 71.9 us -> none
    dot_general x27 -> x21, matrix products: 166 us -> 98 us  [the longest x15 85.2 us: dot(): return jnp.dot(left, right, preferred_element_type=f32)]
    dot_general x7 -> x14, matrix products: 38.1 us -> 99.9 us  [cross_cols(): lax.dot_general(left, right, (((1,), (1,)), ((), ())), preferred_element_...]
    psum x3 -> x0, waiting for transfers between devices: 55.6 us -> none  [the longest x1 22 us: body(): lax.psum(d_routed.astype(jnp.bfloat16), 'tensor').astype(jnp.float32)]
    gather x4 -> x0, local copies, waits for them, and re-layouts: 49.9 us -> none  [the longest x1 15.4 us: body(): padded_grads[owners].reshape(expert_count, 1, slot_count, feat_width)]
  transfers between devices with their start and end apart: 22 -> 30, of which waited for: 19 -> 24; matrix products, arithmetic and copies ran while one was open for 9% -> 16% of each run, Pallas kernels for 0% -> 0%
where the time goes in v1:
time: 1220 us; the launch traced here: 1210 us
  waiting for transfers between devices  764 us (63%)
  matrix products  286 us (23%)
  blocking collectives  49.5 us (4%)
  starting transfers between devices  36.5 us (3%)
  other arithmetic  34.3 us (3%)
  local copies, waits for them, and re-layouts  21.4 us (2%)
  between operations  15.5 us (1%)
    reduce_scatter x13, waiting for transfers between devices, over_dp(): lax.psum_scatter(grad.astype(bf16), 'dp', scatter_dimension=0, tiled=True)  378 us
    reduce_scatter x4, waiting for transfers between devices, scatter(): lax.psum_scatter(values.astype(bf16), SEQ_AXES, scatter_dimension=0, tile...  161 us
    all_gather x4, waiting for transfers between devices, gather(): return lax.all_gather(values, SEQ_AXES, axis=0, tiled=True)  131 us
    dot_general x14, matrix products, cross_cols(): lax.dot_general(left, right, (((1,), (1,)), ((), ())), preferred_element_...  99.9 us
    dot_general x14, matrix products, cross_rows(): lax.dot_general(left, right, (((0,), (0,)), ((), ())), preferred_element_...  88 us
    dot_general x15, matrix products, dot(): return jnp.dot(left, right, preferred_element_type=f32)  85.2 us
    reduce_scatter x1, waiting for transfers between devices, body(): lax.psum_scatter(small_all, ('dp', 'expert'), scatter_dimension=0, tiled=...  60.4 us
    all_to_all x6, starting transfers between devices, over_all(): lax.all_to_all(part, 'expert', split_axis=0, concat_axis=1, tiled=True)  34.6 us
  transfers between devices with their start and end apart: 30, of which 24 were waited for; matrix products, arithmetic and copies ran while one was open for 16% of the time, Pallas kernels for 0%

profile of v1, /device:TPU:8, one launch (start us, length us, event | category | flops | bytes accessed | tf_op | source)
XLA Modules:
  0.0 1206.8 jit_solution(6768008457152341075)
XLA Ops:
  11.3 8.4 all_gather.30
  20.3 37.8 %all-gather.8.cloned.1.call-done = bf16[1024,2048]{1,0:T(8,128)(2,1)} async-done(((bf16[128,2048]{1,0:T(8,128)(2,1)}), bf16[1024,2048]{1,0:T(8,128)(2,1)}) %all-gather.8.cloned.1.call-update) | async-done | bytes 4194320 | tf_op jit(solution)/shard_map/all_gather | solution.py:43
  78.6 46.5 %reduce-scatter.19.cloned.1.call-done = bf16[128,2048]{1,0:T(8,128)(2,1)} async-done(((bf16[1024,2048]{1,0:T(8,128)(2,1)}), bf16[128,2048]{1,0:T(8,128)(2,1)}) %reduce-scatter.19.cloned.1.call-update) | async-done | bytes 524304 | tf_op jit(solution)/shard_map/reduce_scatter | solution.py:47
  130.0 14.6 %all_gather.32 = s32[1024,4]{0,1:T(4,128)S(1)} all-gather(s32[256,4]{0,1:T(4,128)S(1)} %copy-done.21), channel_id=1, replica_groups=mesh['dp'=4,'expert'=4,'tensor'=2] {'expert'}, dimensions={0}, use_global_device_ids=true | all-gather | bytes 20480 | tf_op jit(solution)/shard_map/all_gather | solution.py:86
  144.7 32.1 %all-gather.10.cloned.1.call-done = bf16[1024,2048]{1,0:T(8,128)(2,1)} async-done(((bf16[128,2048]{1,0:T(8,128)(2,1)}), bf16[1024,2048]{1,0:T(8,128)(2,1)}) %all-gather.10.cloned.1.call-update) | async-done | bytes 4194320 | tf_op jit(solution)/shard_map/all_gather | solution.py:43
  180.4 7.7 fusion.39
  188.0 7.7 fusion.43
  195.7 29.0 %all-gather.14.cloned.1.call-done = bf16[1024,2048]{1,0:T(8,128)(2,1)} async-done(((bf16[128,2048]{1,0:T(8,128)(2,1)}), bf16[1024,2048]{1,0:T(8,128)(2,1)}) %all-gather.14.cloned.1.call-update) | async-done | bytes 4194320 | tf_op jit(solution)/shard_map/all_gather | solution.py:43
  224.7 12.7 %multiply_reduce_fusion.1 = (f32[1024]{0:T(1024)S(1)}, bf16[1024,704]{0,1:T(8,128)(2,1)}, bf16[1024,704]{0,1:T(8,128)(2,1)}, bf16[1024,704]{0,1:T(8,128)(2,1)S(1)}) fusion(f32[1024,704]{0,1:T(8,128)} %fusion.39, f32[1024,704]{0,1:T(8,128)} %fusion.43, f32[1024]{0:T(1024)S(1)} %add_divide_fusion.3, bf16[1024,2048]{1,0:T(8,128)(2,1)} %all-gather.14.cloned.1.call-done, ...), kind=kOutput, calls=%fused_computation.50 | convolution fusion | flops 2966486016 | bytes 17440772 | tf_op jit(solution)/shard_map/dot_general | solution.py:34
  238.7 7.1 fusion.13
  260.3 9.0 multiply_reduce_fusion.2
  269.3 8.1 multiply_reduce_fusion.3
  300.3 9.9 fusion.37
  310.3 9.5 fusion.41
  319.8 18.9 %add_convert_fusion.1 = bf16[1024,2048]{1,0:T(8,128)(2,1)} fusion(f32[1024,2048]{1,0:T(8,128)} %fusion.41, f32[1024,2048]{1,0:T(8,128)} %fusion.37, f32[1024,2048]{1,0:T(8,128)} %fusion.15, f32[1024,2048]{1,0:T(8,128)} %fusion.11, f32[1024,2048]{1,0:T(8,128)} %fusion.27, f32[1024,2048]{1,0:T(8,128)} %fusion.23, bf16[2048,1]{0,1:T(2,128)(2,1)S(1)} %reshape.207, ...), kind=kOutput, calls=%fused_computation.4 | convolution fusion | flops 52539392 | bytes 54599680 | tf_op jit(solution)/shard_map/dot_general | solution.py:30
  338.7 46.4 %reduce-scatter.23.cloned.1.call-done = bf16[128,2048]{1,0:T(8,128)(2,1)} async-done(((bf16[1024,2048]{1,0:T(8,128)(2,1)}), bf16[128,2048]{1,0:T(8,128)(2,1)}) %reduce-scatter.23.cloned.1.call-update) | async-done | bytes 524304 | tf_op jit(solution)/shard_map/reduce_scatter | solution.py:47
  389.0 7.4 convolution_convert_fusion.9
  396.4 7.6 convolution_convert_fusion.7
  404.5 32.2 %all-gather.16.cloned.1.call-done = bf16[1024,2048]{1,0:T(8,128)(2,1)} async-done(((bf16[128,2048]{1,0:T(8,128)(2,1)}), bf16[1024,2048]{1,0:T(8,128)(2,1)}) %all-gather.16.cloned.1.call-update) | async-done | bytes 4194320 | tf_op jit(solution)/shard_map/all_gather | solution.py:43
  462.9 6.0 fusion.9
  468.9 7.7 fusion.21
  476.6 10.7 add_convert_fusion.2
  487.3 7.4 convolution_convert_fusion.8
  504.3 7.4 convolution_convert_fusion.1
  511.8 7.3 convolution_convert_fusion.2
  519.2 7.4 convolution_convert_fusion.5
  526.7 7.5 convolution_convert_fusion.6
  539.1 7.4 convolution_convert_fusion.3
  546.6 7.4 convolution_convert_fusion.4
  563.8 6.2 all-to-all-start.4
  572.2 12.3 %reduce-scatter.25.cloned.1.call-done = bf16[128,2048]{1,0:T(8,128)(2,1)} async-done(((bf16[1024,2048]{1,0:T(8,128)(2,1)}), bf16[128,2048]{1,0:T(8,128)(2,1)}) %reduce-scatter.25.cloned.1.call-update) | async-done | bytes 524304 | tf_op jit(solution)/shard_map/reduce_scatter | solution.py:47
  591.0 7.8 all-to-all-start.6
  598.8 55.3 %reduce-scatter.21.cloned.1.call-done = bf16[128,2048]{1,0:T(8,128)(2,1)} async-done(((bf16[1024,2048]{1,0:T(8,128)(2,1)}), bf16[128,2048]{1,0:T(8,128)(2,1)}) %reduce-scatter.21.cloned.1.call-update) | async-done | bytes 524304 | tf_op jit(solution)/shard_map/reduce_scatter | solution.py:47
  657.7 43.2 %reduce-scatter.39.cloned.1.call-done = bf16[512,704]{0,1:T(8,128)(2,1)} async-done(((bf16[2048,704]{0,1:T(8,128)(2,1)}), bf16[512,704]{0,1:T(8,128)(2,1)}) %reduce-scatter.39.cloned.1.call-update) | async-done | bytes 720912 | tf_op jit(solution)/shard_map/reduce_scatter | solution.py:186
  702.2 22.1 %all_to_all.91 = bf16[4,128,704]{1,2,0:T(8,128)(2,1)} all-to-all(bf16[4,128,704]{1,2,0:T(8,128)(2,1)S(1)} %copy_bitcast_fusion.1), channel_id=1, replica_groups=mesh['dp'=4,'expert'=4,'tensor'=2] {'expert'}, dimensions={0} | all-to-all | bytes 1441792 | tf_op jit(solution)/shard_map/all_to_all | solution.py:190
  724.3 7.1 reduce-scatter.35.cloned.1.call-done
  738.9 24.0 %reduce-scatter.33.cloned.1.call-done = bf16[512,256]{1,0:T(8,128)(2,1)} async-done(((bf16[2048,256]{1,0:T(8,128)(2,1)}), bf16[512,256]{1,0:T(8,128)(2,1)}) %reduce-scatter.33.cloned.1.call-update) | async-done | bytes 262160 | tf_op jit(solution)/shard_map/reduce_scatter | solution.py:186
  768.6 39.0 %reduce-scatter.53.cloned.1.call-done = bf16[512,704]{0,1:T(8,128)(2,1)} async-done(((bf16[2048,704]{0,1:T(8,128)(2,1)}), bf16[512,704]{0,1:T(8,128)(2,1)}) %reduce-scatter.53.cloned.1.call-update) | async-done | bytes 720912 | tf_op jit(solution)/shard_map/reduce_scatter | solution.py:186
  807.6 44.7 %reduce-scatter.51.cloned.1.call-done = bf16[512,704]{0,1:T(8,128)(2,1)} async-done(((bf16[2048,704]{0,1:T(8,128)(2,1)}), bf16[512,704]{0,1:T(8,128)(2,1)}) %reduce-scatter.51.cloned.1.call-update) | async-done | bytes 720912 | tf_op jit(solution)/shard_map/reduce_scatter | solution.py:186
  855.4 41.6 %reduce-scatter.45.cloned.1.call-done = bf16[512,704]{0,1:T(8,128)(2,1)} async-done(((bf16[2048,704]{0,1:T(8,128)(2,1)}), bf16[512,704]{0,1:T(8,128)(2,1)}) %reduce-scatter.45.cloned.1.call-update) | async-done | bytes 720912 | tf_op jit(solution)/shard_map/reduce_scatter | solution.py:186
  896.9 44.7 %reduce-scatter.43.cloned.1.call-done = bf16[512,704]{0,1:T(8,128)(2,1)} async-done(((bf16[2048,704]{0,1:T(8,128)(2,1)}), bf16[512,704]{0,1:T(8,128)(2,1)}) %reduce-scatter.43.cloned.1.call-update) | async-done | bytes 720912 | tf_op jit(solution)/shard_map/reduce_scatter | solution.py:186
  944.7 28.0 %reduce-scatter.29.cloned.1.call-done = bf16[512,256]{1,0:T(8,128)(2,1)} async-done(((bf16[2048,256]{1,0:T(8,128)(2,1)}), bf16[512,256]{1,0:T(8,128)(2,1)}) %reduce-scatter.29.cloned.1.call-update) | async-done | bytes 262160 | tf_op jit(solution)/shard_map/reduce_scatter | solution.py:186
  977.8 40.0 %reduce-scatter.49.cloned.1.call-done = bf16[512,704]{0,1:T(8,128)(2,1)} async-done(((bf16[2048,704]{0,1:T(8,128)(2,1)}), bf16[512,704]{0,1:T(8,128)(2,1)}) %reduce-scatter.49.cloned.1.call-update) | async-done | bytes 720912 | tf_op jit(solution)/shard_map/reduce_scatter | solution.py:186
  1017.8 45.0 %reduce-scatter.47.cloned.1.call-done = bf16[512,704]{0,1:T(8,128)(2,1)} async-done(((bf16[2048,704]{0,1:T(8,128)(2,1)}), bf16[512,704]{0,1:T(8,128)(2,1)}) %reduce-scatter.47.cloned.1.call-update) | async-done | bytes 720912 | tf_op jit(solution)/shard_map/reduce_scatter | solution.py:186
  1072.8 20.9 %reduce-scatter.31.cloned.1.call-done = bf16[512,256]{1,0:T(8,128)(2,1)} async-done(((bf16[2048,256]{1,0:T(8,128)(2,1)}), bf16[512,256]{1,0:T(8,128)(2,1)}) %reduce-scatter.31.cloned.1.call-update) | async-done | bytes 262160 | tf_op jit(solution)/shard_map/reduce_scatter | solution.py:186
  1106.8 60.4 %reduce-scatter.27.cloned.1.call-done = f32[128,11]{0,1:T(8,128)} async-done(((f32[2048,11]{0,1:T(8,128)}), f32[128,11]{0,1:T(8,128)}) %reduce-scatter.27.cloned.1.call-update) | async-done | bytes 5648 | tf_op jit(solution)/shard_map/reduce_scatter | solution.py:193
  1170.9 10.3 all-gather.18.cloned.1.call-done
  1181.2 13.8 %all-gather.12.cloned.1.call-done = f32[256,2048]{1,0:T(8,128)} async-done(((f32[128,2048]{1,0:T(8,128)}), f32[256,2048]{1,0:T(8,128)}) %all-gather.12.cloned.1.call-update) | async-done | bytes 2097168 | tf_op jit(solution)/shard_map/all_gather | solution.py:178
  (237 shorter events, 196.2 us)
Async XLA Ops:
  7.2 51.0 %all-gather.8.cloned.1.call-start = ((), (), s32[]{:S(2)}) async-start(), calls=%async_computation.25 | async-start | bytes 4718592 | tf_op jit(solution)/shard_map/all_gather | solution.py:43
  8.5 11.3 copy-start.17
  9.2 10.6 copy-start.15
  11.2 113.9 %reduce-scatter.19.cloned.1.call-start = ((), (), s32[]{:S(2)}) async-start(), calls=%async_computation.26 | async-start | bytes 4718592 | tf_op jit(solution)/shard_map/reduce_scatter | solution.py:47
  73.9 51.2 %copy-start.3 = (bf16[256,2048]{1,0:T(8,128)(2,1)S(1)}, bf16[256,2048]{1,0:T(8,128)(2,1)}, u32[]{:S(2)}) copy-start(bf16[256,2048]{1,0:T(8,128)(2,1)} %param.18) | copy-start | bytes 3145732
  78.5 50.6 %copy-start.7 = (bf16[256,2048]{1,0:T(8,128)(2,1)S(1)}, bf16[256,2048]{1,0:T(8,128)(2,1)}, u32[]{:S(2)}) copy-start(bf16[256,2048]{1,0:T(8,128)(2,1)} %param.35) | copy-start | bytes 3145732
  78.5 51.5 %copy-start.20 = (bf16[2048]{0:T(1024)(128)(2,1)S(1)}, bf16[2048]{0:T(1024)(128)(2,1)}, u32[]{:S(2)}) copy-start(bf16[2048]{0:T(1024)(128)(2,1)} %param.28) | copy-start | bytes 12292
  78.5 51.5 %copy-start.21 = (s32[256,4]{0,1:T(4,128)S(1)}, s32[256,4]{0,1:T(4,128)}, u32[]{:S(2)}) copy-start(s32[256,4]{0,1:T(4,128)} %param.20) | copy-start | bytes 12292
  78.5 98.3 %all-gather.10.cloned.1.call-start = ((), (), s32[]{:S(2)}) async-start(), calls=%async_computation.27 | async-start | bytes 4718592 | tf_op jit(solution)/shard_map/all_gather | solution.py:43
  129.0 95.7 %all-gather.14.cloned.1.call-start = ((), (), s32[]{:S(2)}) async-start(), calls=%async_computation.30 | async-start | bytes 4718592 | tf_op jit(solution)/shard_map/all_gather | solution.py:43
  129.9 255.2 %reduce-scatter.23.cloned.1.call-start = ((), (), s32[]{:S(2)}) async-start(), calls=%async_computation.31 | async-start | bytes 4718592 | tf_op jit(solution)/shard_map/reduce_scatter | solution.py:47
  195.7 41.7 %copy-start.14 = (bf16[2048,8]{0,1:T(8,128)(2,1)S(1)}, bf16[2048,8]{0,1:T(8,128)(2,1)}, u32[]{:S(2)}) copy-start(bf16[2048,8]{0,1:T(8,128)(2,1)} %param.27) | copy-start | bytes 98308
  224.7 12.7 %copy-start.2 = (bf16[1024,2048]{1,0:T(8,128)(2,1)S(1)}, bf16[1024,2048]{1,0:T(8,128)(2,1)}, u32[]{:S(2)}) copy-start(bf16[1024,2048]{1,0:T(8,128)(2,1)} %all-gather.10.cloned.1.call-done) | copy-start | bytes 12582916
  237.4 62.9 %copy-start.26 = (bf16[1024,704]{0,1:T(8,128)(2,1)}, bf16[1024,704]{0,1:T(8,128)(2,1)S(1)}, u32[]{:S(2)}) copy-start(bf16[1024,704]{0,1:T(8,128)(2,1)S(1)} %get-tuple-element.79) | copy-start | bytes 4325380
  238.7 11.8 slice-start.4
  269.3 19.6 %copy-start.29 = (bf16[1024,704]{0,1:T(8,128)(2,1)}, bf16[1024,704]{0,1:T(8,128)(2,1)S(1)}, u32[]{:S(2)}) copy-start(bf16[1024,704]{0,1:T(8,128)(2,1)S(1)} %get-tuple-element.81) | copy-start | bytes 4325380
  300.3 9.9 copy-start.27
  338.7 46.5 %copy-start.4 = (bf16[128,2048]{1,0:T(8,128)(2,1)S(1)}, bf16[128,2048]{1,0:T(8,128)(2,1)}, u32[]{:S(2)}) copy-start(bf16[128,2048]{1,0:T(8,128)(2,1)} %reduce-scatter.19.cloned.1.call-done) | copy-start | bytes 1572868
  338.7 98.0 %all-gather.16.cloned.1.call-start = ((), (), s32[]{:S(2)}) async-start(), calls=%async_computation.32 | async-start | bytes 4718592 | tf_op jit(solution)/shard_map/all_gather | solution.py:43
  389.0 172.7 %reduce-scatter.37.cloned.1.call-start = ((), (), s32[]{:S(2)}) async-start(), calls=%async_computation.40 | async-start | bytes 3604480 | tf_op jit(solution)/shard_map/reduce_scatter | solution.py:186
  396.4 173.7 %reduce-scatter.41.cloned.1.call-start = ((), (), s32[]{:S(2)}) async-start(), calls=%async_computation.42 | async-start | bytes 3604480 | tf_op jit(solution)/shard_map/reduce_scatter | solution.py:186
  404.1 180.4 %reduce-scatter.25.cloned.1.call-start = ((), (), s32[]{:S(2)}) async-start(), calls=%async_computation.33 | async-start | bytes 4718592 | tf_op jit(solution)/shard_map/reduce_scatter | solution.py:47
  462.6 191.5 %reduce-scatter.21.cloned.1.call-start = ((), (), s32[]{:S(2)}) async-start(), calls=%async_computation.28 | async-start | bytes 4718592 | tf_op jit(solution)/shard_map/reduce_scatter | solution.py:47
  487.3 213.7 %reduce-scatter.39.cloned.1.call-start = ((), (), s32[]{:S(2)}) async-start(), calls=%async_computation.41 | async-start | bytes 3604480 | tf_op jit(solution)/shard_map/reduce_scatter | solution.py:186
  494.7 236.8 %reduce-scatter.35.cloned.1.call-start = ((), (), s32[]{:S(2)}) async-start(), calls=%async_computation.39 | async-start | bytes 1310720 | tf_op jit(solution)/shard_map/reduce_scatter | solution.py:186
  499.4 263.5 %reduce-scatter.33.cloned.1.call-start = ((), (), s32[]{:S(2)}) async-start(), calls=%async_computation.38 | async-start | bytes 1310720 | tf_op jit(solution)/shard_map/reduce_scatter | solution.py:186
  504.2 303.4 %reduce-scatter.53.cloned.1.call-start = ((), (), s32[]{:S(2)}) async-start(), calls=%async_computation.48 | async-start | bytes 3604480 | tf_op jit(solution)/shard_map/reduce_scatter | solution.py:186
  511.7 340.5 %reduce-scatter.51.cloned.1.call-start = ((), (), s32[]{:S(2)}) async-start(), calls=%async_computation.47 | async-start | bytes 3604480 | tf_op jit(solution)/shard_map/reduce_scatter | solution.py:186
  519.2 377.8 %reduce-scatter.45.cloned.1.call-start = ((), (), s32[]{:S(2)}) async-start(), calls=%async_computation.44 | async-start | bytes 3604480 | tf_op jit(solution)/shard_map/reduce_scatter | solution.py:186
  526.6 415.0 %reduce-scatter.43.cloned.1.call-start = ((), (), s32[]{:S(2)}) async-start(), calls=%async_computation.43 | async-start | bytes 3604480 | tf_op jit(solution)/shard_map/reduce_scatter | solution.py:186
  534.2 438.5 %reduce-scatter.29.cloned.1.call-start = ((), (), s32[]{:S(2)}) async-start(), calls=%async_computation.36 | async-start | bytes 1310720 | tf_op jit(solution)/shard_map/reduce_scatter | solution.py:186
  538.8 479.0 %reduce-scatter.49.cloned.1.call-start = ((), (), s32[]{:S(2)}) async-start(), calls=%async_computation.46 | async-start | bytes 3604480 | tf_op jit(solution)/shard_map/reduce_scatter | solution.py:186
  546.5 516.3 %reduce-scatter.47.cloned.1.call-start = ((), (), s32[]{:S(2)}) async-start(), calls=%async_computation.45 | async-start | bytes 3604480 | tf_op jit(solution)/shard_map/reduce_scatter | solution.py:186
  554.0 539.7 %reduce-scatter.31.cloned.1.call-start = ((), (), s32[]{:S(2)}) async-start(), calls=%async_computation.37 | async-start | bytes 1310720 | tf_op jit(solution)/shard_map/reduce_scatter | solution.py:186
  558.7 25.8 %copy-start.16 = (f32[2048]{0:T(1024)S(1)}, f32[2048]{0:T(1024)}, u32[]{:S(2)}) copy-start(f32[2048]{0:T(1024)} %copy-done.15) | copy-start | bytes 24580
  558.7 25.8 %copy-start.18 = (f32[128]{0:T(128)S(1)}, f32[128]{0:T(128)}, u32[]{:S(2)}) copy-start(f32[128]{0:T(128)} %copy-done.17) | copy-start | bytes 1540
  561.6 92.5 %copy-start.5 = (bf16[128,2048]{1,0:T(8,128)(2,1)S(1)}, bf16[128,2048]{1,0:T(8,128)(2,1)}, u32[]{:S(2)}) copy-start(bf16[128,2048]{1,0:T(8,128)(2,1)} %reduce-scatter.23.cloned.1.call-done) | copy-start | bytes 1572868
  563.8 27.2 %all-to-all-start.4 = ((bf16[4,128,704]{1,2,0:T(8,128)(2,1)}), bf16[4,128,704]{1,2,0:T(8,128)(2,1)S(1)}, u32[]{:S(2)}, u32[]{:S(2)}) async-start(bf16[4,128,704]{1,2,0:T(8,128)(2,1)} %copy_bitcast_fusion.2), calls=%async_computation.14 | async-start | bytes 1441792 | tf_op jit(solution)/shard_map/all_to_all | solution.py:190
  570.0 597.2 %reduce-scatter.27.cloned.1.call-start = ((), (), s32[]{:S(2)}) async-start(), calls=%async_computation.35 | async-start | bytes 139264 | tf_op jit(solution)/shard_map/reduce_scatter | solution.py:193
  591.0 111.2 %all-to-all-start.6 = ((bf16[4,128,704]{1,2,0:T(8,128)(2,1)}), bf16[4,128,704]{1,2,0:T(8,128)(2,1)}, u32[]{:S(2)}, u32[]{:S(2)}) async-start(bf16[4,128,704]{1,2,0:T(8,128)(2,1)} %copy_bitcast_fusion), calls=%async_computation.18 | async-start | bytes 1441792 | tf_op jit(solution)/shard_map/all_to_all | solution.py:190
  598.8 582.4 %all-gather.18.cloned.1.call-start = ((), (), s32[]{:S(2)}) async-start(), calls=%async_computation.34 | async-start | bytes 3145728 | tf_op jit(solution)/shard_map/all_gather | solution.py:178
  657.7 79.5 %copy-start.24 = (f32[1,1,128]{2,1,0:T(1,128)S(1)}, f32[1,1,128]{2,1,0:T(1,128)}, u32[]{:S(2)}) copy-start(f32[1,1,128]{2,1,0:T(1,128)} %get-tuple-element.91) | copy-start | bytes 1540
  731.5 31.5 %all-to-all-start.3 = ((bf16[4,128,256]{2,1,0:T(8,128)(2,1)}), bf16[4,128,256]{2,1,0:T(8,128)(2,1)S(1)}, u32[]{:S(2)}, u32[]{:S(2)}) async-start(bf16[4,128,256]{2,1,0:T(8,128)(2,1)} %bitcast.219), calls=%async_computation.12 | async-start | bytes 524288 | tf_op jit(solution)/shard_map/all_to_all | solution.py:190
  736.6 458.5 %all-gather.12.cloned.1.call-start = ((), (), s32[]{:S(2)}) async-start(), calls=%async_computation.29 | async-start | bytes 3145728 | tf_op jit(solution)/shard_map/all_gather | solution.py:178
  762.9 209.7 %all-to-all-start.2 = ((bf16[4,128,256]{2,1,0:T(8,128)(2,1)}), bf16[4,128,256]{2,1,0:T(8,128)(2,1)S(1)}, u32[]{:S(2)}, u32[]{:S(2)}) async-start(bf16[4,128,256]{2,1,0:T(8,128)(2,1)} %bitcast.217), calls=%async_computation.10 | async-start | bytes 524288 | tf_op jit(solution)/shard_map/all_to_all | solution.py:190
  972.6 121.0 %all-to-all-start = ((bf16[4,128,256]{2,1,0:T(8,128)(2,1)}), bf16[4,128,256]{2,1,0:T(8,128)(2,1)}, u32[]{:S(2)}, u32[]{:S(2)}) async-start(bf16[4,128,256]{2,1,0:T(8,128)(2,1)} %bitcast.218), calls=%async_computation.6 | async-start | bytes 524288 | tf_op jit(solution)/shard_map/all_to_all | solution.py:190
  1093.7 12.2 %all-to-all-start.1 = ((bf16[4,128,256]{2,1,0:T(8,128)(2,1)}), bf16[4,128,256]{2,1,0:T(8,128)(2,1)S(1)}, u32[]{:S(2)}, u32[]{:S(2)}) async-start(bf16[4,128,256]{2,1,0:T(8,128)(2,1)} %bitcast.220), calls=%async_computation.8 | async-start | bytes 524288 | tf_op jit(solution)/shard_map/all_to_all | solution.py:190
  1181.2 17.0 %copy-start.8 = (f32[256,2048]{1,0:T(8,128)S(1)}, f32[256,2048]{1,0:T(8,128)}, u32[]{:S(2)}) copy-start(f32[256,2048]{1,0:T(8,128)} %all-gather.18.cloned.1.call-done) | copy-start | bytes 6291460
  (23 other events, 116.7 us)
Sparse Core Ops, SparseCore 0:
  11.4 46.7 all-gather.7
  78.7 46.4 reduce-scatter.18
  129.1 47.6 all-gather.9
  178.9 45.8 all-gather.13
  338.8 46.3 reduce-scatter.22
  389.1 47.5 all-gather.15
  440.3 42.0 reduce-scatter.36
  486.0 41.7 reduce-scatter.40
  530.1 54.3 reduce-scatter.24
  586.6 67.4 reduce-scatter.20
  657.8 43.1 reduce-scatter.38
  703.7 27.6 reduce-scatter.34
  735.2 27.6 reduce-scatter.32
  765.8 41.7 reduce-scatter.52
  810.5 41.7 reduce-scatter.50
  855.2 41.7 reduce-scatter.44
  899.8 41.7 reduce-scatter.42
  944.9 27.6 reduce-scatter.28
  976.0 41.7 reduce-scatter.48
  1021.0 41.7 reduce-scatter.46
  1065.9 27.6 reduce-scatter.30
  1095.9 71.2 reduce-scatter.26
  1169.4 11.7 all-gather.17
  1183.3 11.7 all-gather.11

commit v2 on v1

v2 whole, which is shorter than its diff:
```python
import functools

import jax
import jax.numpy as jnp
from jax import lax
from jax.experimental import pallas as pl
from jax.experimental.pallas import tpu as pltpu
from jax.sharding import PartitionSpec as P

HD = 128
MESH = pl.DeviceIdType.MESH
PIECES = 2
STRIP = 16
epsilon = 1e-06
f32 = jnp.float32
bf16 = jnp.bfloat16
UP, DOWN = 0, 1


def here():
    return lax.axis_index("expert"), lax.axis_index("tensor")


def greet(nz):
    z, c = here()
    barrier = pltpu.get_barrier_semaphore()

    def tell(device):
        pl.semaphore_signal(barrier, inc=1, device_id=device, device_id_type=MESH)

    tell({"tensor": 1 - c})
    for d in range(1, nz):
        tell({"expert": lax.rem(z + d, nz)})
    pl.semaphore_wait(barrier, nz)


def remote(src, dst, send, recv, device):
    return pltpu.make_async_remote_copy(
        src_ref=src, dst_ref=dst, send_sem=send, recv_sem=recv, device_id=device, device_id_type=MESH
    )


def strips(rows, step):
    def one(i, carry):
        step(pl.ds(pl.multiple_of(i * STRIP, STRIP), STRIP))
        return carry

    lax.fori_loop(0, rows // STRIP, one, 0)


GATHER_SEMS = 4


def gather_sems(nz):
    return [pltpu.SemaphoreType.DMA((2, nz, PIECES))] * GATHER_SEMS + [pltpu.SemaphoreType.DMA]


def gather_rows(nz, own_ref, out_ref, z_send, z_recv, s_send, s_recv, local_sem):
    z, c = here()
    rows = own_ref.shape[0]
    piece = rows // PIECES

    def origin(way, d):
        return z - d if way == UP else z + d

    def inside(way, d):
        return z >= d if way == UP else z + d < nz

    def onward(way):
        return z < nz - 1 if way == UP else z > 0

    def place(block, core, p):
        return out_ref.at[pl.ds(pl.multiple_of((block * 2 + core) * rows + p * piece, piece), piece)]

    def source(way, d, p):
        return own_ref.at[pl.ds(p * piece, piece)] if d == 0 else place(origin(way, d), c, p)

    def along(way, d, p):
        device = {"expert": z + 1 if way == UP else z - 1}
        return remote(
            source(way, d, p), place(origin(way, d), c, p), z_send.at[way, d, p], z_recv.at[way, d, p], device
        )

    def across(way, d, p):
        return remote(
            source(way, d, p), place(origin(way, d), c, p), s_send.at[way, d, p], s_recv.at[way, d, p],
            {"tensor": 1 - c},
        )

    def arrived(way, d, p):
        dst = place(origin(way, d), c, p)
        remote(dst, dst, z_send.at[way, d - 1, p], z_recv.at[way, d - 1, p], {"tensor": 1 - c}).wait_recv()

    def crossed(way, d, p):
        dst = place(origin(way, d), 1 - c, p)
        remote(dst, dst, s_send.at[way, d, p], s_recv.at[way, d, p], {"tensor": 1 - c}).wait_recv()

    mine = pltpu.make_async_copy(
        own_ref, out_ref.at[pl.ds(pl.multiple_of((z * 2 + c) * rows, rows), rows)], local_sem
    )
    for p in range(PIECES):
        for way in (UP, DOWN):
            pl.when(onward(way))(lambda way=way, p=p: along(way, 0, p).start())
        across(UP, 0, p).start()
    mine.start()
    for d in range(1, nz):
        for p in range(PIECES):
            for way in (UP, DOWN):

                @pl.when(inside(way, d))
                def _(way=way, d=d, p=p):
                    arrived(way, d, p)
                    pl.when(onward(way))(lambda: along(way, d, p).start())
                    across(way, d, p).start()

    for p in range(PIECES):
        crossed(UP, 0, p)
        across(UP, 0, p).wait_send()
        for way in (UP, DOWN):
            pl.when(onward(way))(lambda way=way, p=p: along(way, 0, p).wait_send())
            for d in range(1, nz):

                @pl.when(inside(way, d))
                def _(way=way, d=d, p=p):
                    crossed(way, d, p)
                    across(way, d, p).wait_send()
                    pl.when(onward(way))(lambda: along(way, d, p).wait_send())

    mine.wait()


REDUCE_SCRATCH = 8


def reduce_scratch(nz, rows, width):
    return [
        pltpu.VMEM((2, nz, rows, width), bf16),
        pltpu.VMEM((2, nz, rows, width), bf16),
        pltpu.VMEM((2, nz, rows, width), bf16),
        pltpu.VMEM((rows, width), f32),
        pltpu.SemaphoreType.DMA((2, nz, PIECES)),
        pltpu.SemaphoreType.DMA((2, nz, PIECES)),
        pltpu.SemaphoreType.DMA((2, nz, PIECES)),
        pltpu.SemaphoreType.DMA((2, nz, PIECES)),
    ]


def reduce_rows(nz, part_ref, side, inbox, outbox, total, s_send, s_recv, z_send, z_recv):
    z, c = here()
    rows = total.shape[0]
    piece = rows // PIECES

    def target(way, d):
        return z + d if way == UP else z - d

    def inside(way, d):
        return z + d < nz if way == UP else z >= d

    def behind(way):
        return z > 0 if way == UP else z < nz - 1

    def cut(p):
        return pl.ds(p * piece, piece)

    def across(way, d, p):
        src = part_ref.at[pl.ds(pl.multiple_of((target(way, d) * 2 + 1 - c) * rows + p * piece, piece), piece)]
        return remote(
            src, side.at[way, d, cut(p)], s_send.at[way, d, p], s_recv.at[way, d, p], {"tensor": 1 - c}
        )

    def along(way, d, p):
        device = {"expert": z + 1 if way == UP else z - 1}
        return remote(
            outbox.at[way, d, cut(p)], inbox.at[way, d - 1, cut(p)], z_send.at[way, d, p], z_recv.at[way, d - 1, p],
            device,
        )

    def arrived(way, d, p):
        dst = inbox.at[way, d, cut(p)]
        remote(dst, dst, z_send.at[way, d, p], z_recv.at[way, d, p], {"tensor": 1 - c}).wait_recv()

    def mine(way, d, p, strip):
        base = (target(way, d) * 2 + c) * rows + p * piece
        own = part_ref[pl.ds(pl.multiple_of(base + strip.start, STRIP), STRIP), :].astype(f32)
        return own + side[way, d, pl.ds(pl.multiple_of(p * piece + strip.start, STRIP), STRIP), :].astype(f32)

    for d in range(nz - 1, 0, -1):
        for p in range(PIECES):
            for way in (UP, DOWN):
                pl.when(inside(way, d))(lambda way=way, d=d, p=p: across(way, d, p).start())
    for p in range(PIECES):
        across(UP, 0, p).start()

    for d in range(nz - 1, 0, -1):
        for p in range(PIECES):
            for way in (UP, DOWN):

                @pl.when(inside(way, d))
                def _(way=way, d=d, p=p):
                    across(way, d, p).wait_recv()

                    @pl.when(behind(way))
                    def _():
                        arrived(way, d, p)

                        def add(strip):
                            at = pl.ds(pl.multiple_of(p * piece + strip.start, STRIP), STRIP)
                            value = mine(way, d, p, strip) + inbox[way, d, at, :].astype(f32)
                            outbox[way, d, at, :] = value.astype(bf16)

                        strips(piece, add)

                    @pl.when(jnp.logical_not(behind(way)))
                    def _():
                        def add(strip):
                            at = pl.ds(pl.multiple_of(p * piece + strip.start, STRIP), STRIP)
                            outbox[way, d, at, :] = mine(way, d, p, strip).astype(bf16)

                        strips(piece, add)

                    along(way, d, p).start()

    for p in range(PIECES):
        across(UP, 0, p).wait_recv()

        def first(strip, p=p):
            at = pl.ds(pl.multiple_of(p * piece + strip.start, STRIP), STRIP)
            total[at, :] = mine(UP, 0, p, strip)

        strips(piece, first)
        for way in (UP, DOWN):

            @pl.when(behind(way))
            def _(way=way, p=p):
                arrived(way, 0, p)

                def add(strip):
                    at = pl.ds(pl.multiple_of(p * piece + strip.start, STRIP), STRIP)
                    total[at, :] += inbox[way, 0, at, :].astype(f32)

                strips(piece, add)

    for p in range(PIECES):
        across(UP, 0, p).wait_send()
        for way in (UP, DOWN):
            for d in range(1, nz):

                @pl.when(inside(way, d))
                def _(way=way, d=d, p=p):
                    across(way, d, p).wait_send()
                    along(way, d, p).wait_send()


COST = pl.CostEstimate(flops=2 * 10**10, bytes_accessed=10**8, transcendentals=0)


def params(name, **more):
    return pltpu.CompilerParams(
        collective_id=name, has_side_effects=True, vmem_limit_bytes=56 * 1024 * 1024, **more
    )


VMEM = pl.BlockSpec(memory_space=pltpu.VMEM)
ANY = pl.BlockSpec(memory_space=pl.ANY)


def norm_rows(values, gain):
    inverse = lax.rsqrt(jnp.mean(values * values, axis=-1, keepdims=True) + epsilon)
    return values * inverse * gain, inverse


def norm_back(values, gain, upstream):
    inverse = lax.rsqrt(jnp.mean(values * values, axis=-1, keepdims=True) + epsilon)
    scaled = upstream * gain
    inner = jnp.mean(scaled * values, axis=-1, keepdims=True)
    change = inverse * scaled - values * inverse * inverse * inverse * inner
    return change, upstream * values * inverse


def first_gather(nz, x, gain, marks, name):
    rows, width = x.shape

    def kernel(x_ref, gain_ref, marks_ref, out_ref, all_ref, own, m_send, m_recv, m_local, *sems):
        z, c = here()
        greet(nz)
        keep = pltpu.make_async_copy(marks_ref, all_ref.at[z], m_local)
        keep.start()

        def send(way, d):
            to = z + d if way == UP else z - d
            return remote(marks_ref, all_ref.at[z], m_send.at[way, d], m_recv.at[way, d], {"expert": to})

        def take(way, d):
            dst = all_ref.at[z - d if way == UP else z + d]
            remote(dst, dst, m_send.at[way, d], m_recv.at[way, d], {"tensor": 1 - c}).wait_recv()

        for d in range(1, nz):
            for way in (UP, DOWN):
                pl.when(z + d < nz if way == UP else z >= d)(lambda way=way, d=d: send(way, d).start())

        def step(at):
            normed, _ = norm_rows(x_ref[at, :].astype(f32), gain_ref[...])
            own[at, :] = normed.astype(bf16)

        strips(rows, step)
        gather_rows(nz, own, out_ref, *sems)
        keep.wait()
        for d in range(1, nz):
            for way in (UP, DOWN):
                pl.when(z + d < nz if way == UP else z >= d)(lambda way=way, d=d: send(way, d).wait_send())
                pl.when(z >= d if way == UP else z + d < nz)(lambda way=way, d=d: take(way, d))

    return pl.pallas_call(
        kernel,
        out_shape=[
            jax.ShapeDtypeStruct((nz * 2 * rows, width), bf16),
            jax.ShapeDtypeStruct((nz,) + marks.shape, jnp.int32),
        ],
        in_specs=[VMEM, VMEM, VMEM],
        out_specs=[ANY, ANY],
        scratch_shapes=[
            pltpu.VMEM((rows, width), bf16),
            pltpu.SemaphoreType.DMA((2, nz)),
            pltpu.SemaphoreType.DMA((2, nz)),
            pltpu.SemaphoreType.DMA,
        ]
        + gather_sems(nz),
        compiler_params=params(name),
    )(x, gain, marks)


def project_and_gather(nz, o, weight, x, gain, name):
    rows, width = x.shape
    full = 2 * rows
    cols = o.shape[1]

    def kernel(o_ref, w_ref, x_ref, gain_ref, n2_ref, h_ref, inv_ref, heads, acc, give, take, own, inv_own, a_send,
               a_recv, e_send, e_recv, i_sems, *sems):
        z, c = here()
        greet(nz)

        def inside(way, d):
            return z + d < nz if way == UP else z >= d

        def send(way, d):
            to = z + d if way == UP else z - d
            src = o_ref.at[pl.ds(pl.multiple_of(to * full, full), full)]
            return remote(src, heads.at[way, d], a_send.at[way, d], a_recv.at[way, d], {"expert": to})

        for d in range(nz - 1, 0, -1):
            for way in (UP, DOWN):
                pl.when(inside(way, d))(lambda way=way, d=d: send(way, d).start())

        tile = 512 if width % 512 == 0 else width

        def project(block, left, fresh):
            at = pl.ds(pl.multiple_of(block * cols, cols), cols)

            def one(i, carry):
                to = pl.ds(pl.multiple_of(i * tile, tile), tile)
                value = lax.dot_general(
                    left(), w_ref[to, at], (((1,), (1,)), ((), ())), preferred_element_type=f32
                )
                acc[:, to] = value if fresh else acc[:, to] + value
                return carry

            lax.fori_loop(0, width // tile, one, 0)

        project(z, lambda: o_ref[pl.ds(pl.multiple_of(z * full, full), full), :], True)
        for d in range(1, nz):
            for way in (UP, DOWN):
                @pl.when(z >= d if way == UP else z + d < nz)
                def _(way=way, d=d):
                    remote(
                        heads.at[way, d], heads.at[way, d], a_send.at[way, d], a_recv.at[way, d], {"tensor": 1 - c}
                    ).wait_recv()
                    project(z - d if way == UP else z + d, lambda: heads[way, d], False)

        def pack(at):
            give[at, :] = acc[pl.ds(pl.multiple_of((1 - c) * rows + at.start, STRIP), STRIP), :].astype(bf16)

        strips(rows, pack)
        swap = remote(give, take, e_send, e_recv, {"tensor": 1 - c})
        swap.start()
        swap.wait_recv()

        def norm(at):
            mixed = acc[pl.ds(pl.multiple_of(c * rows + at.start, STRIP), STRIP), :] + take[at, :].astype(f32)
            h = x_ref[at, :].astype(f32) + mixed
            normed, inverse = norm_rows(h, gain_ref[...])
            h_ref[at, :] = h
            own[at, :] = normed.astype(bf16)
            inv_own[at, :] = jnp.broadcast_to(inverse, (STRIP, 128))

        strips(rows, norm)
        spot = inv_ref.at[pl.ds(pl.multiple_of(c * rows, rows), rows)]
        keep = pltpu.make_async_copy(inv_own, spot, i_sems.at[0])
        pass_on = remote(inv_own, spot, i_sems.at[1], i_sems.at[2], {"tensor": 1 - c})
        keep.start()
        pass_on.start()
        gather_rows(nz, own, n2_ref, *sems)
        keep.wait()
        pass_on.wait()
        swap.wait_send()
        for d in range(1, nz):
            for way in (UP, DOWN):
                pl.when(inside(way, d))(lambda way=way, d=d: send(way, d).wait_send())

    return pl.pallas_call(
        kernel,
        out_shape=[
            jax.ShapeDtypeStruct((nz * full, width), bf16),
            jax.ShapeDtypeStruct((rows, width), f32),
            jax.ShapeDtypeStruct((full, 128), f32),
        ],
        in_specs=[VMEM] * 4,
        out_specs=[ANY, VMEM, ANY],
        scratch_shapes=[
            pltpu.VMEM((2, nz, full, cols), bf16),
            pltpu.VMEM((full, width), f32),
            pltpu.VMEM((rows, width), bf16),
            pltpu.VMEM((rows, width), bf16),
            pltpu.VMEM((rows, width), bf16),
            pltpu.VMEM((rows, 128), f32),
            pltpu.SemaphoreType.DMA((2, nz)),
            pltpu.SemaphoreType.DMA((2, nz)),
            pltpu.SemaphoreType.DMA,
            pltpu.SemaphoreType.DMA,
            pltpu.SemaphoreType.DMA((3,)),
        ]
        + gather_sems(nz),
        compiler_params=params(name),
    )(o, weight, x, gain)


def reduce_and_gather(nz, part, h, gain, upstream, name):
    rows, width = h.shape

    def kernel(part_ref, h_ref, gain_ref, up_ref, out_ref, dh_ref, gg_ref, own, *rest):
        scratch, sems = rest[:REDUCE_SCRATCH], rest[REDUCE_SCRATCH:]
        total = scratch[3]
        greet(nz)
        reduce_rows(nz, part_ref, *scratch)
        gg_ref[...] = jnp.zeros_like(gg_ref)

        def step(at):
            change, along = norm_back(h_ref[at, :], gain_ref[...], total[at, :])
            dh = up_ref[at, :].astype(f32) + change
            dh_ref[at, :] = dh
            own[at, :] = dh.astype(bf16)
            gg_ref[...] += along

        strips(rows, step)
        gather_rows(nz, own, out_ref, *sems)

    return pl.pallas_call(
        kernel,
        out_shape=[
            jax.ShapeDtypeStruct((nz * 2 * rows, width), bf16),
            jax.ShapeDtypeStruct((rows, width), f32),
            jax.ShapeDtypeStruct((STRIP, width), f32),
        ],
        in_specs=[VMEM] * 4,
        out_specs=[ANY, VMEM, VMEM],
        scratch_shapes=[pltpu.VMEM((rows, width), bf16)] + reduce_scratch(nz, rows, width) + gather_sems(nz),
        compiler_params=params(name),
    )(part, h, gain, upstream)


def swap_rows(nz, own, out_ref, sems):
    z, c = here()
    rows = own.shape[0]
    spot = out_ref.at[pl.ds(pl.multiple_of(c * rows, rows), rows)]
    keep = pltpu.make_async_copy(own, spot, sems.at[0])
    pass_on = remote(own, spot, sems.at[1], sems.at[2], {"tensor": 1 - c})
    keep.start()
    pass_on.start()
    keep.wait()
    pass_on.wait()


def reduce_input(nz, part, x, gain, dh, name):
    rows, width = x.shape

    def kernel(part_ref, x_ref, gain_ref, dh_ref, out_ref, gg_ref, own, sems, *scratch):
        total = scratch[3]
        greet(nz)
        reduce_rows(nz, part_ref, *scratch)
        gg_ref[...] = jnp.zeros_like(gg_ref)

        def step(at):
            change, along = norm_back(x_ref[at, :].astype(f32), gain_ref[...], total[at, :])
            own[at, :] = dh_ref[at, :] + change
            gg_ref[...] += along

        strips(rows, step)
        swap_rows(nz, own, out_ref, sems)

    return pl.pallas_call(
        kernel,
        out_shape=[
            jax.ShapeDtypeStruct((2 * rows, width), f32),
            jax.ShapeDtypeStruct((STRIP, width), f32),
        ],
        in_specs=[VMEM] * 4,
        out_specs=[ANY, VMEM],
        scratch_shapes=[pltpu.VMEM((rows, width), f32), pltpu.SemaphoreType.DMA((3,))] + reduce_scratch(nz, rows, width),
        compiler_params=params(name),
    )(part, x, gain, dh)


def reduce_output(nz, part, h, name):
    rows, width = h.shape

    def kernel(part_ref, h_ref, out_ref, own, sems, *scratch):
        total = scratch[3]
        greet(nz)
        reduce_rows(nz, part_ref, *scratch)

        def step(at):
            own[at, :] = h_ref[at, :] + total[at, :]

        strips(rows, step)
        swap_rows(nz, own, out_ref, sems)

    return pl.pallas_call(
        kernel,
        out_shape=jax.ShapeDtypeStruct((2 * rows, width), f32),
        in_specs=[VMEM] * 2,
        out_specs=ANY,
        scratch_shapes=[pltpu.VMEM((rows, width), f32), pltpu.SemaphoreType.DMA((3,))] + reduce_scratch(nz, rows, width),
        compiler_params=params(name),
    )(part, h)


def spread(nz, parts, splits, name):
    block = parts[0].shape[0] // nz
    count = len(parts)
    outs = [(i, s) for i in range(count) for s in range(splits[i])]

    def kernel(*refs):
        ins, outs_refs, rest = refs[:count], refs[count : count + len(outs)], refs[count + len(outs) :]
        boxes, send_sem, recv_sem = rest[:count], rest[count], rest[count + 1]
        z, c = here()
        greet(nz)

        def cut(i, to):
            return ins[i].at[pl.ds(pl.multiple_of(to * block, block), block)]

        def send(i, way, d):
            to = z + d if way == UP else z - d
            return remote(cut(i, to), boxes[i].at[z], send_sem.at[i, way, d], recv_sem.at[i, way, d], {"expert": to})

        def take(i, way, d):
            dst = boxes[i].at[z - d if way == UP else z + d]
            remote(dst, dst, send_sem.at[i, way, d], recv_sem.at[i, way, d], {"tensor": 1 - c}).wait_recv()

        for i in range(count):
            for d in range(nz - 1, 0, -1):
                for way in (UP, DOWN):
                    pl.when(z + d < nz if way == UP else z >= d)(lambda i=i, way=way, d=d: send(i, way, d).start())
        for i in range(count):
            boxes[i][z] = ins[i][pl.ds(pl.multiple_of(z * block, block), block), :]
        for i in range(count):
            for d in range(1, nz):
                for way in (UP, DOWN):
                    pl.when(z + d < nz if way == UP else z >= d)(lambda i=i, way=way, d=d: send(i, way, d).wait_send())
                    pl.when(z >= d if way == UP else z + d < nz)(lambda i=i, way=way, d=d: take(i, way, d))
            for j, (k, s) in enumerate(outs):
                if k == i:
                    cols = ins[i].shape[1] // splits[i]
                    for b in range(nz):
                        outs_refs[j][:, b * cols : (b + 1) * cols] = boxes[i][b, :, s * cols : (s + 1) * cols].astype(f32)

    return pl.pallas_call(
        kernel,
        out_shape=[
            jax.ShapeDtypeStruct((block, nz * parts[i].shape[1] // splits[i]), f32) for i, _ in outs
        ],
        in_specs=[VMEM] * count,
        out_specs=[VMEM] * len(outs),
        scratch_shapes=[pltpu.VMEM((nz, block, p.shape[1]), bf16) for p in parts]
        + [pltpu.SemaphoreType.DMA((count, 2, nz)), pltpu.SemaphoreType.DMA((count, 2, nz))],
        compiler_params=params(name),
    )(*parts)


TILE = 256
TALL = 512
LANES = 128


def nt_dot(left, right):
    return lax.dot_general(left, right, (((1,), (1,)), ((), ())), preferred_element_type=f32)


def nn_dot(left, right):
    return jnp.dot(left, right, preferred_element_type=f32)


def tiles(count, step, size=TILE):
    def one(i, carry):
        step(i, pl.ds(pl.multiple_of(i * size, size), size))
        return carry

    lax.fori_loop(0, count, one, 0)


def padded(columns):
    return -(-columns // LANES) * LANES


def window(columns, place):
    first = place * columns // LANES * LANES
    return first, place * columns - first


def window_width(columns, places):
    return max(padded(window(columns, i)[1] + columns) for i in range(places))


def hidden_layer(nz, n2, dy, gate, weights, index, groups):
    seq, width = n2.shape
    shared = index is None
    ffn = weights[0].shape[1] // nz if shared else weights[0].shape[1]
    held = window_width(ffn, nz) if shared else ffn
    kept = held if shared else padded(ffn)
    block = width // groups
    lane = min(block, TILE)
    per = TILE // lane
    count, slabs = seq // TILE, width // TILE
    strip = 32
    product = nn_dot if shared else nt_dot
    w_shape = (width, held) if shared else (held, width)

    def kernel(n2_hbm, dy_hbm, wg_hbm, wu_hbm, wd_hbm, gate_ref, grad_hbm, da_hbm, db_hbm, gu_hbm, dgate_ref,
               n2_ref, dy_ref, wg, wu, wd, a, b, back, da, db, gu, turned, slab, in_sem, out_sem, slab_sem):
        z = lax.axis_index("expert")
        first = pl.multiple_of(z * ffn // LANES * LANES, LANES)
        skip = z * ffn - first

        def pick(ref):
            return ref.at[:, pl.ds(first, held)] if shared else ref.at[index]

        loads = [
            pltpu.make_async_copy(src, dst, in_sem.at[i])
            for i, (src, dst) in enumerate(
                ((pick(wg_hbm), wg), (n2_hbm, n2_ref), (pick(wu_hbm), wu), (pick(wd_hbm), wd), (dy_hbm, dy_ref))
            )
        ]
        for load in loads:
            load.start()
        if kept > held:
            for ref in (da, db, gu):
                ref[:, held:] = jnp.zeros((seq, kept - held), bf16)
        loads[0].wait()
        loads[1].wait()

        def one(i, at):
            a[at, :] = product(n2_ref[at, :], wg[...])

        tiles(seq // TALL, one, TALL)
        loads[2].wait()

        def two(i, at):
            b[at, :] = product(n2_ref[at, :], wu[...])

        tiles(seq // TALL, two, TALL)
        loads[3].wait()
        loads[4].wait()

        def three(i, at):
            back[...] = product(dy_ref[at, :], wd[...])

            def point(j, carry):
                row = pl.ds(pl.multiple_of(i * TILE + j * strip, strip), strip)
                local = pl.ds(pl.multiple_of(j * strip, strip), strip)
                av, bv, kv, gv = a[row, :], b[row, :], back[local, :], gate_ref[row, :]
                sig = 1.0 / (1.0 + jnp.exp(-av))
                act = av * sig
                u = act * bv
                if shared:
                    column = lax.broadcasted_iota(jnp.int32, (strip, held), 1)
                    mine = jnp.logical_and(column >= skip, column < skip + ffn)
                    u, kv = jnp.where(mine, u, 0.0), jnp.where(mine, kv, 0.0)
                dgate_ref[row, :] = jnp.sum(u * kv, axis=-1, keepdims=True)
                gu[row, :held] = (gv * u).astype(bf16)
                du = gv * kv
                da[row, :held] = (du * bv * (sig + act * (1.0 - sig))).astype(bf16)
                db[row, :held] = (du * act).astype(bf16)
                return carry

            lax.fori_loop(0, TILE // strip, point, 0)
            for k, ref in enumerate((da, db, gu)):
                turned[k, :, at] = ref[at, :held].T

        tiles(count, three)
        saves = [
            pltpu.make_async_copy(src, dst, out_sem.at[i])
            for i, (src, dst) in enumerate(((da, da_hbm), (db, db_hbm), (gu, gu_hbm)))
        ]
        for save in saves:
            save.start()

        def leave(i):
            slot = lax.rem(i, 2)
            if per > 1:
                dst = grad_hbm.at[pl.ds(i * per, per)]
            else:
                many = block // TILE
                dst = grad_hbm.at[pl.ds(i // many, 1), :, pl.ds(pl.multiple_of(lax.rem(i, many) * TILE, TILE), TILE)]
            return pltpu.make_async_copy(slab.at[slot], dst, slab_sem.at[slot])

        def four(i, at):
            slot = lax.rem(i, 2)
            pl.when(i >= 2)(lambda: leave(i).wait())
            for k, right in enumerate((n2_ref, n2_ref, dy_ref)):
                value = nn_dot(turned[k], right[:, at]).astype(bf16)
                for j in range(per):
                    slab[slot, j, k * held : (k + 1) * held, :] = value[:, j * lane : (j + 1) * lane]
            leave(i).start()

        tiles(slabs, four)
        leave(slabs - 2).wait()
        leave(slabs - 1).wait()
        for save in saves:
            save.wait()

    hidden = jax.ShapeDtypeStruct((seq, kept), bf16)
    return pl.pallas_call(
        kernel,
        out_shape=[
            jax.ShapeDtypeStruct((groups, 3 * held, block), bf16), hidden, hidden, hidden,
            jax.ShapeDtypeStruct((seq, 1), f32),
        ],
        in_specs=[ANY] * 5 + [VMEM],
        out_specs=[ANY] * 4 + [VMEM],
        scratch_shapes=[
            pltpu.VMEM((seq, width), bf16), pltpu.VMEM((seq, width), bf16),
            pltpu.VMEM(w_shape, bf16), pltpu.VMEM(w_shape, bf16), pltpu.VMEM(w_shape, bf16),
            pltpu.VMEM((seq, held), f32), pltpu.VMEM((seq, held), f32), pltpu.VMEM((TILE, held), f32),
            pltpu.VMEM((seq, kept), bf16), pltpu.VMEM((seq, kept), bf16), pltpu.VMEM((seq, kept), bf16),
            pltpu.VMEM((3, held, seq), bf16),
            pltpu.VMEM((2, per, 3 * held, lane), bf16),
            pltpu.SemaphoreType.DMA((5,)), pltpu.SemaphoreType.DMA((3,)), pltpu.SemaphoreType.DMA((2,)),
        ],
        compiler_params=pltpu.CompilerParams(vmem_limit_bytes=58 * 1024 * 1024),
    )(n2, dy, *weights, gate)


def sum_products(nz, experts, shared, extra):
    seq, kept = experts[0][0].shape
    _, ffn, width = experts[0][1][0].shape
    held = shared[0][0].shape[1]
    own = shared[0][1].shape[1] // nz
    ne, ns = len(experts), len(shared)
    step = 512
    more = [] if extra is None else list(extra)

    def kernel(*refs):
        e_left, e_right = refs[:ne], refs[ne : 2 * ne]
        s_left, s_right = refs[2 * ne : 2 * ne + ns], refs[2 * ne + ns : 2 * (ne + ns)]
        base = 2 * (ne + ns)
        small = refs[base : base + len(more)]
        out_hbm, left, right, sleft, sright, out, l_sem, r_sem, o_sem = refs[base + len(more) :]
        first = pl.multiple_of(lax.axis_index("expert") * own // LANES * LANES, LANES)

        def lefts():
            for i in range(ne):
                yield pltpu.make_async_copy(e_left[i], left.at[:, pl.ds(i * kept, kept)], l_sem.at[i])
            for i in range(ns):
                yield pltpu.make_async_copy(s_left[i], sleft.at[:, pl.ds(i * held, held)], l_sem.at[ne + i])

        def rights(j):
            to = pl.ds(j * step, step)
            for i in range(ne):
                src = e_right[i].at[experts[i][1][1], :, to]
                yield pltpu.make_async_copy(src, right.at[j % 2, pl.ds(i * kept, ffn)], r_sem.at[j % 2, i])
            for i in range(ns):
                src = s_right[i].at[to, pl.ds(first, held)]
                yield pltpu.make_async_copy(src, sright.at[j % 2, :, pl.ds(i * held, held)], r_sem.at[j % 2, ne + i])

        for copy in (*rights(0), *lefts()):
            copy.start()
        if kept > ffn:
            for j in range(2):
                for i in range(ne):
                    right[j, i * kept + ffn : (i + 1) * kept, :] = jnp.zeros((kept - ffn, step), bf16)
        for j in range(width // step):
            for copy in rights(j):
                copy.wait()
            if j == 0:
                for copy in lefts():
                    copy.wait()
            if (j + 1) * step < width:
                for copy in rights(j + 1):
                    copy.start()

            def one(m, at, j=j):
                value = nn_dot(left[at, :], right[j % 2]) + nt_dot(sleft[at, :], sright[j % 2])
                if more:
                    value += nt_dot(small[0][at, :], small[1][j * step : (j + 1) * step, :])
                out[at, j * step : (j + 1) * step] = value.astype(bf16)

            tiles(seq // TALL, one, TALL)
            to = pl.ds(j * step, step)
            pltpu.make_async_copy(out.at[:, to], out_hbm.at[:, to], o_sem).start()
        pltpu.make_async_copy(out, out_hbm, o_sem).wait()

    return pl.pallas_call(
        kernel,
        out_shape=jax.ShapeDtypeStruct((seq, width), bf16),
        in_specs=[ANY] * (2 * (ne + ns)) + [VMEM] * len(more),
        out_specs=ANY,
        scratch_shapes=[
            pltpu.VMEM((seq, ne * kept), bf16), pltpu.VMEM((2, ne * kept, step), bf16),
            pltpu.VMEM((seq, ns * held), bf16), pltpu.VMEM((2, step, ns * held), bf16),
            pltpu.VMEM((seq, width), bf16),
            pltpu.SemaphoreType.DMA((ne + ns,)), pltpu.SemaphoreType.DMA((2, ne + ns)), pltpu.SemaphoreType.DMA,
        ],
        compiler_params=pltpu.CompilerParams(vmem_limit_bytes=58 * 1024 * 1024),
    )(
        *[left for left, _ in experts], *[right[0] for _, right in experts],
        *[left for left, _ in shared], *[right for _, right in shared], *more,
    )


def spread_turned(nz, part, columns, places, name):
    _, held, block = part.shape
    count = 3
    held //= count

    def kernel(in_ref, *rest):
        outs, box, send_sem, recv_sem = rest[:count], rest[count], rest[count + 1], rest[count + 2]
        z, c = here()
        greet(nz)

        def send(way, d):
            to = z + d if way == UP else z - d
            return remote(in_ref.at[to], box.at[z], send_sem.at[way, d], recv_sem.at[way, d], {"expert": to})

        def take(way, d):
            dst = box.at[z - d if way == UP else z + d]
            remote(dst, dst, send_sem.at[way, d], recv_sem.at[way, d], {"tensor": 1 - c}).wait_recv()

        for d in range(nz - 1, 0, -1):
            for way in (UP, DOWN):
                pl.when(z + d < nz if way == UP else z >= d)(lambda way=way, d=d: send(way, d).start())
        box[z] = in_ref[z]
        for d in range(1, nz):
            for way in (UP, DOWN):
                pl.when(z + d < nz if way == UP else z >= d)(lambda way=way, d=d: send(way, d).wait_send())
                pl.when(z >= d if way == UP else z + d < nz)(lambda way=way, d=d: take(way, d))
        for k in range(count):
            end = 0
            for b in range(nz):
                first, _ = window(columns, b)
                value = box[b, k * held : (k + 1) * held, :].astype(f32).T
                shared = max(end - first, 0)
                if shared:
                    outs[k][:, first:end] += value[:, :shared]
                last = min(first + held, nz * columns)
                outs[k][:, first + shared : last] = value[:, shared : last - first]
                end = last

    return pl.pallas_call(
        kernel,
        out_shape=[jax.ShapeDtypeStruct((block, nz * columns), f32)] * count,
        in_specs=[VMEM],
        out_specs=[VMEM] * count,
        scratch_shapes=[
            pltpu.VMEM(part.shape, bf16), pltpu.SemaphoreType.DMA((2, nz)), pltpu.SemaphoreType.DMA((2, nz)),
        ],
        compiler_params=params(name),
    )(part)


def sum_everywhere(nz, ndp, parts, name):
    n, rows, block = parts.shape

    def kernel(in_ref, out_ref, box, total, other, send_sem, recv_sem, swap_sem):
        z, c = here()
        me = lax.axis_index("dp") * nz + z
        barrier = pltpu.get_barrier_semaphore()

        def peer(k):
            at = lax.rem(me + k, n)
            return at, {"dp": at // nz, "expert": lax.rem(at, nz)}

        pl.semaphore_signal(barrier, inc=1, device_id={"tensor": 1 - c}, device_id_type=MESH)
        for k in range(1, n):
            pl.semaphore_signal(barrier, inc=1, device_id=peer(k)[1], device_id_type=MESH)
        pl.semaphore_wait(barrier, n)

        def send(k):
            at, device = peer(k)
            return remote(in_ref.at[at], box.at[k], send_sem.at[k], recv_sem.at[k], device)

        for k in range(1, n):
            send(k).start()
        total[...] = in_ref[me]
        for k in range(1, n):
            send(k).wait_recv()
            total[...] += box[k]
        swap = remote(total, other, swap_sem.at[0], swap_sem.at[1], {"tensor": 1 - c})
        swap.start()
        swap.wait_recv()
        out_ref[...] = total[...] + other[...]
        swap.wait_send()
        for k in range(1, n):
            send(k).wait_send()

    return pl.pallas_call(
        kernel,
        out_shape=jax.ShapeDtypeStruct((rows, block), f32),
        in_specs=[VMEM],
        out_specs=VMEM,
        scratch_shapes=[
            pltpu.VMEM((n, rows, block), f32), pltpu.VMEM((rows, block), f32), pltpu.VMEM((rows, block), f32),
            pltpu.SemaphoreType.DMA((n,)), pltpu.SemaphoreType.DMA((n,)), pltpu.SemaphoreType.DMA((2,)),
        ],
        compiler_params=params(name),
    )(parts)


SEQ_AXES = ("expert", "tensor")


def cross_rows(left, right):
    return lax.dot_general(left, right, (((0,), (0,)), ((), ())), preferred_element_type=f32)


def cross_cols(left, right):
    return lax.dot_general(left, right, (((1,), (1,)), ((), ())), preferred_element_type=f32)


def dot(left, right):
    return jnp.dot(left, right, preferred_element_type=f32)


def two_parts(values):
    high = values.astype(bf16)
    return high, (values - high.astype(f32)).astype(bf16)


def body(
    tokens, segments, routes, norm1_gain, q_weight, k_weight, v_weight, o_weight, norm2_gain,
    router_weight, shared_gate_vector, shared_gate_weight, shared_up_weight, shared_down_weight,
    expert_gate_weight, expert_up_weight, expert_down_weight, out_grad,
):
    nz = lax.axis_size("expert")
    nc = lax.axis_size("tensor")
    z = lax.axis_index("expert")
    c = lax.axis_index("tensor")
    rows, width = tokens.shape
    own_rows = rows // nc
    local_count, _, ffn = expert_gate_weight.shape
    expert_count = local_count * nz
    head_cols = q_weight.shape[1] // nz
    shared_cols = shared_gate_weight.shape[1] // nz
    heads = head_cols // HD
    seq = rows * nz
    scale = HD ** (-0.5)
    gain1 = norm1_gain.astype(f32)[None]
    gain2 = norm2_gain.astype(f32)[None]

    def own(values):
        return lax.dynamic_slice_in_dim(values, c * own_rows, own_rows, 0)

    def head_slice(values):
        return lax.dynamic_slice_in_dim(values, z * head_cols, head_cols, 1)

    x_all_rows = tokens.astype(f32)
    inverse_one_rows = lax.rsqrt(jnp.mean(x_all_rows * x_all_rows, axis=-1) + epsilon)
    x = own(tokens)
    marks = jnp.concatenate([segments, routes.T, jnp.zeros((7 - routes.shape[1], rows), jnp.int32)], axis=0)
    n1, all_marks = first_gather(nz, x, gain1, marks, 0)
    labels = all_marks[:, 0].reshape(seq)
    all_routes = jnp.transpose(all_marks[:, 1 : 1 + routes.shape[1]], (0, 2, 1)).reshape(seq, routes.shape[1])
    upstream = own(out_grad)
    upstream_later, _ = lax.optimization_barrier((upstream, n1))
    dy = lax.all_gather(upstream_later, SEQ_AXES, axis=0, tiled=True)

    wq, wk, wv, wo = head_slice(q_weight), head_slice(k_weight), head_slice(v_weight), head_slice(o_weight)
    q = dot(n1, wq).astype(bf16).reshape(seq, heads, HD)
    k = dot(n1, wk).astype(bf16).reshape(seq, heads, HD)
    v = dot(n1, wv).astype(bf16).reshape(seq, heads, HD)
    pos = jnp.arange(seq)
    allowed = (pos[None, :] <= pos[:, None]) & (labels[None, :] == labels[:, None])

    def masked_scores():
        raw = jnp.einsum("qhd,khd->hqk", q, k, preferred_element_type=f32) * scale
        return jnp.where(allowed[None], raw, -jnp.inf)

    scores = masked_scores()
    top = jnp.max(scores, axis=-1, keepdims=True)
    expd = jnp.exp(scores - top)
    total = jnp.sum(expd, axis=-1, keepdims=True)
    log_total = top + jnp.log(total)
    p_low = (expd / total).astype(bf16)
    o = jnp.einsum("hqk,khd->qhd", p_low, v, preferred_element_type=f32).reshape(seq, head_cols).astype(bf16)
    n2, h, inverse_two = project_and_gather(nz, o, o_weight, x, gain2, 1)

    probs = jax.nn.softmax(dot(n2, router_weight), axis=-1)
    chosen = jnp.any(all_routes[:, :, None] == jnp.arange(expert_count)[None, None, :], axis=1)
    gates = jnp.where(chosen, probs, 0.0)
    sigma = jax.nn.sigmoid(dot(n2, shared_gate_vector))

    turned = [jnp.swapaxes(w, 1, 2) for w in (expert_gate_weight, expert_up_weight, expert_down_weight)]
    shared_weights = (shared_gate_weight, shared_up_weight, shared_down_weight)
    ndp = lax.axis_size("dp")
    grads, d_a, d_b, g_u, d_gate = {}, {}, {}, {}, {}
    n2_now = n2
    for index in (local_count, *range(local_count)):
        if index < local_count:
            gate = lax.dynamic_slice_in_dim(gates, z * local_count + index, 1, 1)
            out = hidden_layer(nz, n2_now, dy, gate, turned, index, ndp)
        else:
            out = hidden_layer(nz, n2_now, dy, sigma[:, None], shared_weights, None, ndp * nz)
        grads[index], d_a[index], d_b[index], g_u[index], d_gate[index] = out
        n2_now, d_gate[index] = lax.optimization_barrier((n2_now, d_gate[index]))

    d_expert = jnp.concatenate([d_gate[i] for i in range(local_count)], axis=1)
    d_probs = lax.dynamic_update_slice_in_dim(jnp.zeros_like(probs), d_expert, z * local_count, 1)
    d_probs = jnp.where(chosen, d_probs, 0.0)
    d_logits = probs * (d_probs - jnp.sum(probs * d_probs, axis=-1, keepdims=True))
    d_vector = d_gate[local_count] * (sigma * (1.0 - sigma))[:, None]
    small = jnp.concatenate([d_logits, d_vector], axis=1)
    small_high, small_low = two_parts(small)
    small_weights = jnp.concatenate([router_weight, shared_gate_vector[:, None]], axis=1)
    fill = ((0, 0), (0, 128 - small.shape[1]))
    experts = range(local_count)
    d_n2 = sum_products(
        nz,
        [(d_a[i], (turned[0], i)) for i in experts] + [(d_b[i], (turned[1], i)) for i in experts],
        [(d_a[local_count], shared_gate_weight), (d_b[local_count], shared_up_weight)],
        (jnp.pad(small_high, fill), jnp.pad(small_weights, fill)),
    )
    small_grad = cross_rows(n2, jnp.concatenate([small_high, small_low], axis=1))
    small_grad = small_grad[:, : expert_count + 1] + small_grad[:, expert_count + 1 :]


    def over_dp(grad):
        rows = grad.reshape(-1, grad.shape[-1])
        return lax.psum_scatter(rows, "dp", scatter_dimension=0, tiled=True)

    shared_grads = grads[local_count]
    shared_part = over_dp(shared_grads).reshape((nz,) + shared_grads.shape[1:])
    expert_parts = [over_dp(grads[i]) for i in experts]
    d_n2_low, shared_part = lax.optimization_barrier((d_n2, shared_part))
    dhr, dh, grad_two = reduce_and_gather(nz, d_n2_low, h, gain2, upstream, 2)
    d_o = dot(dhr, wo).astype(bf16).reshape(seq, heads, HD)
    grad_o = cross_rows(dhr, o)

    pf = jnp.exp(masked_scores() - log_total)
    pb = pf.astype(bf16)
    d_v = jnp.einsum("hqk,qhd->khd", pb, d_o, preferred_element_type=f32)
    dp = jnp.einsum("qhd,khd->hqk", d_o, v, preferred_element_type=f32)
    ds = (pf * (dp - jnp.sum(pf * dp, axis=-1, keepdims=True))).astype(bf16)
    d_q = jnp.einsum("hqk,khd->qhd", ds, k, preferred_element_type=f32) * scale
    d_k = jnp.einsum("hqk,qhd->khd", ds, q, preferred_element_type=f32) * scale
    d_q, d_k, d_v = (t.reshape(seq, head_cols).astype(bf16) for t in (d_q, d_k, d_v))
    grad_attention = jnp.concatenate(
        [cross_rows(n1, jnp.concatenate([d_q, d_k, d_v], axis=1)).astype(bf16), grad_o.astype(bf16)], axis=1
    )
    attention_part = over_dp(grad_attention)
    d_n1 = (cross_cols(d_q, wq) + cross_cols(d_k, wk) + cross_cols(d_v, wv)).astype(bf16)
    d_n1, _, expert_parts[0] = lax.optimization_barrier((d_n1, grad_attention, expert_parts[0]))
    input_grad, grad_one = reduce_input(nz, d_n1, x, gain1, dh, 3)
    branch = sum_products(
        nz,
        [(g_u[i], (turned[2], i)) for i in experts],
        [(g_u[local_count], shared_down_weight)],
        None,
    )
    branch, _ = lax.optimization_barrier((branch, grad_one))
    layer_out = reduce_output(nz, branch, h, 4)
    stats = jnp.stack([inverse_one_rows, inverse_two[:, 0]])

    small_rows = jnp.concatenate(
        [
            jnp.sum(grad_one, axis=0)[None], jnp.sum(grad_two, axis=0)[None], small_grad.T,
            jnp.zeros((13 - expert_count, width), f32),
        ],
        axis=0,
    )
    count = ndp * nz
    small_all = sum_everywhere(nz, ndp, jnp.swapaxes(small_rows.reshape(16, count, width // count), 0, 1), 7)
    g_one, g_two, g_router, g_vector = small_all[0], small_all[1], small_all[2 : 2 + expert_count].T, small_all[2 + expert_count]
    s_gate, s_up, s_down = spread_turned(nz, shared_part, shared_cols, nz, 5)
    (g_q, g_k, g_v, g_o) = spread(nz, [attention_part], (4,), 6)

    def whole(k):
        stack = jnp.stack([t[k * ffn : (k + 1) * ffn] for t in expert_parts]).astype(f32)
        return jnp.swapaxes(stack, 1, 2)

    e_gate, e_up, e_down = whole(0), whole(1), whole(2)
    return (
        layer_out, input_grad, stats, g_one, g_q, g_k, g_v, g_o, g_two, g_router, g_vector,
        s_gate, s_up, s_down, e_gate, e_up, e_down,
    )


def solution(mesh):
    both = ("dp", "expert")
    cols = P(None, "tensor")
    placed = (
        P(both, None), P("dp", "expert"), P(both, None), P(), cols, cols, cols, cols, P(), P(), P(),
        cols, cols, cols, P("expert", None, "tensor"), P("expert", None, "tensor"),
        P("expert", None, "tensor"), P(both, None),
    )
    split = P(both, "tensor")
    experts = P("expert", "dp", "tensor")
    return jax.shard_map(
        body,
        mesh=mesh,
        in_specs=placed,
        out_specs=(
            P(both, None), P(both, None), P(None, both), P(both), split, split, split, split, P(both),
            P(both, None), P(both), split, split, split, experts, experts, experts,
        ),
        check_vma=False,
    )
```

time: 1220 us -> 664 us (0.54)
  waiting for transfers between devices: 764 us -> 0.61 us
  Pallas kernels: 0 us -> 538 us
  matrix products: 286 us -> 47.3 us
  blocking collectives: 49.5 us -> 0 us
  starting transfers between devices: 36.5 us -> 0.2 us
  other arithmetic: 34.3 us -> 20.7 us
    reduce_scatter x18 -> x4, waiting for transfers between devices: 599 us -> 0.05 us  [over_dp(): return lax.psum_scatter(rows, 'dp', scatter_dimension=0, tiled=True)]
    pallas_call x0 -> x13, Pallas kernels: none -> 538 us  [the longest x3 102 us: hidden_layer(): pl.pallas_call(kernel, out_shape=[jax.ShapeDtypeStruct((groups, 3 * held,...]
    all_gather x6 -> x1, waiting for transfers between devices: 155 us -> 0.01 us  [body(): dy = lax.all_gather(upstream_later, SEQ_AXES, axis=0, tiled=True)]
    dot_general x14 -> x3, matrix products: 99.9 us -> 10.1 us  [cross_cols(): lax.dot_general(left, right, (((1,), (1,)), ((), ())), preferred_element_...]
    dot_general x14 -> x3, matrix products: 88 us -> 7.98 us  [cross_rows(): lax.dot_general(left, right, (((0,), (0,)), ((), ())), preferred_element_...]
    dot_general x15 -> x6, matrix products: 85.2 us -> 19.9 us  [dot(): return jnp.dot(left, right, preferred_element_type=f32)]
    all_to_all x6 -> x0, starting transfers between devices: 34.6 us -> none  [over_all(): lax.all_to_all(part, 'expert', split_axis=0, concat_axis=1, tiled=True)]
    all_gather x3 -> x0, blocking collectives: 24.8 us -> none  [the longest x1 14.6 us: body(): all_routes = lax.all_gather(routes, 'expert', axis=0, tiled=True)]
  transfers between devices with their start and end apart: 30 -> 5, of which waited for: 24 -> 0; matrix products, arithmetic and copies ran while one was open for 16% -> 12% of each run, Pallas kernels for 0% -> 66%
where the time goes in v2:
time: 664 us; the launch traced here: 655 us
  Pallas kernels  538 us (81%)
  matrix products  47.3 us (7%)
  local copies, waits for them, and re-layouts  32.9 us (5%)
  other arithmetic  20.7 us (3%)
  between operations  15 us (2%)
    pallas_call x3, Pallas kernels, hidden_layer(): pl.pallas_call(kernel, out_shape=[jax.ShapeDtypeStruct((groups, 3 * held,...  102 us
    pallas_call x1, Pallas kernels, reduce_and_gather(): pl.pallas_call(kernel, out_shape=[jax.ShapeDtypeStruct((nz * 2 * rows, wi...  85.2 us
    pallas_call x1, Pallas kernels, project_and_gather(): pl.pallas_call(kernel, out_shape=[jax.ShapeDtypeStruct((nz * full, width)...  74.7 us
    pallas_call x1, Pallas kernels, spread_turned(): pl.pallas_call(kernel, out_shape=[jax.ShapeDtypeStruct((block, nz * colum...  61 us
    pallas_call x1, Pallas kernels, reduce_input(): pl.pallas_call(kernel, out_shape=[jax.ShapeDtypeStruct((2 * rows, width),...  46.1 us
    pallas_call x2, Pallas kernels, sum_products(): pl.pallas_call(kernel, out_shape=jax.ShapeDtypeStruct((seq, width), bf16)...  45.5 us
    pallas_call x1, Pallas kernels, reduce_output(): pl.pallas_call(kernel, out_shape=jax.ShapeDtypeStruct((2 * rows, width),...  45 us
    pallas_call x1, Pallas kernels, first_gather(): pl.pallas_call(kernel, out_shape=[jax.ShapeDtypeStruct((nz * 2 * rows, wi...  39.3 us
  transfers between devices with their start and end apart: 5, of which 0 were waited for; matrix products, arithmetic and copies ran while one was open for 12% of the time, Pallas kernels for 66%

profile of v2, /device:TPU:8, one launch (start us, length us, event | category | flops | bytes accessed | tf_op | source)
XLA Modules:
  0.0 654.9 jit_solution(10339742950453861327)
XLA Ops:
  7.3 1.3 broadcast_in_dim.75
  8.6 1.4 add_add_fusion.marks_ref
  10.0 2.3 constant_dynamic-slice_fusion.2
  12.2 39.3 %shard_map.305 = (bf16[1024,2048]{1,0:T(8,128)(2,1)}, s32[4,8,256]{2,1,0:T(8,128)}) custom-call(bf16[128,2048]{1,0:T(8,128)(2,1)} %get-tuple-element.125.x_ref, f32[1,2048]{1,0:T(1,128)} %bitcast.130, s32[8,256]{1,0:T(8,128)} %add_add_fusion.marks_ref), custom_call_target="tpu_custom_call" | custom-call | tf_op jit(solution)/shard_map/pallas_call | solution.py:313
  52.4 1.3 broadcast_in_dim.76
  55.0 3.9 convolution_convert_fusion.3
  59.0 2.7 convolution_convert_fusion.4
  61.7 2.6 convolution_convert_fusion.5
  64.3 1.9 fusion.44
  66.3 1.2 fusion
  67.5 2.1 copy-done
  69.5 1.6 fusion.12
  72.2 74.7 %shard_map.306 = (bf16[1024,2048]{1,0:T(8,128)(2,1)}, f32[128,2048]{1,0:T(8,128)}, f32[256,128]{1,0:T(8,128)}) custom-call(bf16[1024,256]{1,0:T(8,128)(2,1)} %copy.149.o_ref, bf16[2048,1024]{1,0:T(8,128)(2,1)} %w_ref.1, bf16[128,2048]{1,0:T(8,128)(2,1)} %get-tuple-element.125.x_ref, f32[1,2048]{1,0:T(1,128)} %bitcast.132), custom_call_target="tpu_custom_call" | custom-call | tf_op jit(solution)/shard_map/pallas_call | solution.py:409
  146.9 3.4 fusion.46
  151.3 34.3 %shard_map.307 = (bf16[16,2304,128]{2,1,0:T(8,128)(2,1)}, bf16[1024,768]{1,0:T(8,128)(2,1)}, bf16[1024,768]{1,0:T(8,128)(2,1)}, bf16[1024,768]{1,0:T(8,128)(2,1)}, f32[1024,1]{1,0:T(8,128)}) custom-call(bf16[1024,2048]{1,0:T(8,128)(2,1)} %get-tuple-element.68.n2_hbm, bf16[1024,2048]{1,0:T(8,128)(2,1)} %all-gather.2.cloned.1.call-done.dy_hbm, ...), custom_call_target="tpu_custom_call" | custom-call | tf_op jit(solution)/shard_map/pallas_call | solution.py:730
  186.7 3.4 fusion.45
  191.0 1.3 constant_dynamic-slice_fusion
  192.3 33.7 %shard_map.308 = (bf16[4,2112,512]{2,1,0:T(8,128)(2,1)}, bf16[1024,768]{1,0:T(8,128)(2,1)}, bf16[1024,768]{1,0:T(8,128)(2,1)}, bf16[1024,768]{1,0:T(8,128)(2,1)}, f32[1024,1]{1,0:T(8,128)}) custom-call(bf16[1024,2048]{1,0:T(8,128)(2,1)} %get-tuple-element.68.n2_hbm, bf16[1024,2048]{1,0:T(8,128)(2,1)} %all-gather.2.cloned.1.call-done.dy_hbm, ...), custom_call_target="tpu_custom_call" | custom-call | tf_op jit(solution)/shard_map/pallas_call | solution.py:730
  226.0 33.8 %shard_map.309 = (bf16[4,2112,512]{2,1,0:T(8,128)(2,1)}, bf16[1024,768]{1,0:T(8,128)(2,1)}, bf16[1024,768]{1,0:T(8,128)(2,1)}, bf16[1024,768]{1,0:T(8,128)(2,1)}, f32[1024,1]{1,0:T(8,128)}) custom-call(bf16[1024,2048]{1,0:T(8,128)(2,1)} %get-tuple-element.68.n2_hbm, bf16[1024,2048]{1,0:T(8,128)(2,1)} %all-gather.2.cloned.1.call-done.dy_hbm, ...), custom_call_target="tpu_custom_call" | custom-call | tf_op jit(solution)/shard_map/pallas_call | solution.py:730
  262.1 1.2 copy.125
  263.9 3.2 select_n.41
  269.2 29.8 %shard_map.311.part_ref = bf16[1024,2048]{1,0:T(8,128)(2,1)} custom-call(bf16[1024,768]{1,0:T(8,128)(2,1)} %get-tuple-element.71.refs_0_, bf16[1024,768]{1,0:T(8,128)(2,1)} %get-tuple-element.72.refs_1_, bf16[1024,768]{1,0:T(8,128)(2,1)} %get-tuple-element.73.refs_2_, bf16[1024,768]{1,0:T(8,128)(2,1)} %get-tuple-element.74.refs_3_, ...), custom_call_target="tpu_custom_call" | custom-call | tf_op jit(solution)/shard_map/pallas_call | solution.py:810
  299.1 85.2 %shard_map.312 = (bf16[1024,2048]{1,0:T(8,128)(2,1)}, f32[128,2048]{1,0:T(8,128)}, f32[16,2048]{1,0:T(8,128)}) custom-call(bf16[1024,2048]{1,0:T(8,128)(2,1)} %shard_map.311.part_ref, f32[128,2048]{1,0:T(8,128)} %get-tuple-element.83.h_ref, f32[1,2048]{1,0:T(1,128)} %bitcast.133, bf16[128,2048]{1,0:T(8,128)(2,1)} %get-tuple-element.63.up_ref), custom_call_target="tpu_custom_call" | custom-call | tf_op jit(solution)/shard_map/pallas_call | solution.py:456
  384.3 3.9 convolution_convert_fusion.2
  388.9 1.9 multiply_reduce_fusion
  390.8 2.3 multiply_convert_fusion
  393.1 1.5 fusion.14
  395.8 1.4 convolution_convert_fusion.1
  397.2 1.5 fusion.15
  399.4 3.7 convolution_convert_fusion
  403.1 2.5 pad_maximum_fusion
  408.1 2.9 fusion.31
  411.1 15.7 %shard_map.310.part_ref = bf16[1024,2048]{1,0:T(8,128)(2,1)} custom-call(bf16[1024,768]{1,0:T(8,128)(2,1)} %get-tuple-element.66.refs_0_, bf16[1024,768]{1,0:T(8,128)(2,1)} %get-tuple-element.69.refs_1_, bf16[2,704,2048]{2,1,0:T(8,128)(2,1)} %bitcast.106, bf16[2,704,2048]{2,1,0:T(8,128)(2,1)} %bitcast.107, bf16[1024,768]{1,0:T(8,128)(2,1)} %get-tuple-element.70.refs_4_, ...), custom_call_target="tpu_custom_call" | custom-call | tf_op jit(solution)/shard_map/pallas_call | solution.py:810
  426.9 1.7 slice_bitcast_fusion
  428.6 61.0 %shard_map.317 = (f32[128,2816]{1,0:T(8,128)}, f32[128,2816]{1,0:T(8,128)}, f32[128,2816]{1,0:T(8,128)}) custom-call(bf16[4,2304,128]{2,1,0:T(8,128)(2,1)} %bitcast.111), custom_call_target="tpu_custom_call" | custom-call | tf_op jit(solution)/shard_map/pallas_call | solution.py:866
  489.6 2.7 fusion.22
  492.3 2.7 fusion.19
  495.1 4.7 add_convert_fusion.part_ref
  499.8 46.1 %shard_map.313 = (f32[256,2048]{1,0:T(8,128)}, f32[16,2048]{1,0:T(8,128)}) custom-call(bf16[1024,2048]{1,0:T(8,128)(2,1)} %add_convert_fusion.part_ref, bf16[128,2048]{1,0:T(8,128)(2,1)} %get-tuple-element.125.x_ref, f32[1,2048]{1,0:T(1,128)} %bitcast.131, f32[128,2048]{1,0:T(8,128)} %get-tuple-element.87.dh_ref), custom_call_target="tpu_custom_call" | custom-call | tf_op jit(solution)/shard_map/pallas_call | solution.py:499
  546.8 45.0 %shard_map.314 = f32[256,2048]{1,0:T(8,128)} custom-call(bf16[1024,2048]{1,0:T(8,128)(2,1)} %shard_map.310.part_ref, f32[128,2048]{1,0:T(8,128)} %get-tuple-element.83.h_ref), custom_call_target="tpu_custom_call" | custom-call | tf_op jit(solution)/shard_map/pallas_call | solution.py:526
  592.6 10.4 %shard_map.315 = f32[16,128]{1,0:T(8,128)} custom-call(f32[16,16,128]{2,1,0:T(8,128)} %maximum_bitcast_fusion.in_ref), custom_call_target="tpu_custom_call" | custom-call | tf_op jit(solution)/shard_map/pallas_call | solution.py:913
  603.1 1.8 convert_bitcast_fusion
  604.9 1.8 convert_bitcast_fusion.1
  606.7 1.8 convert_bitcast_fusion.2
  609.5 29.2 %shard_map.316 = (f32[128,1024]{1,0:T(8,128)}, f32[128,1024]{1,0:T(8,128)}, f32[128,1024]{1,0:T(8,128)}, f32[128,1024]{1,0:T(8,128)}) custom-call(bf16[512,1024]{1,0:T(8,128)(2,1)} %reduce-scatter.9.cloned.1.call-done.refs_0_), custom_call_target="tpu_custom_call" | custom-call | tf_op jit(solution)/shard_map/pallas_call | solution.py:575
  638.7 1.3 copy.161
  640.1 1.3 copy.162
  644.6 1.1 copy.167
  (133 shorter events, 24.3 us)
Async XLA Ops:
  7.2 144.1 %all-gather.2.cloned.1.call-start = ((), (), s32[]{:S(2)}) async-start(), calls=%async_computation.4 | async-start | bytes 4718592 | tf_op jit(solution)/shard_map/all_gather | solution.py:982
  51.6 247.4 %reduce-scatter.5.cloned.1.call-start = ((), (), s32[]{:S(2)}) async-start(), calls=%async_computation.5 | async-start | bytes 11796480 | tf_op jit(solution)/shard_map/reduce_scatter | solution.py:1045
  55.0 4.0 copy-start.27
  59.0 5.4 copy-start.10
  64.3 3.1 copy-start.12
  66.3 3.2 copy-start
  71.2 79.1 %copy-start.15 = (bf16[2,128,1024]{2,1,0:T(8,128)(2,1)}, bf16[2,128,1024]{2,1,0:T(8,128)(2,1)S(1)}, u32[]{:S(2)}) copy-start(bf16[2,128,1024]{2,1,0:T(8,128)(2,1)S(1)} %fusion.12) | copy-start | bytes 1572868
  185.6 0.8 copy-start.26
  185.6 1.0 copy-start.22
  185.6 241.2 %reduce-scatter.11.cloned.1.call-start = ((), (), s32[]{:S(2)}) async-start(), calls=%async_computation.8 | async-start | bytes 10813440 | tf_op jit(solution)/shard_map/reduce_scatter | solution.py:1045
  259.8 240.0 %reduce-scatter.7.cloned.1.call-start = ((), (), s32[]{:S(2)}) async-start(), calls=%async_computation.6 | async-start | bytes 10813440 | tf_op jit(solution)/shard_map/reduce_scatter | solution.py:1045
  259.9 2.1 copy-start.17
  259.9 3.7 copy-start.14
  260.4 349.2 %reduce-scatter.9.cloned.1.call-start = ((), (), s32[]{:S(2)}) async-start(), calls=%async_computation.7 | async-start | bytes 5242880 | tf_op jit(solution)/shard_map/reduce_scatter | solution.py:1045
  299.0 89.2 %slice-start = ((s8[8388608]{0:T(1024)(128)(4,1)}), s8[4194304]{0:T(1024)(128)(4,1)S(1)}, s32[]{:S(2)}) async-start(s8[8388608]{0:T(1024)(128)(4,1)} %bitcast.94), calls=%async_computation.9 | async-start | bytes 8388608
  384.3 4.5 slice-start.1
  384.3 4.6 copy-start.13
  393.1 1.6 copy-start.11
  393.1 2.3 copy-start.16
  393.1 2.6 copy-start.29
  397.2 2.2 copy-start.28
  398.7 4.4 copy-start.5
  405.6 0.9 copy-start.23
  405.6 1.3 copy-start.2
  426.8 1.8 copy-start.24
  492.3 2.7 copy-start.6
  546.8 56.2 %copy-start.3 = (bf16[2112,512]{1,0:T(8,128)(2,1)S(1)}, bf16[2112,512]{1,0:T(8,128)(2,1)}, u32[]{:S(2)}) copy-start(bf16[2112,512]{1,0:T(8,128)(2,1)} %reduce-scatter.7.cloned.1.call-done) | copy-start | bytes 6488068
  604.9 3.5 copy-start.25
  604.9 33.8 %copy-start.1 = (f32[256,2048]{1,0:T(8,128)S(1)}, f32[256,2048]{1,0:T(8,128)}, u32[]{:S(2)}) copy-start(f32[256,2048]{1,0:T(8,128)} %shard_map.314) | copy-start | bytes 6291460
  609.5 30.5 %copy-start.4 = (f32[256,2048]{1,0:T(8,128)S(1)}, f32[256,2048]{1,0:T(8,128)}, u32[]{:S(2)}) copy-start(f32[256,2048]{1,0:T(8,128)} %get-tuple-element.144) | copy-start | bytes 6291460
  638.7 2.7 copy-start.21
  638.7 3.5 copy-start.20
  640.1 2.9 copy-start.19
  640.1 3.7 copy-start.18
  640.1 4.5 copy-start.9
  641.4 4.3 copy-start.8
  643.0 3.8 copy-start.7
Sparse Core Ops, SparseCore 0:
  51.7 59.1 all-gather.1
  185.8 99.8 reduce-scatter.4
  288.8 88.5 reduce-scatter.10
  380.3 88.5 reduce-scatter.6
  471.8 52.6 reduce-scatter.8

commit v3 on v2

v3 whole, which is shorter than its diff:
```python
import functools

import jax
import jax.numpy as jnp
from jax import lax
from jax.experimental import pallas as pl
from jax.experimental.pallas import tpu as pltpu
from jax.sharding import PartitionSpec as P

HD = 128
MESH = pl.DeviceIdType.MESH
PIECES = 2
STRIP = 16
epsilon = 1e-06
f32 = jnp.float32
bf16 = jnp.bfloat16
UP, DOWN = 0, 1


def here():
    return lax.axis_index("expert"), lax.axis_index("tensor")


def greet(nz):
    z, c = here()
    barrier = pltpu.get_barrier_semaphore()

    def tell(device):
        pl.semaphore_signal(barrier, inc=1, device_id=device, device_id_type=MESH)

    tell({"tensor": 1 - c})
    for d in range(1, nz):
        tell({"expert": lax.rem(z + d, nz)})
    pl.semaphore_wait(barrier, nz)


def remote(src, dst, send, recv, device):
    return pltpu.make_async_remote_copy(
        src_ref=src, dst_ref=dst, send_sem=send, recv_sem=recv, device_id=device, device_id_type=MESH
    )


def strips(rows, step):
    def one(i, carry):
        step(pl.ds(pl.multiple_of(i * STRIP, STRIP), STRIP))
        return carry

    lax.fori_loop(0, rows // STRIP, one, 0)


GATHER_SEMS = 4


def gather_sems(nz):
    return [pltpu.SemaphoreType.DMA((2, nz, PIECES))] * GATHER_SEMS + [pltpu.SemaphoreType.DMA]


def gather_rows(nz, own_ref, out_ref, z_send, z_recv, s_send, s_recv, local_sem):
    z, c = here()
    rows = own_ref.shape[0]
    piece = rows // PIECES

    def origin(way, d):
        return z - d if way == UP else z + d

    def inside(way, d):
        return z >= d if way == UP else z + d < nz

    def onward(way):
        return z < nz - 1 if way == UP else z > 0

    def place(block, core, p):
        return out_ref.at[pl.ds(pl.multiple_of((block * 2 + core) * rows + p * piece, piece), piece)]

    def source(way, d, p):
        return own_ref.at[pl.ds(p * piece, piece)] if d == 0 else place(origin(way, d), c, p)

    def along(way, d, p):
        device = {"expert": z + 1 if way == UP else z - 1}
        return remote(
            source(way, d, p), place(origin(way, d), c, p), z_send.at[way, d, p], z_recv.at[way, d, p], device
        )

    def across(way, d, p):
        return remote(
            source(way, d, p), place(origin(way, d), c, p), s_send.at[way, d, p], s_recv.at[way, d, p],
            {"tensor": 1 - c},
        )

    def arrived(way, d, p):
        dst = place(origin(way, d), c, p)
        remote(dst, dst, z_send.at[way, d - 1, p], z_recv.at[way, d - 1, p], {"tensor": 1 - c}).wait_recv()

    def crossed(way, d, p):
        dst = place(origin(way, d), 1 - c, p)
        remote(dst, dst, s_send.at[way, d, p], s_recv.at[way, d, p], {"tensor": 1 - c}).wait_recv()

    mine = pltpu.make_async_copy(
        own_ref, out_ref.at[pl.ds(pl.multiple_of((z * 2 + c) * rows, rows), rows)], local_sem
    )
    for p in range(PIECES):
        for way in (UP, DOWN):
            pl.when(onward(way))(lambda way=way, p=p: along(way, 0, p).start())
        across(UP, 0, p).start()
    mine.start()
    for d in range(1, nz):
        for p in range(PIECES):
            for way in (UP, DOWN):

                @pl.when(inside(way, d))
                def _(way=way, d=d, p=p):
                    arrived(way, d, p)
                    pl.when(onward(way))(lambda: along(way, d, p).start())
                    across(way, d, p).start()

    for p in range(PIECES):
        crossed(UP, 0, p)
        across(UP, 0, p).wait_send()
        for way in (UP, DOWN):
            pl.when(onward(way))(lambda way=way, p=p: along(way, 0, p).wait_send())
            for d in range(1, nz):

                @pl.when(inside(way, d))
                def _(way=way, d=d, p=p):
                    crossed(way, d, p)
                    across(way, d, p).wait_send()
                    pl.when(onward(way))(lambda: along(way, d, p).wait_send())

    mine.wait()


REDUCE_SCRATCH = 8


def reduce_scratch(nz, rows, width):
    return [
        pltpu.VMEM((nz, rows, width), bf16),
        pltpu.VMEM((nz + 1, rows, width), bf16),
        pltpu.VMEM((nz, rows, width), bf16),
        pltpu.VMEM((rows, width), f32),
        pltpu.SemaphoreType.DMA((nz, PIECES)),
        pltpu.SemaphoreType.DMA((nz, PIECES)),
        pltpu.SemaphoreType.DMA((nz, PIECES)),
        pltpu.SemaphoreType.DMA((nz + 1, PIECES)),
    ]


def block_order(nz, z, s):
    down = 2 * z // nz
    far = jnp.maximum(z, nz - 1 - z)
    near = nz - 1 - far
    late = s - (far - near)
    distance = jnp.where(late < 0, far - s, near - late // 2)
    sign = (1 - 2 * down) * jnp.where(late < 0, 1, 1 - 2 * lax.rem(late + nz * 2, 2))
    return z + sign * distance


class Reducer:
    def __init__(self, nz, part, side, inbox, outbox, total, s_send, s_recv, z_send, z_recv):
        self.nz, self.part, self.side, self.inbox, self.outbox, self.total = nz, part, side, inbox, outbox, total
        self.s_send, self.s_recv, self.z_send, self.z_recv = s_send, s_recv, z_send, z_recv
        self.z, self.c = here()
        self.rows = total.shape[0]
        self.piece = self.rows // PIECES

    def block(self, s):
        return block_order(self.nz, self.z, s)

    def cut(self, p):
        return pl.ds(p * self.piece, self.piece)

    def across(self, block, p):
        start = (block * 2 + 1 - self.c) * self.rows + p * self.piece
        src = self.part.at[pl.ds(pl.multiple_of(start, self.piece), self.piece)]
        return remote(
            src, self.side.at[block, self.cut(p)], self.s_send.at[block, p], self.s_recv.at[block, p],
            {"tensor": 1 - self.c},
        )

    def along(self, block, p):
        up = block > self.z
        slot = jnp.where(block == self.z - 1, self.nz, block)
        return remote(
            self.outbox.at[block, self.cut(p)], self.inbox.at[slot, self.cut(p)], self.z_send.at[block, p],
            self.z_recv.at[slot, p], {"expert": self.z + jnp.where(up, 1, -1)},
        )

    def arrived(self, slot, p):
        dst = self.inbox.at[slot, self.cut(p)]
        remote(dst, dst, self.z_send.at[0, p], self.z_recv.at[slot, p], {"tensor": 1 - self.c}).wait_recv()

    def mine(self, block, at):
        base = (block * 2 + self.c) * self.rows
        own = self.part[pl.ds(pl.multiple_of(base + at.start, STRIP), STRIP), :].astype(f32)
        return own + self.side[block, at, :].astype(f32)

    def strips(self, p, step):
        def one(i, carry):
            step(pl.ds(pl.multiple_of(p * self.piece + i * STRIP, STRIP), STRIP))
            return carry

        lax.fori_loop(0, self.piece // STRIP, one, 0)

    def begin(self, s):
        for p in range(PIECES):
            self.across(self.block(s), p).start()

    def forward(self, s):
        block = self.block(s)
        behind = jnp.where(block > self.z, self.z, self.nz - 1 - self.z) > 0
        for p in range(PIECES):
            self.across(block, p).wait_recv()

            @pl.when(behind)
            def _(p=p):
                self.arrived(block, p)

                def add(at):
                    self.outbox[block, at, :] = (self.mine(block, at) + self.inbox[block, at, :].astype(f32)).astype(bf16)

                self.strips(p, add)

            @pl.when(jnp.logical_not(behind))
            def _(p=p):
                def keep(at):
                    self.outbox[block, at, :] = self.mine(block, at).astype(bf16)

                self.strips(p, keep)

            self.along(block, p).start()

    def finish(self):
        z, nz = self.z, self.nz
        for p in range(PIECES):
            self.across(z, p).wait_recv()

            def first(at):
                self.total[at, :] = self.mine(z, at)

            self.strips(p, first)
            for slot, some in ((z, z > 0), (nz, z < nz - 1)):

                @pl.when(some)
                def _(slot=slot, p=p):
                    self.arrived(slot, p)

                    def add(at):
                        self.total[at, :] += self.inbox[slot, at, :].astype(f32)

                    self.strips(p, add)

    def drain(self):
        def one(s, carry):
            block = self.block(s)
            for p in range(PIECES):
                self.across(block, p).wait_send()
                pl.when(s < self.nz - 1)(lambda p=p: self.along(block, p).wait_send())
            return carry

        lax.fori_loop(0, self.nz, one, 0)


def params(name, **more):
    return pltpu.CompilerParams(
        collective_id=name, has_side_effects=True, vmem_limit_bytes=56 * 1024 * 1024, **more
    )


VMEM = pl.BlockSpec(memory_space=pltpu.VMEM)
ANY = pl.BlockSpec(memory_space=pl.ANY)


def norm_rows(values, gain):
    inverse = lax.rsqrt(jnp.mean(values * values, axis=-1, keepdims=True) + epsilon)
    return values * inverse * gain, inverse


def norm_back(values, gain, upstream):
    inverse = lax.rsqrt(jnp.mean(values * values, axis=-1, keepdims=True) + epsilon)
    scaled = upstream * gain
    inner = jnp.mean(scaled * values, axis=-1, keepdims=True)
    change = inverse * scaled - values * inverse * inverse * inverse * inner
    return change, upstream * values * inverse


def first_gather(nz, x, gain, marks, name):
    rows, width = x.shape

    def kernel(x_ref, gain_ref, marks_ref, out_ref, all_ref, own, m_send, m_recv, m_local, *sems):
        z, c = here()
        greet(nz)
        keep = pltpu.make_async_copy(marks_ref, all_ref.at[z], m_local)
        keep.start()

        def send(way, d):
            to = z + d if way == UP else z - d
            return remote(marks_ref, all_ref.at[z], m_send.at[way, d], m_recv.at[way, d], {"expert": to})

        def take(way, d):
            dst = all_ref.at[z - d if way == UP else z + d]
            remote(dst, dst, m_send.at[way, d], m_recv.at[way, d], {"tensor": 1 - c}).wait_recv()

        for d in range(1, nz):
            for way in (UP, DOWN):
                pl.when(z + d < nz if way == UP else z >= d)(lambda way=way, d=d: send(way, d).start())

        def step(at):
            normed, _ = norm_rows(x_ref[at, :].astype(f32), gain_ref[...])
            own[at, :] = normed.astype(bf16)

        strips(rows, step)
        gather_rows(nz, own, out_ref, *sems)
        keep.wait()
        for d in range(1, nz):
            for way in (UP, DOWN):
                pl.when(z + d < nz if way == UP else z >= d)(lambda way=way, d=d: send(way, d).wait_send())
                pl.when(z >= d if way == UP else z + d < nz)(lambda way=way, d=d: take(way, d))

    return pl.pallas_call(
        kernel,
        out_shape=[
            jax.ShapeDtypeStruct((nz * 2 * rows, width), bf16),
            jax.ShapeDtypeStruct((nz,) + marks.shape, jnp.int32),
        ],
        in_specs=[VMEM, VMEM, VMEM],
        out_specs=[ANY, ANY],
        scratch_shapes=[
            pltpu.VMEM((rows, width), bf16),
            pltpu.SemaphoreType.DMA((2, nz)),
            pltpu.SemaphoreType.DMA((2, nz)),
            pltpu.SemaphoreType.DMA,
        ]
        + gather_sems(nz),
        compiler_params=params(name),
    )(x, gain, marks)


def project_and_gather(nz, o, weight, x, gain, name):
    rows, width = x.shape
    full = 2 * rows
    cols = o.shape[1]

    def kernel(o_ref, w_ref, x_ref, gain_ref, n2_ref, h_ref, inv_ref, heads, acc, give, take, own, inv_own, a_send,
               a_recv, e_send, e_recv, i_sems, *sems):
        z, c = here()
        greet(nz)

        def inside(way, d):
            return z + d < nz if way == UP else z >= d

        def send(way, d):
            to = z + d if way == UP else z - d
            src = o_ref.at[pl.ds(pl.multiple_of(to * full, full), full)]
            return remote(src, heads.at[way, d], a_send.at[way, d], a_recv.at[way, d], {"expert": to})

        for d in range(nz - 1, 0, -1):
            for way in (UP, DOWN):
                pl.when(inside(way, d))(lambda way=way, d=d: send(way, d).start())

        tile = 512 if width % 512 == 0 else width

        def project(block, left, fresh):
            at = pl.ds(pl.multiple_of(block * cols, cols), cols)

            def one(i, carry):
                to = pl.ds(pl.multiple_of(i * tile, tile), tile)
                value = lax.dot_general(
                    left(), w_ref[to, at], (((1,), (1,)), ((), ())), preferred_element_type=f32
                )
                acc[:, to] = value if fresh else acc[:, to] + value
                return carry

            lax.fori_loop(0, width // tile, one, 0)

        project(z, lambda: o_ref[pl.ds(pl.multiple_of(z * full, full), full), :], True)
        for d in range(1, nz):
            for way in (UP, DOWN):
                @pl.when(z >= d if way == UP else z + d < nz)
                def _(way=way, d=d):
                    remote(
                        heads.at[way, d], heads.at[way, d], a_send.at[way, d], a_recv.at[way, d], {"tensor": 1 - c}
                    ).wait_recv()
                    project(z - d if way == UP else z + d, lambda: heads[way, d], False)

        def pack(at):
            give[at, :] = acc[pl.ds(pl.multiple_of((1 - c) * rows + at.start, STRIP), STRIP), :].astype(bf16)

        strips(rows, pack)
        swap = remote(give, take, e_send, e_recv, {"tensor": 1 - c})
        swap.start()
        swap.wait_recv()

        def norm(at):
            mixed = acc[pl.ds(pl.multiple_of(c * rows + at.start, STRIP), STRIP), :] + take[at, :].astype(f32)
            h = x_ref[at, :].astype(f32) + mixed
            normed, inverse = norm_rows(h, gain_ref[...])
            h_ref[at, :] = h
            own[at, :] = normed.astype(bf16)
            inv_own[at, :] = jnp.broadcast_to(inverse, (STRIP, 128))

        strips(rows, norm)
        spot = inv_ref.at[pl.ds(pl.multiple_of(c * rows, rows), rows)]
        keep = pltpu.make_async_copy(inv_own, spot, i_sems.at[0])
        pass_on = remote(inv_own, spot, i_sems.at[1], i_sems.at[2], {"tensor": 1 - c})
        keep.start()
        pass_on.start()
        gather_rows(nz, own, n2_ref, *sems)
        keep.wait()
        pass_on.wait()
        swap.wait_send()
        for d in range(1, nz):
            for way in (UP, DOWN):
                pl.when(inside(way, d))(lambda way=way, d=d: send(way, d).wait_send())

    return pl.pallas_call(
        kernel,
        out_shape=[
            jax.ShapeDtypeStruct((nz * full, width), bf16),
            jax.ShapeDtypeStruct((rows, width), f32),
            jax.ShapeDtypeStruct((full, 128), f32),
        ],
        in_specs=[VMEM] * 4,
        out_specs=[ANY, VMEM, ANY],
        scratch_shapes=[
            pltpu.VMEM((2, nz, full, cols), bf16),
            pltpu.VMEM((full, width), f32),
            pltpu.VMEM((rows, width), bf16),
            pltpu.VMEM((rows, width), bf16),
            pltpu.VMEM((rows, width), bf16),
            pltpu.VMEM((rows, 128), f32),
            pltpu.SemaphoreType.DMA((2, nz)),
            pltpu.SemaphoreType.DMA((2, nz)),
            pltpu.SemaphoreType.DMA,
            pltpu.SemaphoreType.DMA,
            pltpu.SemaphoreType.DMA((3,)),
        ]
        + gather_sems(nz),
        compiler_params=params(name),
    )(o, weight, x, gain)


def swap_rows(nz, own, out_ref, sems):
    z, c = here()
    rows = own.shape[0]
    spot = out_ref.at[pl.ds(pl.multiple_of(c * rows, rows), rows)]
    keep = pltpu.make_async_copy(own, spot, sems.at[0])
    pass_on = remote(own, spot, sems.at[1], sems.at[2], {"tensor": 1 - c})
    keep.start()
    pass_on.start()
    keep.wait()
    pass_on.wait()


def spread(nz, parts, splits, name):
    block = parts[0].shape[0] // nz
    count = len(parts)
    outs = [(i, s) for i in range(count) for s in range(splits[i])]

    def kernel(*refs):
        ins, outs_refs, rest = refs[:count], refs[count : count + len(outs)], refs[count + len(outs) :]
        boxes, send_sem, recv_sem = rest[:count], rest[count], rest[count + 1]
        z, c = here()
        greet(nz)

        def cut(i, to):
            return ins[i].at[pl.ds(pl.multiple_of(to * block, block), block)]

        def send(i, way, d):
            to = z + d if way == UP else z - d
            return remote(cut(i, to), boxes[i].at[z], send_sem.at[i, way, d], recv_sem.at[i, way, d], {"expert": to})

        def take(i, way, d):
            dst = boxes[i].at[z - d if way == UP else z + d]
            remote(dst, dst, send_sem.at[i, way, d], recv_sem.at[i, way, d], {"tensor": 1 - c}).wait_recv()

        for i in range(count):
            for d in range(nz - 1, 0, -1):
                for way in (UP, DOWN):
                    pl.when(z + d < nz if way == UP else z >= d)(lambda i=i, way=way, d=d: send(i, way, d).start())
        for i in range(count):
            boxes[i][z] = ins[i][pl.ds(pl.multiple_of(z * block, block), block), :]
        for i in range(count):
            for d in range(1, nz):
                for way in (UP, DOWN):
                    pl.when(z + d < nz if way == UP else z >= d)(lambda i=i, way=way, d=d: send(i, way, d).wait_send())
                    pl.when(z >= d if way == UP else z + d < nz)(lambda i=i, way=way, d=d: take(i, way, d))
            for j, (k, s) in enumerate(outs):
                if k == i:
                    cols = ins[i].shape[1] // splits[i]
                    for b in range(nz):
                        outs_refs[j][:, b * cols : (b + 1) * cols] = boxes[i][b, :, s * cols : (s + 1) * cols].astype(f32)

    return pl.pallas_call(
        kernel,
        out_shape=[
            jax.ShapeDtypeStruct((block, nz * parts[i].shape[1] // splits[i]), f32) for i, _ in outs
        ],
        in_specs=[VMEM] * count,
        out_specs=[VMEM] * len(outs),
        scratch_shapes=[pltpu.VMEM((nz, block, p.shape[1]), bf16) for p in parts]
        + [pltpu.SemaphoreType.DMA((count, 2, nz)), pltpu.SemaphoreType.DMA((count, 2, nz))],
        compiler_params=params(name),
    )(*parts)


TILE = 256
TALL = 512
LANES = 128


def nt_dot(left, right):
    return lax.dot_general(left, right, (((1,), (1,)), ((), ())), preferred_element_type=f32)


def nn_dot(left, right):
    return jnp.dot(left, right, preferred_element_type=f32)


def tiles(count, step, size=TILE):
    def one(i, carry):
        step(i, pl.ds(pl.multiple_of(i * size, size), size))
        return carry

    lax.fori_loop(0, count, one, 0)


def padded(columns):
    return -(-columns // LANES) * LANES


def window(columns, place):
    first = place * columns // LANES * LANES
    return first, place * columns - first


def window_width(columns, places):
    return max(padded(window(columns, i)[1] + columns) for i in range(places))


def hidden_layer(nz, n2, dy, gate, weights, groups):
    seq, width = n2.shape
    shared = weights[0].ndim == 2
    experts = 1 if shared else weights[0].shape[0]
    buffers = min(experts, 2)
    ffn = weights[0].shape[1] // nz if shared else weights[0].shape[1]
    held = window_width(ffn, nz) if shared else ffn
    kept = held if shared else padded(ffn)
    block = width // groups
    lane = min(block, TILE)
    per = TILE // lane
    count, slabs = seq // TILE, width // TILE
    strip = 32
    product = nn_dot if shared else nt_dot
    w_shape = (width, held) if shared else (held, width)

    def kernel(n2_hbm, dy_hbm, wg_hbm, wu_hbm, wd_hbm, gate_ref, grad_hbm, da_hbm, db_hbm, gu_hbm, dgate_ref,
               n2_ref, dy_ref, wg, wu, wd, a, b, back, da, db, gu, turned, slab, in_sem, row_sem, out_sem, slab_sem):
        z = lax.axis_index("expert")
        first = pl.multiple_of(z * ffn // LANES * LANES, LANES)
        skip = z * ffn - first

        def pick(ref, e):
            return ref.at[:, pl.ds(first, held)] if shared else ref.at[e]

        def weight(i, e):
            slot = lax.rem(e, buffers)
            src, dst = ((wg_hbm, wg), (wu_hbm, wu), (wd_hbm, wd))[i]
            return pltpu.make_async_copy(pick(src, e), dst.at[slot], in_sem.at[i, slot])

        rows_in = [
            pltpu.make_async_copy(n2_hbm, n2_ref, row_sem.at[0]), pltpu.make_async_copy(dy_hbm, dy_ref, row_sem.at[1])
        ]
        weight(0, 0).start()
        rows_in[0].start()
        weight(1, 0).start()
        weight(2, 0).start()
        rows_in[1].start()
        if kept > held:
            for ref in (da, db, gu):
                ref[:, held:] = jnp.zeros((seq, kept - held), bf16)

        def expert(e, carry):
            slot = lax.rem(e, buffers)
            weight(0, e).wait()
            pl.when(e == 0)(rows_in[0].wait)

            def one(i, at):
                a[at, :] = product(n2_ref[at, :], wg[slot])

            tiles(seq // TALL, one, TALL)
            weight(1, e).wait()

            def two(i, at):
                b[at, :] = product(n2_ref[at, :], wu[slot])

            tiles(seq // TALL, two, TALL)
            weight(2, e).wait()
            pl.when(e == 0)(rows_in[1].wait)
            if experts > 1:

                @pl.when(e + 1 < experts)
                def _():
                    for i in range(3):
                        weight(i, e + 1).start()

            def three(i, at):
                back[...] = product(dy_ref[at, :], wd[slot])

                def point(j, carry):
                    row = pl.ds(pl.multiple_of(i * TILE + j * strip, strip), strip)
                    local = pl.ds(pl.multiple_of(j * strip, strip), strip)
                    av, bv, kv, gv = a[row, :], b[row, :], back[local, :], gate_ref[e, row, :]
                    sig = 1.0 / (1.0 + jnp.exp(-av))
                    act = av * sig
                    u = act * bv
                    if shared:
                        column = lax.broadcasted_iota(jnp.int32, (strip, held), 1)
                        mine = jnp.logical_and(column >= skip, column < skip + ffn)
                        u, kv = jnp.where(mine, u, 0.0), jnp.where(mine, kv, 0.0)
                    dgate_ref[e, row, :] = jnp.sum(u * kv, axis=-1, keepdims=True)
                    gu[row, :held] = (gv * u).astype(bf16)
                    du = gv * kv
                    da[row, :held] = (du * bv * (sig + act * (1.0 - sig))).astype(bf16)
                    db[row, :held] = (du * act).astype(bf16)
                    return carry

                lax.fori_loop(0, TILE // strip, point, 0)
                for k, ref in enumerate((da, db, gu)):
                    turned[k, :, at] = ref[at, :held].T

            tiles(count, three)
            saves = [
                pltpu.make_async_copy(src, dst.at[e], out_sem.at[i])
                for i, (src, dst) in enumerate(((da, da_hbm), (db, db_hbm), (gu, gu_hbm)))
            ]
            for save in saves:
                save.start()

            def leave(i):
                slot = lax.rem(i, 2)
                below = pl.ds(pl.multiple_of(e * 3 * held, 16), 3 * held)
                if per > 1:
                    dst = grad_hbm.at[pl.ds(i * per, per), below]
                else:
                    many = block // TILE
                    to = pl.ds(pl.multiple_of(lax.rem(i, many) * TILE, TILE), TILE)
                    dst = grad_hbm.at[pl.ds(i // many, 1), below, to]
                return pltpu.make_async_copy(slab.at[slot], dst, slab_sem.at[slot])

            def four(i, at):
                slot = lax.rem(i, 2)
                pl.when(i >= 2)(lambda: leave(i).wait())
                for k, right in enumerate((n2_ref, n2_ref, dy_ref)):
                    value = nn_dot(turned[k], right[:, at]).astype(bf16)
                    for j in range(per):
                        slab[slot, j, k * held : (k + 1) * held, :] = value[:, j * lane : (j + 1) * lane]
                leave(i).start()

            tiles(slabs, four)
            leave(slabs - 2).wait()
            leave(slabs - 1).wait()
            for save in saves:
                save.wait()
            return carry

        if experts == 1:
            expert(0, 0)
        else:
            lax.fori_loop(0, experts, expert, 0)

    hidden = jax.ShapeDtypeStruct((experts, seq, kept), bf16)
    return pl.pallas_call(
        kernel,
        out_shape=[
            jax.ShapeDtypeStruct((groups, experts * 3 * held, block), bf16), hidden, hidden, hidden,
            jax.ShapeDtypeStruct((experts, seq, 1), f32),
        ],
        in_specs=[ANY] * 5 + [VMEM],
        out_specs=[ANY] * 4 + [VMEM],
        scratch_shapes=[
            pltpu.VMEM((seq, width), bf16), pltpu.VMEM((seq, width), bf16),
            pltpu.VMEM((buffers,) + w_shape, bf16), pltpu.VMEM((buffers,) + w_shape, bf16), pltpu.VMEM((buffers,) + w_shape, bf16),
            pltpu.VMEM((seq, held), f32), pltpu.VMEM((seq, held), f32), pltpu.VMEM((TILE, held), f32),
            pltpu.VMEM((seq, kept), bf16), pltpu.VMEM((seq, kept), bf16), pltpu.VMEM((seq, kept), bf16),
            pltpu.VMEM((3, held, seq), bf16),
            pltpu.VMEM((2, per, 3 * held, lane), bf16),
            pltpu.SemaphoreType.DMA((3, buffers)), pltpu.SemaphoreType.DMA((2,)), pltpu.SemaphoreType.DMA((3,)),
            pltpu.SemaphoreType.DMA((2,)),
        ],
        compiler_params=pltpu.CompilerParams(vmem_limit_bytes=58 * 1024 * 1024),
    )(n2, dy, *weights, gate)


class Products:
    def __init__(self, nz, experts, shared, extra):
        self.nz, self.experts, self.shared = nz, experts, shared
        _, self.seq, self.kept = experts[0][0][0].shape
        _, self.ffn, self.width = experts[0][1][0].shape
        self.held = shared[0][0][0].shape[2]
        self.own = shared[0][1].shape[1] // nz
        self.more = [] if extra is None else list(extra)
        self.inputs = (
            [left[0] for left, _ in experts] + [right[0] for _, right in experts] + [left[0] for left, _ in shared]
            + [right for _, right in shared] + self.more
        )
        ne, ns = len(experts), len(shared)
        self.specs = [ANY] * (2 * (ne + ns)) + [VMEM] * len(self.more)
        self.scratch = [
            pltpu.VMEM((self.seq, ne * self.kept), bf16), pltpu.VMEM((ne * self.kept, self.width), bf16),
            pltpu.VMEM((self.seq, ns * self.held), bf16), pltpu.VMEM((self.width, ns * self.held), bf16),
            pltpu.SemaphoreType.DMA((2 * (ne + ns),)),
        ]
        self.step = 512 if self.width % 512 == 0 else self.width

    def bind(self, refs, scratch):
        ne, ns = len(self.experts), len(self.shared)
        self.refs = refs
        self.left, self.right, self.sleft, self.sright, self.sem = scratch
        first = pl.multiple_of(lax.axis_index("expert") * self.own // LANES * LANES, LANES)
        kept, held = self.kept, self.held
        pairs = []
        for i in range(ne):
            pairs.append((refs[ne + i].at[self.experts[i][1][1]], self.right.at[pl.ds(i * kept, self.ffn)]))
            pairs.append((refs[i].at[self.experts[i][0][1]], self.left.at[:, pl.ds(i * kept, kept)]))
        base = 2 * ne
        for i in range(ns):
            pairs.append((refs[base + ns + i].at[:, pl.ds(first, held)], self.sright.at[:, pl.ds(i * held, held)]))
            pairs.append((refs[base + i].at[self.shared[i][0][1]], self.sleft.at[:, pl.ds(i * held, held)]))
        self.loads = [pltpu.make_async_copy(src, dst, self.sem.at[i]) for i, (src, dst) in enumerate(pairs)]
        self.small = refs[2 * (ne + ns) :]

    def fetch(self):
        for load in self.loads:
            load.start()
        if self.kept > self.ffn:
            for i in range(len(self.experts)):
                self.right[i * self.kept + self.ffn : (i + 1) * self.kept, :] = jnp.zeros(
                    (self.kept - self.ffn, self.width), bf16
                )

    def wait(self):
        for load in self.loads:
            load.wait()

    def block(self, b, out):
        rows = self.seq // self.nz
        at = pl.ds(pl.multiple_of(b * rows, rows), rows)

        def one(j, carry):
            to = pl.ds(pl.multiple_of(j * self.step, self.step), self.step)
            value = nn_dot(self.left[at, :], self.right[:, to]) + nt_dot(self.sleft[at, :], self.sright[to, :])
            if self.more:
                value += nt_dot(self.small[0][at, :], self.small[1][to, :])
            out[at, to] = value.astype(bf16)
            return carry

        lax.fori_loop(0, self.width // self.step, one, 0)


def reduce_and_gather(nz, products, h, gain, upstream, name):
    rows, width = h.shape
    n_in, n_scratch = len(products.inputs), len(products.scratch)

    def kernel(*refs):
        p_refs, (h_ref, gain_ref, up_ref, out_ref, dh_ref, gg_ref) = refs[:n_in], refs[n_in : n_in + 6]
        rest = refs[n_in + 6 :]
        p_scratch, (part, own), rest = rest[:n_scratch], rest[n_scratch : n_scratch + 2], rest[n_scratch + 2 :]
        scratch, sems = rest[:REDUCE_SCRATCH], rest[REDUCE_SCRATCH:]
        total = scratch[3]
        products.bind(p_refs, p_scratch)
        products.fetch()
        greet(nz)
        reducer = Reducer(nz, part, *scratch)
        products.wait()

        def one(s, carry):
            products.block(reducer.block(s), part)
            reducer.begin(s)
            pl.when(s >= 1)(lambda: reducer.forward(s - 1))
            return carry

        lax.fori_loop(0, nz, one, 0)
        reducer.finish()
        gg_ref[...] = jnp.zeros_like(gg_ref)

        def step(at):
            change, along = norm_back(h_ref[at, :], gain_ref[...], total[at, :])
            dh = up_ref[at, :].astype(f32) + change
            dh_ref[at, :] = dh
            own[at, :] = dh.astype(bf16)
            gg_ref[...] += along

        strips(rows, step)
        gather_rows(nz, own, out_ref, *sems)
        reducer.drain()

    return pl.pallas_call(
        kernel,
        out_shape=[
            jax.ShapeDtypeStruct((nz * 2 * rows, width), bf16),
            jax.ShapeDtypeStruct((rows, width), f32),
            jax.ShapeDtypeStruct((STRIP, width), f32),
        ],
        in_specs=products.specs + [VMEM] * 3,
        out_specs=[ANY, VMEM, VMEM],
        scratch_shapes=products.scratch
        + [pltpu.VMEM((nz * 2 * rows, width), bf16), pltpu.VMEM((rows, width), bf16)]
        + reduce_scratch(nz, rows, width)
        + gather_sems(nz),
        compiler_params=params(name),
    )(*products.inputs, h, gain, upstream)


def reduce_last(nz, d_heads, weights, x, gain, dh, products, h, name):
    rows, width = x.shape
    n_in, n_scratch = len(products.inputs), len(products.scratch)

    def kernel(*refs):
        p_refs, (d_ref, w_ref, x_ref, gain_ref, dh_ref, h_ref, in_ref, out_ref, gg_ref) = (
            refs[:n_in], refs[n_in : n_in + 9],
        )
        rest = refs[n_in + 9 :]
        p_scratch, (d_part, b_part, own, sems), rest = (
            rest[:n_scratch], rest[n_scratch : n_scratch + 4], rest[n_scratch + 4 :],
        )
        d_scratch, b_scratch = rest[:REDUCE_SCRATCH], rest[REDUCE_SCRATCH:]
        d_total, b_total = d_scratch[3], b_scratch[3]
        products.bind(p_refs, p_scratch)
        products.fetch()
        greet(nz)
        z, c = here()
        first, second = Reducer(nz, d_part, *d_scratch), Reducer(nz, b_part, *b_scratch)
        step_cols = products.step

        def inner(block):
            at = pl.ds(pl.multiple_of(block * 2 * rows, 2 * rows), 2 * rows)

            def one(j, carry):
                to = pl.ds(pl.multiple_of(j * step_cols, step_cols), step_cols)
                d_part[at, to] = nt_dot(d_ref[at, :], w_ref[to, :]).astype(bf16)
                return carry

            lax.fori_loop(0, width // step_cols, one, 0)

        def one(s, carry):
            inner(first.block(s))
            first.begin(s)
            pl.when(s == 0)(products.wait)
            products.block(second.block(s), b_part)
            second.begin(s)

            @pl.when(s >= 1)
            def _():
                first.forward(s - 1)
                second.forward(s - 1)

            return carry

        lax.fori_loop(0, nz, one, 0)
        first.finish()
        gg_ref[...] = jnp.zeros_like(gg_ref)

        def step(at):
            change, along = norm_back(x_ref[at, :].astype(f32), gain_ref[...], d_total[at, :])
            own[0, at, :] = dh_ref[at, :] + change
            gg_ref[...] += along

        strips(rows, step)

        def leave(i, ref):
            spot = ref.at[pl.ds(pl.multiple_of(c * rows, rows), rows)]
            return (
                pltpu.make_async_copy(own.at[i], spot, sems.at[i, 0]),
                remote(own.at[i], spot, sems.at[i, 1], sems.at[i, 2], {"tensor": 1 - c}),
            )

        for copy in leave(0, in_ref):
            copy.start()
        second.finish()

        def last(at):
            own[1, at, :] = h_ref[at, :] + b_total[at, :]

        strips(rows, last)
        for copy in leave(1, out_ref):
            copy.start()
        first.drain()
        second.drain()
        for copy in (*leave(0, in_ref), *leave(1, out_ref)):
            copy.wait()

    return pl.pallas_call(
        kernel,
        out_shape=[
            jax.ShapeDtypeStruct((2 * rows, width), f32),
            jax.ShapeDtypeStruct((2 * rows, width), f32),
            jax.ShapeDtypeStruct((STRIP, width), f32),
        ],
        in_specs=products.specs + [VMEM] * 6,
        out_specs=[ANY, ANY, VMEM],
        scratch_shapes=products.scratch
        + [
            pltpu.VMEM((nz * 2 * rows, width), bf16), pltpu.VMEM((nz * 2 * rows, width), bf16),
            pltpu.VMEM((2, rows, width), f32), pltpu.SemaphoreType.DMA((2, 3)),
        ]
        + reduce_scratch(nz, rows, width) * 2,
        compiler_params=params(name),
    )(*products.inputs, d_heads, weights, x, gain, dh, h)


def assemble(nz, box, columns):
    _, held, block = box.shape
    count = 3
    held //= count

    def kernel(box_ref, *outs):
        for k in range(count):
            end = 0
            for b in range(nz):
                first, _ = window(columns, b)
                value = box_ref[b, k * held : (k + 1) * held, :].astype(f32).T
                shared = max(end - first, 0)
                if shared:
                    outs[k][:, first:end] += value[:, :shared]
                last = min(first + held, nz * columns)
                outs[k][:, first + shared : last] = value[:, shared : last - first]
                end = last

    return pl.pallas_call(
        kernel,
        out_shape=[jax.ShapeDtypeStruct((block, nz * columns), f32)] * count,
        in_specs=[VMEM],
        out_specs=[VMEM] * count,
        compiler_params=pltpu.CompilerParams(vmem_limit_bytes=40 * 1024 * 1024),
    )(box)


def sum_everywhere(nz, ndp, parts, name):
    n, rows, block = parts.shape

    def kernel(in_ref, out_ref, box, total, other, send_sem, recv_sem, swap_sem):
        z, c = here()
        me = lax.axis_index("dp") * nz + z
        barrier = pltpu.get_barrier_semaphore()

        def peer(k):
            at = lax.rem(me + k, n)
            return at, {"dp": at // nz, "expert": lax.rem(at, nz)}

        pl.semaphore_signal(barrier, inc=1, device_id={"tensor": 1 - c}, device_id_type=MESH)
        for k in range(1, n):
            pl.semaphore_signal(barrier, inc=1, device_id=peer(k)[1], device_id_type=MESH)
        pl.semaphore_wait(barrier, n)

        def send(k):
            at, device = peer(k)
            return remote(in_ref.at[at], box.at[k], send_sem.at[k], recv_sem.at[k], device)

        for k in range(1, n):
            send(k).start()
        total[...] = in_ref[me]
        for k in range(1, n):
            send(k).wait_recv()
            total[...] += box[k]
        swap = remote(total, other, swap_sem.at[0], swap_sem.at[1], {"tensor": 1 - c})
        swap.start()
        swap.wait_recv()
        out_ref[...] = total[...] + other[...]
        swap.wait_send()
        for k in range(1, n):
            send(k).wait_send()

    return pl.pallas_call(
        kernel,
        out_shape=jax.ShapeDtypeStruct((rows, block), f32),
        in_specs=[VMEM],
        out_specs=VMEM,
        scratch_shapes=[
            pltpu.VMEM((n, rows, block), f32), pltpu.VMEM((rows, block), f32), pltpu.VMEM((rows, block), f32),
            pltpu.SemaphoreType.DMA((n,)), pltpu.SemaphoreType.DMA((n,)), pltpu.SemaphoreType.DMA((2,)),
        ],
        compiler_params=params(name),
    )(parts)


SEQ_AXES = ("expert", "tensor")


def cross_rows(left, right):
    return lax.dot_general(left, right, (((0,), (0,)), ((), ())), preferred_element_type=f32)


def cross_cols(left, right):
    return lax.dot_general(left, right, (((1,), (1,)), ((), ())), preferred_element_type=f32)


def dot(left, right):
    return jnp.dot(left, right, preferred_element_type=f32)


def two_parts(values):
    high = values.astype(bf16)
    return high, (values - high.astype(f32)).astype(bf16)


def body(
    tokens, segments, routes, norm1_gain, q_weight, k_weight, v_weight, o_weight, norm2_gain,
    router_weight, shared_gate_vector, shared_gate_weight, shared_up_weight, shared_down_weight,
    expert_gate_weight, expert_up_weight, expert_down_weight, out_grad,
):
    nz = lax.axis_size("expert")
    nc = lax.axis_size("tensor")
    z = lax.axis_index("expert")
    c = lax.axis_index("tensor")
    rows, width = tokens.shape
    own_rows = rows // nc
    local_count, _, ffn = expert_gate_weight.shape
    expert_count = local_count * nz
    head_cols = q_weight.shape[1] // nz
    shared_cols = shared_gate_weight.shape[1] // nz
    heads = head_cols // HD
    seq = rows * nz
    scale = HD ** (-0.5)
    gain1 = norm1_gain.astype(f32)[None]
    gain2 = norm2_gain.astype(f32)[None]

    def own(values):
        return lax.dynamic_slice_in_dim(values, c * own_rows, own_rows, 0)

    def head_slice(values):
        return lax.dynamic_slice_in_dim(values, z * head_cols, head_cols, 1)

    x_all_rows = tokens.astype(f32)
    inverse_one_rows = lax.rsqrt(jnp.mean(x_all_rows * x_all_rows, axis=-1) + epsilon)
    x = own(tokens)
    marks = jnp.concatenate([segments, routes.T, jnp.zeros((7 - routes.shape[1], rows), jnp.int32)], axis=0)
    n1, all_marks = first_gather(nz, x, gain1, marks, 0)
    labels = all_marks[:, 0].reshape(seq)
    all_routes = jnp.transpose(all_marks[:, 1 : 1 + routes.shape[1]], (0, 2, 1)).reshape(seq, routes.shape[1])
    upstream = own(out_grad)
    upstream_later, _ = lax.optimization_barrier((upstream, n1))
    dy = lax.all_gather(upstream_later, SEQ_AXES, axis=0, tiled=True)

    wo = head_slice(o_weight)
    w_heads = jnp.concatenate([head_slice(q_weight), head_slice(k_weight), head_slice(v_weight)], axis=1)
    qkv = dot(n1, w_heads).astype(bf16)
    q, k, v = (qkv[:, i * head_cols : (i + 1) * head_cols].reshape(seq, heads, HD) for i in range(3))
    pos = jnp.arange(seq)
    allowed = (pos[None, :] <= pos[:, None]) & (labels[None, :] == labels[:, None])

    raw = jnp.einsum("qhd,khd->hqk", q, k, preferred_element_type=f32) * scale
    scores = jnp.where(allowed[None], raw, -jnp.inf)
    expd = jnp.exp(scores - jnp.max(scores, axis=-1, keepdims=True))
    p_low = (expd / jnp.sum(expd, axis=-1, keepdims=True)).astype(bf16)
    o = jnp.einsum("hqk,khd->qhd", p_low, v, preferred_element_type=f32).reshape(seq, head_cols).astype(bf16)
    n2, h, inverse_two = project_and_gather(nz, o, o_weight, x, gain2, 1)

    probs = jax.nn.softmax(dot(n2, router_weight), axis=-1)
    chosen = jnp.any(all_routes[:, :, None] == jnp.arange(expert_count)[None, None, :], axis=1)
    gates = jnp.where(chosen, probs, 0.0)
    sigma = jax.nn.sigmoid(dot(n2, shared_gate_vector))

    turned = [jnp.swapaxes(w, 1, 2) for w in (expert_gate_weight, expert_up_weight, expert_down_weight)]
    shared_weights = (shared_gate_weight, shared_up_weight, shared_down_weight)
    ndp = lax.axis_size("dp")
    grad_s, da_s, db_s, gu_s, dgate_s = hidden_layer(nz, n2, dy, sigma[None, :, None], shared_weights, ndp * nz)
    n2_now, dgate_s = lax.optimization_barrier((n2, dgate_s))
    gate = jnp.swapaxes(lax.dynamic_slice_in_dim(gates, z * local_count, local_count, 1), 0, 1)[:, :, None]
    grad_e, da_e, db_e, gu_e, dgate_e = hidden_layer(nz, n2_now, dy, gate, turned, ndp)

    d_expert = jnp.swapaxes(dgate_e[:, :, 0], 0, 1)
    d_probs = lax.dynamic_update_slice_in_dim(jnp.zeros_like(probs), d_expert, z * local_count, 1)
    d_probs = jnp.where(chosen, d_probs, 0.0)
    d_logits = probs * (d_probs - jnp.sum(probs * d_probs, axis=-1, keepdims=True))
    d_vector = dgate_s[0] * (sigma * (1.0 - sigma))[:, None]
    small = jnp.concatenate([d_logits, d_vector], axis=1)
    small_high, small_low = two_parts(small)
    small_weights = jnp.concatenate([router_weight, shared_gate_vector[:, None]], axis=1)
    fill = ((0, 0), (0, 128 - small.shape[1]))
    experts = range(local_count)
    d_n2 = Products(
        nz,
        [((da_e, i), (turned[0], i)) for i in experts] + [((db_e, i), (turned[1], i)) for i in experts],
        [((da_s, 0), shared_gate_weight), ((db_s, 0), shared_up_weight)],
        (jnp.pad(small_high, fill), jnp.pad(small_weights, fill)),
    )
    small_grad = cross_rows(n2, jnp.concatenate([small_high, small_low], axis=1))
    small_grad = small_grad[:, : expert_count + 1] + small_grad[:, expert_count + 1 :]


    def over_dp(grad):
        rows = grad.reshape(-1, grad.shape[-1])
        return lax.psum_scatter(rows, "dp", scatter_dimension=0, tiled=True)

    shared_part = over_dp(grad_s).reshape((nz,) + grad_s.shape[1:])
    expert_part = over_dp(grad_e).reshape(local_count, 3, ffn, -1)
    dhr, dh, grad_two = reduce_and_gather(nz, d_n2, h, gain2, upstream, 2)
    shared_part, dhr = lax.optimization_barrier((shared_part, dhr))
    shared_box = lax.all_to_all(shared_part, "expert", split_axis=0, concat_axis=0, tiled=True)
    d_o = dot(dhr, wo).astype(bf16).reshape(seq, heads, HD)
    grad_o = cross_rows(dhr, o)

    d_v = jnp.einsum("hqk,qhd->khd", p_low, d_o, preferred_element_type=f32)
    dp = jnp.einsum("qhd,khd->hqk", d_o, v, preferred_element_type=f32)
    mean = jnp.sum(d_o.astype(f32) * o.reshape(seq, heads, HD).astype(f32), axis=-1).T
    ds = (p_low.astype(f32) * (dp - mean[:, :, None])).astype(bf16)
    d_q = jnp.einsum("hqk,khd->qhd", ds, k, preferred_element_type=f32) * scale
    d_k = jnp.einsum("hqk,qhd->khd", ds, q, preferred_element_type=f32) * scale
    d_heads = jnp.concatenate([t.reshape(seq, head_cols).astype(bf16) for t in (d_q, d_k, d_v)], axis=1)
    grad_attention = jnp.concatenate(
        [cross_rows(n1, d_heads).astype(bf16), grad_o.astype(bf16)], axis=1
    )
    attention_part = over_dp(grad_attention)
    branch = Products(
        nz,
        [((gu_e, i), (turned[2], i)) for i in experts],
        [((gu_s, 0), shared_down_weight)],
        None,
    )
    dh_now, _ = lax.optimization_barrier((dh, grad_attention))
    input_grad, layer_out, grad_one = reduce_last(
        nz, d_heads, w_heads, x, gain1, dh_now, branch, h, 3
    )
    stats = jnp.stack([inverse_one_rows, inverse_two[:, 0]])

    small_rows = jnp.concatenate(
        [
            jnp.sum(grad_one, axis=0)[None], jnp.sum(grad_two, axis=0)[None], small_grad.T,
            jnp.zeros((13 - expert_count, width), f32),
        ],
        axis=0,
    )
    small_rows, expert_part = lax.optimization_barrier((small_rows, expert_part))
    count = ndp * nz
    small_all = sum_everywhere(nz, ndp, jnp.swapaxes(small_rows.reshape(16, count, width // count), 0, 1), 7)
    s_gate, s_up, s_down = assemble(nz, shared_box, shared_cols)
    attention_part, small_all = lax.optimization_barrier((attention_part, small_all))
    (g_q, g_k, g_v, g_o) = spread(nz, [attention_part], (4,), 6)

    g_one, g_two, g_router, g_vector = small_all[0], small_all[1], small_all[2 : 2 + expert_count].T, small_all[2 + expert_count]
    e_gate, e_up, e_down = (jnp.swapaxes(expert_part[:, k].astype(f32), 1, 2) for k in range(3))
    return (
        layer_out, input_grad, stats, g_one, g_q, g_k, g_v, g_o, g_two, g_router, g_vector,
        s_gate, s_up, s_down, e_gate, e_up, e_down,
    )


def solution(mesh):
    both = ("dp", "expert")
    cols = P(None, "tensor")
    placed = (
        P(both, None), P("dp", "expert"), P(both, None), P(), cols, cols, cols, cols, P(), P(), P(),
        cols, cols, cols, P("expert", None, "tensor"), P("expert", None, "tensor"),
        P("expert", None, "tensor"), P(both, None),
    )
    split = P(both, "tensor")
    experts = P("expert", "dp", "tensor")
    return jax.shard_map(
        body,
        mesh=mesh,
        in_specs=placed,
        out_specs=(
            P(both, None), P(both, None), P(None, both), P(both), split, split, split, split, P(both),
            P(both, None), P(both), split, split, split, experts, experts, experts,
        ),
        check_vma=False,
    )
```

time: 664 us -> 600 us (0.904)
  Pallas kernels: 538 us -> 464 us
  other arithmetic: 20.7 us -> 30.7 us
  starting transfers between devices: 0.2 us -> 8.42 us
    pallas_call x8 -> x4, Pallas kernels: 299 us -> 202 us  [the longest x1 102 us: reduce_last(): pl.pallas_call(kernel, out_shape=[jax.ShapeDtypeStruct((2 * rows, width),...]
    pallas_call x1, Pallas kernels: 85.2 us -> 105 us  [reduce_and_gather(): pl.pallas_call(kernel, out_shape=[jax.ShapeDtypeStruct((nz * 2 * rows, wi...]
    dot_general x5 -> x1, matrix products: 13.6 us -> 4.11 us  [body(): d_v = jnp.einsum('hqk,qhd->khd', p_low, d_o, preferred_element_type=f32)]
    all_to_all x0 -> x1, starting transfers between devices: none -> 8.09 us  [body(): lax.all_to_all(shared_part, 'expert', split_axis=0, concat_axis=0, tiled=...]
    sub x0 -> x1, matrix products: none -> 6.79 us  [body(): expd = jnp.exp(scores - jnp.max(scores, axis=-1, keepdims=True))]
    dot_general x6 -> x4, matrix products: 19.9 us -> 14.3 us  [dot(): return jnp.dot(left, right, preferred_element_type=f32)]
    unnamed x75 -> x53, local copies, waits for them, and re-layouts: 15.3 us -> 12.1 us
  transfers between devices with their start and end apart: 5 -> 5, of which waited for: 0 -> 0; matrix products, arithmetic and copies ran while one was open for 12% -> 13% of each run, Pallas kernels for 66% -> 61%
where the time goes in v3:
time: 600 us; the launch traced here: 591 us
  Pallas kernels  464 us (77%)
  matrix products  42.2 us (7%)
  local copies, waits for them, and re-layouts  31.1 us (5%)
  other arithmetic  30.7 us (5%)
  between operations  14.6 us (2%)
  starting transfers between devices  8.42 us (1%)
    pallas_call x1, Pallas kernels, reduce_and_gather(): pl.pallas_call(kernel, out_shape=[jax.ShapeDtypeStruct((nz * 2 * rows, wi...  105 us
    pallas_call x1, Pallas kernels, reduce_last(): pl.pallas_call(kernel, out_shape=[jax.ShapeDtypeStruct((2 * rows, width),...  102 us
    pallas_call x2, Pallas kernels, hidden_layer(): pl.pallas_call(kernel, out_shape=[jax.ShapeDtypeStruct((groups, experts *...  97.5 us
    pallas_call x1, Pallas kernels, project_and_gather(): pl.pallas_call(kernel, out_shape=[jax.ShapeDtypeStruct((nz * full, width)...  73.3 us
    pallas_call x1, Pallas kernels, first_gather(): pl.pallas_call(kernel, out_shape=[jax.ShapeDtypeStruct((nz * 2 * rows, wi...  39.3 us
    pallas_call x1, Pallas kernels, spread(): pl.pallas_call(kernel, out_shape=[jax.ShapeDtypeStruct((block, nz * parts...  29.2 us
    pallas_call x1, Pallas kernels, sum_everywhere(): pl.pallas_call(kernel, out_shape=jax.ShapeDtypeStruct((rows, block), f32)...  15.6 us
    dot_general x4, matrix products, dot(): return jnp.dot(left, right, preferred_element_type=f32)  14.3 us
  transfers between devices with their start and end apart: 5, of which 0 were waited for; matrix products, arithmetic and copies ran while one was open for 13% of the time, Pallas kernels for 61%

profile of v3, /device:TPU:8, one launch (start us, length us, event | category | flops | bytes accessed | tf_op | source)
XLA Modules:
  0.0 591.3 jit_solution(9601462808743019928)
XLA Ops:
  7.3 1.3 broadcast_in_dim.77
  8.6 1.4 add_add_fusion.marks_ref
  10.0 2.3 constant_dynamic-slice_fusion
  12.2 39.3 %shard_map.305 = (bf16[1024,2048]{1,0:T(8,128)(2,1)}, s32[4,8,256]{2,1,0:T(8,128)}) custom-call(bf16[128,2048]{1,0:T(8,128)(2,1)} %get-tuple-element.109.x_ref.refs_8_, f32[1,2048]{1,0:T(1,128)} %bitcast.132, s32[8,256]{1,0:T(8,128)} %add_add_fusion.marks_ref), custom_call_target="tpu_custom_call" | custom-call | tf_op jit(solution)/shard_map/pallas_call | solution.py:319
  52.4 1.3 broadcast_in_dim.78
  54.4 1.4 constant_dynamic-slice_fusion.3
  55.9 2.2 constant_dynamic-slice_fusion.1
  58.1 3.5 convolution_convert_fusion.2
  61.8 1.6 fusion.4
  63.3 6.8 %fusion.30 = (f32[2,1024]{1,0:T(2,128)S(1)}, f32[2,1024,1024]{1,2,0:T(8,128)}) fusion(pred[1024,1024]{0,1:T(8,128)(4,1)} %fusion.4, bf16[1024,2,128]{0,2,1:T(8,128)(2,1)S(1)} %bitcast.126, bf16[1024,2,128]{0,2,1:T(8,128)(2,1)S(1)} %bitcast.128), kind=kOutput, calls=%fused_computation.76 | convolution fusion | flops 545260544 | bytes 10493952 | tf_op jit(solution)/shard_map/sub | solution.py:1053
  70.1 4.7 divide_convert_fusion
  74.9 2.0 copy-done
  77.6 1.0 copy.179.o_ref
  78.6 73.3 %shard_map.306 = (bf16[1024,2048]{1,0:T(8,128)(2,1)}, f32[128,2048]{1,0:T(8,128)}, f32[256,128]{1,0:T(8,128)}) custom-call(bf16[1024,256]{1,0:T(8,128)(2,1)} %copy.179.o_ref, bf16[2048,1024]{1,0:T(8,128)(2,1)} %w_ref.1, bf16[128,2048]{1,0:T(8,128)(2,1)} %get-tuple-element.109.x_ref.refs_8_, f32[1,2048]{1,0:T(1,128)} %bitcast.130), custom_call_target="tpu_custom_call" | custom-call | tf_op jit(solution)/shard_map/pallas_call | solution.py:415
  151.8 3.4 fusion.32
  155.2 1.1 copy.152.gate_ref
  156.3 35.5 %shard_map.307 = (bf16[16,2304,128]{2,1,0:T(8,128)(2,1)}, bf16[1,1024,768]{2,1,0:T(8,128)(2,1)}, bf16[1,1024,768]{2,1,0:T(8,128)(2,1)}, bf16[1,1024,768]{2,1,0:T(8,128)(2,1)}, f32[1,1024,1]{2,1,0:T(8,128)}) custom-call(bf16[1024,2048]{1,0:T(8,128)(2,1)} %get-tuple-element.60.n2_hbm, bf16[1024,2048]{1,0:T(8,128)(2,1)} %all-gather.2.cloned.1.call-done.dy_hbm, ...), custom_call_target="tpu_custom_call" | custom-call | tf_op jit(solution)/shard_map/pallas_call | solution.py:672
  192.5 3.4 fusion.31
  196.0 1.3 copy.153.gate_ref
  197.4 62.0 %shard_map.308 = (bf16[4,4224,512]{2,1,0:T(8,128)(2,1)}, bf16[2,1024,768]{2,1,0:T(8,128)(2,1)}, bf16[2,1024,768]{2,1,0:T(8,128)(2,1)}, bf16[2,1024,768]{2,1,0:T(8,128)(2,1)}, f32[2,1024,1]{2,1,0:T(8,128)}) custom-call(bf16[1024,2048]{1,0:T(8,128)(2,1)} %get-tuple-element.60.n2_hbm, bf16[1024,2048]{1,0:T(8,128)(2,1)} %all-gather.2.cloned.1.call-done.dy_hbm, ...), custom_call_target="tpu_custom_call" | custom-call | tf_op jit(solution)/shard_map/pallas_call | solution.py:672
  260.7 1.3 reduce.1
  262.1 1.6 reduce
  264.8 104.9 %shard_map.309 = (bf16[1024,2048]{1,0:T(8,128)(2,1)}, f32[128,2048]{1,0:T(8,128)}, f32[16,2048]{1,0:T(8,128)}) custom-call(bf16[2,1024,768]{2,1,0:T(8,128)(2,1)} %get-tuple-element.64.refs_0_.refs_1_, bf16[2,1024,768]{2,1,0:T(8,128)(2,1)} %get-tuple-element.64.refs_0_.refs_1_, bf16[2,1024,768]{2,1,0:T(8,128)(2,1)} %get-tuple-element.65.refs_2_.refs_3_, ...), custom_call_target="tpu_custom_call" | custom-call | tf_op jit(solution)/shard_map/pallas_call | solution.py:797
  369.8 4.1 multiply_reduce_fusion.1
  374.0 1.3 multiply_convert_fusion
  375.3 2.0 copy-done.2
  379.0 3.7 fusion.7
  383.0 4.1 convolution_convert_fusion.3
  388.1 3.7 convolution_convert_fusion.1
  391.8 3.8 convolution_convert_fusion
  395.6 2.6 pad_maximum_fusion
  398.2 8.1 %all-to-all-start = ((bf16[4,2304,128]{2,1,0:T(8,128)(2,1)}), bf16[4,2304,128]{2,1,0:T(8,128)(2,1)S(1)}, u32[]{:S(2)}, u32[]{:S(2)}) async-start(bf16[4,2304,128]{2,1,0:T(8,128)(2,1)} %bitcast.118), calls=%async_computation.3 | async-start | bytes 4718592 | tf_op jit(solution)/shard_map/all_to_all | solution.py:1099
  406.4 1.0 slice_reduce_fusion
  407.4 1.7 multiply_reduce_fusion
  409.7 3.0 pad_maximum_fusion.1.refs_7_
  412.7 1.0 reduce_sum.69
  413.7 3.0 fusion.16
  416.8 1.2 pad_maximum_fusion.2.refs_6_
  418.0 101.9 %shard_map.310 = (f32[256,2048]{1,0:T(8,128)}, f32[256,2048]{1,0:T(8,128)}, f32[16,2048]{1,0:T(8,128)}) custom-call(bf16[2,1024,768]{2,1,0:T(8,128)(2,1)} %get-tuple-element.61.refs_0_.refs_1_, bf16[2,1024,768]{2,1,0:T(8,128)(2,1)} %get-tuple-element.61.refs_0_.refs_1_, bf16[2,704,2048]{2,1,0:T(8,128)(2,1)} %bitcast.111, bf16[2,704,2048]{2,1,0:T(8,128)(2,1)} %bitcast.112, ...), custom_call_target="tpu_custom_call" | custom-call | tf_op jit(solution)/shard_map/pallas_call | solution.py:892
  520.9 2.3 shard_map.313
  523.9 15.6 %shard_map.311 = f32[16,128]{1,0:T(8,128)} custom-call(f32[16,16,128]{2,1,0:T(8,128)} %bitcast_bitcast_fusion.in_ref), custom_call_target="tpu_custom_call" | custom-call | tf_op jit(solution)/shard_map/pallas_call | solution.py:973
  539.6 1.3 slice_bitcast_fusion.1
  540.8 1.3 slice_bitcast_fusion
  542.1 29.2 %shard_map.312 = (f32[128,1024]{1,0:T(8,128)}, f32[128,1024]{1,0:T(8,128)}, f32[128,1024]{1,0:T(8,128)}, f32[128,1024]{1,0:T(8,128)}) custom-call(bf16[512,1024]{1,0:T(8,128)(2,1)} %reduce-scatter.6.cloned.1.call-done.refs_0_), custom_call_target="tpu_custom_call" | custom-call | tf_op jit(solution)/shard_map/pallas_call | solution.py:493
  571.4 6.3 %convert_bitcast_fusion = (f32[2,512,704]{1,2,0:T(8,128)}, f32[2,512,704]{1,2,0:T(8,128)}, f32[2,512,704]{1,2,0:T(8,128)}) fusion(bf16[2,3,704,512]{3,2,1,0:T(8,128)(2,1)} %bitcast.117), kind=kLoop, calls=%fused_computation.14 | loop fusion | flops 2162688 | bytes 12976128 | tf_op jit(solution)/shard_map/transpose | solution.py:1141
  577.6 1.3 copy.192
  579.0 1.0 copy-done.5
  580.0 1.3 copy.193
  (96 shorter events, 14.4 us)
Async XLA Ops:
  7.2 149.1 %all-gather.2.cloned.1.call-start = ((), (), s32[]{:S(2)}) async-start(), calls=%async_computation.4 | async-start | bytes 4718592 | tf_op jit(solution)/shard_map/all_gather | solution.py:1042
  51.6 318.1 %reduce-scatter.4.cloned.1.call-start = ((), (), s32[]{:S(2)}) async-start(), calls=%async_computation.5 | async-start | bytes 11796480 | tf_op jit(solution)/shard_map/reduce_scatter | solution.py:1093
  54.4 3.7 copy-start.21
  55.9 5.7 copy-start.4
  58.1 3.5 copy-start.3
  61.8 8.4 %copy-start.7 = (bf16[1024,256]{0,1:T(8,128)(2,1)}, bf16[1024,256]{0,1:T(8,128)(2,1)S(1)}, u32[]{:S(2)}) copy-start(bf16[1024,256]{0,1:T(8,128)(2,1)S(1)} %get-tuple-element.96) | copy-start | bytes 1572868
  74.9 2.0 copy-start
  191.7 0.8 copy-start.20
  191.8 0.8 copy-start.19
  191.8 331.4 %reduce-scatter.8.cloned.1.call-start = ((), (), s32[]{:S(2)}) async-start(), calls=%async_computation.7 | async-start | bytes 21626880 | tf_op jit(solution)/shard_map/reduce_scatter | solution.py:1093
  259.4 280.1 %reduce-scatter.6.cloned.1.call-start = ((), (), s32[]{:S(2)}) async-start(), calls=%async_computation.6 | async-start | bytes 5242880 | tf_op jit(solution)/shard_map/reduce_scatter | solution.py:1093
  369.7 4.2 copy-start.1
  374.0 3.3 copy-start.8
  375.3 2.0 copy-start.2
  382.9 8.8 %copy-start.11 = (bf16[1024,256]{1,0:T(8,128)(2,1)}, bf16[1024,256]{1,0:T(8,128)(2,1)S(1)}, u32[]{:S(2)}) copy-start(bf16[1024,256]{1,0:T(8,128)(2,1)S(1)} %copy.181) | copy-start | bytes 1572868
  387.1 4.7 copy-start.9
  388.1 3.7 copy-start.13
  388.1 3.7 copy-start.22
  398.2 122.7 %all-to-all-start = ((bf16[4,2304,128]{2,1,0:T(8,128)(2,1)}), bf16[4,2304,128]{2,1,0:T(8,128)(2,1)S(1)}, u32[]{:S(2)}, u32[]{:S(2)}) async-start(bf16[4,2304,128]{2,1,0:T(8,128)(2,1)} %bitcast.118), calls=%async_computation.3 | async-start | bytes 4718592 | tf_op jit(solution)/shard_map/all_to_all | solution.py:1099
  412.7 4.1 copy-start.10
  412.7 4.1 copy-start.12
  413.7 3.1 copy-start.14
  571.4 6.3 %copy-start.6 = (f32[256,2048]{1,0:T(8,128)S(1)}, f32[256,2048]{1,0:T(8,128)}, u32[]{:S(2)}) copy-start(f32[256,2048]{1,0:T(8,128)} %get-tuple-element.129) | copy-start | bytes 6291460
  577.6 2.3 copy-start.5
  577.6 3.7 copy-start.18
  577.6 4.5 copy-start.17
  580.0 2.9 copy-start.16
  580.0 3.7 copy-start.15
Sparse Core Ops, SparseCore 0:
  51.8 56.7 all-gather.1
  191.9 98.3 reduce-scatter.3
  293.4 158.1 reduce-scatter.7
  454.6 52.6 reduce-scatter.5
